TPU v7x, 32 devices: a whole 2x2x4 slice. The times are simulated.
32 devices in a mesh: dp: 4 (over z), seq: 4 (over x, core), tensor: 2 (over y).
Axes of the slice: x: 2, y: 2, z: 4, core: 2. Of those that a mesh axis runs over, the one named last changes fastest.
Arguments:
- layer_in: bfloat16 [1024, 16, 1472], P('tensor', ('dp', 'seq')), may hold values from -6 to 6
- out_grad: bfloat16 [1024, 16, 1472], P('tensor', ('dp', 'seq')), may hold values from -6 to 6
- doc_lengths: int32 [16, 4], P(('dp', 'seq')), may hold values from 1 to 512, 1024 in all within a row
- valid_length: int32 [16], P(('dp', 'seq')), may hold values from 256 to 1024
- gain_attn: bfloat16 [1472], replicated, may hold values from 0.5 to 1.5
- query_weight: bfloat16 [1472, 384], P(None, 'tensor'), may hold values from -0.078125 to 0.078125
- key_weight: bfloat16 [1472, 384], P(None, 'tensor'), may hold values from -0.078125 to 0.078125
- value_weight: bfloat16 [1472, 384], P(None, 'tensor'), may hold values from -0.15625 to 0.15625
- position_bias: float32 [32, 6], P(None, 'tensor'), may hold values from -4 to 4
- output_weight: bfloat16 [384, 1472], P('tensor'), may hold values from -1.75 to 1.75
- gain_ffn: bfloat16 [1472], replicated, may hold values from 0.5 to 1.5
- gate_weight: bfloat16 [1472, 3584], P(None, 'tensor'), may hold values from -0.15625 to 0.15625
- up_weight: bfloat16 [1472, 3584], P(None, 'tensor'), may hold values from -0.15625 to 0.15625
- down_weight: bfloat16 [3584, 1472], P('tensor'), may hold values from -0.09375 to 0.09375
Outputs:
- out_y: bfloat16 [1024, 16, 1472], P('tensor', ('dp', 'seq'))
- grad_layer_in: float32 [1024, 16, 1472], P('tensor', ('dp', 'seq'))
- grad_gain_attn: float32 [1472], replicated
- grad_query_weight: float32 [1472, 384], P('dp', 'tensor')
- grad_key_weight: float32 [1472, 384], P('dp', 'tensor')
- grad_value_weight: float32 [1472, 384], P('dp', 'tensor')
- grad_position_bias: float32 [32, 6], replicated
- grad_output_weight: float32 [384, 1472], P('tensor', 'dp')
- grad_gain_ffn: float32 [1472], replicated
- grad_gate_weight: float32 [1472, 3584], P('dp', 'tensor')
- grad_up_weight: float32 [1472, 3584], P('dp', 'tensor')
- grad_down_weight: float32 [3584, 1472], P('tensor', 'dp')
Inputs may be any that keep to these rules, and one draw needn't show every extreme that they name: `doc_lengths`: in each row the 4 lengths sum to 1024.
All inputs are finite; a program needn't handle non-finite values.
Results may differ from a plain program's by a relative error of at most 0.019.
Values may be sent and summed in bfloat16 or wider, within the bound.
A program may use at most 192 MiB of HBM per device.

v0:
```python
import jax
import jax.numpy as jnp
from jax import lax
from jax.sharding import PartitionSpec as P

far_steps = (12, 16, 23, 32, 46, 64, 91)
eps_norm = 1e-06
masked_score = -1e30


def bucket_table(first, count, length):
    rows_at = first + jnp.arange(count, dtype=jnp.int32)[:, None]
    cols_at = jnp.arange(length, dtype=jnp.int32)[None, :]
    offset = cols_at - rows_at
    distance = jnp.abs(offset)
    far = 8 + sum(((distance >= step).astype(jnp.int32) for step in far_steps))
    near = jnp.where(distance < 8, distance, far)
    return near + jnp.where(offset > 0, 16, 0)


def segment_ids(lengths, valid, length):
    ends = jnp.cumsum(lengths, axis=-1)
    where_at = jnp.arange(length, dtype=jnp.int32)
    counted = jnp.sum((where_at[None, :, None] >= ends[:, None, :]).astype(jnp.int32), axis=-1)
    padded = jnp.int32(lengths.shape[-1])
    return jnp.where(where_at[None, :] < valid[:, None], counted, padded)


def rms_scale(values, gain):
    return values * lax.rsqrt(jnp.mean(values * values, axis=-1, keepdims=True) + eps_norm) * gain


def gelu_product(gate, up_part):
    return jax.nn.gelu(gate, approximate=True) * up_part


def local(
    layer_in,
    out_grad,
    doc_lengths,
    valid_length,
    gain_attn,
    query_weight,
    key_weight,
    value_weight,
    position_bias,
    output_weight,
    gain_ffn,
    gate_weight,
    up_weight,
    down_weight,
):
    local_len, rows, width = layer_in.shape
    length = local_len * lax.axis_size("tensor")
    heads = position_bias.shape[1]
    buckets_all = position_bias.shape[0]
    head_dim = query_weight.shape[1] // heads
    block = min(512, length)
    first_pos = lax.axis_index("tensor") * local_len
    segment = segment_ids(doc_lengths, valid_length, length)
    bucket_range = jnp.arange(buckets_all, dtype=jnp.int32)
    input_float = layer_in.astype(jnp.float32)
    norm_one, undo_one = jax.vjp(rms_scale, input_float, gain_attn.astype(jnp.float32))
    xn_full = lax.all_gather(norm_one.astype(jnp.bfloat16), "tensor", axis=0, tiled=True)
    query = jnp.einsum(
        "lrd,dh->lrh", xn_full, query_weight, preferred_element_type=jnp.float32
    ).astype(jnp.bfloat16)
    keys = jnp.einsum(
        "lrd,dh->lrh", xn_full, key_weight, preferred_element_type=jnp.float32
    ).astype(jnp.bfloat16)
    values = jnp.einsum(
        "lrd,dh->lrh", xn_full, value_weight, preferred_element_type=jnp.float32
    ).astype(jnp.bfloat16)
    query_heads = query.reshape(length, rows, heads, head_dim)
    key_heads = keys.reshape(length, rows, heads, head_dim)
    value_heads = values.reshape(length, rows, heads, head_dim)

    def block_scores(first, query_block):
        pieces = bucket_table(first, block, length)
        picks = (pieces[:, :, None] == bucket_range[None, None, :]).astype(jnp.bfloat16)
        bias_block = jnp.einsum(
            "qkb,bh->hqk",
            picks.astype(jnp.float32),
            position_bias,
            precision=lax.Precision.HIGHEST,
            preferred_element_type=jnp.float32,
        )
        scores = jnp.einsum(
            "qrhd,krhd->rhqk", query_block, key_heads, preferred_element_type=jnp.float32
        )
        scores = scores + bias_block[None]
        allowed = segment[:, first : first + block, None] == segment[:, None, :]
        return (jnp.where(allowed[:, None], scores, masked_score), picks)

    mixed_parts = []
    log_totals = []
    for first in range(0, length, block):
        scores, picks = block_scores(first, query_heads[first : first + block])
        top_score = jnp.max(scores, axis=-1, keepdims=True)
        raised = jnp.exp(scores - top_score)
        total = jnp.sum(raised, axis=-1, keepdims=True)
        attn_low = (raised / total).astype(jnp.bfloat16)
        log_totals.append(top_score + jnp.log(total))
        mixed_parts.append(
            jnp.einsum(
                "rhqk,krhd->qrhd", attn_low, value_heads, preferred_element_type=jnp.float32
            ).astype(jnp.bfloat16)
        )
    mixed = jnp.concatenate(mixed_parts, axis=0).reshape(length, rows, heads * head_dim)
    part = mixed
    hres = input_float + lax.psum_scatter(
        jnp.einsum("lrh,hd->lrd", part, output_weight, preferred_element_type=jnp.float32),
        "tensor",
        scatter_dimension=0,
        tiled=True,
    )
    norm_two, undo_two = jax.vjp(rms_scale, hres, gain_ffn.astype(jnp.float32))
    xn_two_full = lax.all_gather(norm_two.astype(jnp.bfloat16), "tensor", axis=0, tiled=True)
    gate = jnp.einsum("lrd,df->lrf", xn_two_full, gate_weight, preferred_element_type=jnp.float32)
    up_part = jnp.einsum("lrd,df->lrf", xn_two_full, up_weight, preferred_element_type=jnp.float32)
    hidden_float, undo_gelu = jax.vjp(gelu_product, gate, up_part)
    hidden = hidden_float.astype(jnp.bfloat16)
    part = hidden
    out_y = (
        hres
        + lax.psum_scatter(
            jnp.einsum("lrf,fd->lrd", part, down_weight, preferred_element_type=jnp.float32).astype(
                jnp.bfloat16
            ),
            "tensor",
            scatter_dimension=0,
            tiled=True,
        ).astype(jnp.float32)
    ).astype(jnp.bfloat16)
    positions = first_pos + jnp.arange(local_len, dtype=jnp.int32)
    live = (positions[:, None] < valid_length[None, :]).astype(jnp.float32)
    grad_y = out_grad.astype(jnp.float32) * live[:, :, None]
    grad_y_full = lax.all_gather(grad_y.astype(jnp.bfloat16), "tensor", axis=0, tiled=True)
    grad_down = jnp.einsum("lrf,lrd->fd", hidden, grad_y_full, preferred_element_type=jnp.float32)
    grad_hidden = jnp.einsum(
        "lrd,fd->lrf", grad_y_full, down_weight, preferred_element_type=jnp.float32
    )
    grad_gate_float, grad_up_float = undo_gelu(grad_hidden)
    grad_gate = grad_gate_float.astype(jnp.bfloat16)
    grad_up = grad_up_float.astype(jnp.bfloat16)
    grad_gate_w = jnp.einsum(
        "lrd,lrf->df", xn_two_full, grad_gate, preferred_element_type=jnp.float32
    )
    grad_up_w = jnp.einsum("lrd,lrf->df", xn_two_full, grad_up, preferred_element_type=jnp.float32)
    grad_xn_two = lax.psum_scatter(
        (
            jnp.einsum("lrf,df->lrd", grad_gate, gate_weight, preferred_element_type=jnp.float32)
            + jnp.einsum("lrf,df->lrd", grad_up, up_weight, preferred_element_type=jnp.float32)
        ).astype(jnp.bfloat16),
        "tensor",
        scatter_dimension=0,
        tiled=True,
    ).astype(jnp.float32)
    grad_h_norm, grad_gain_two = undo_two(grad_xn_two)
    grad_hres = grad_y + grad_h_norm
    branch_full = lax.all_gather(grad_hres.astype(jnp.bfloat16), "tensor", axis=0, tiled=True)
    grad_out_w = jnp.einsum("lrh,lrd->hd", mixed, branch_full, preferred_element_type=jnp.float32)
    grad_mixed = jnp.einsum(
        "lrd,hd->lrh", branch_full, output_weight, preferred_element_type=jnp.float32
    ).astype(jnp.bfloat16)
    grad_mixed = grad_mixed.reshape(length, rows, heads, head_dim)
    grad_key_acc = jnp.zeros((length, rows, heads, head_dim), jnp.float32)
    grad_value_acc = jnp.zeros((length, rows, heads, head_dim), jnp.float32)
    grad_bias = jnp.zeros((heads, buckets_all), jnp.float32)
    query_parts = []
    for number, first in enumerate(range(0, length, block)):
        query_block = query_heads[first : first + block]
        mixed_block = grad_mixed[first : first + block]
        scores, picks = block_scores(first, query_block)
        attn_probs = jnp.exp(scores - log_totals[number])
        grad_probs = jnp.einsum(
            "qrhd,krhd->rhqk", mixed_block, value_heads, preferred_element_type=jnp.float32
        )
        inner = jnp.sum(grad_probs * attn_probs, axis=-1, keepdims=True)
        grad_scores = (attn_probs * (grad_probs - inner)).astype(jnp.bfloat16)
        query_parts.append(
            jnp.einsum(
                "rhqk,krhd->qrhd", grad_scores, key_heads, preferred_element_type=jnp.float32
            )
        )
        grad_key_acc = grad_key_acc + jnp.einsum(
            "rhqk,qrhd->krhd", grad_scores, query_block, preferred_element_type=jnp.float32
        )
        grad_value_acc = grad_value_acc + jnp.einsum(
            "rhqk,qrhd->krhd",
            attn_probs.astype(jnp.bfloat16),
            mixed_block,
            preferred_element_type=jnp.float32,
        )
        grad_bias = grad_bias + jnp.einsum(
            "rhqk,qkb->hb", grad_scores, picks, preferred_element_type=jnp.float32
        )
    grad_query = (
        jnp.concatenate(query_parts, axis=0)
        .reshape(length, rows, heads * head_dim)
        .astype(jnp.bfloat16)
    )
    grad_key = grad_key_acc.reshape(length, rows, heads * head_dim).astype(jnp.bfloat16)
    grad_value = grad_value_acc.reshape(length, rows, heads * head_dim).astype(jnp.bfloat16)
    grad_query_w = jnp.einsum(
        "lrd,lrh->dh", xn_full, grad_query, preferred_element_type=jnp.float32
    )
    grad_key_w = jnp.einsum("lrd,lrh->dh", xn_full, grad_key, preferred_element_type=jnp.float32)
    grad_value_w = jnp.einsum(
        "lrd,lrh->dh", xn_full, grad_value, preferred_element_type=jnp.float32
    )
    grad_xn_one = lax.psum_scatter(
        (
            jnp.einsum("lrh,dh->lrd", grad_query, query_weight, preferred_element_type=jnp.float32)
            + jnp.einsum("lrh,dh->lrd", grad_key, key_weight, preferred_element_type=jnp.float32)
            + jnp.einsum(
                "lrh,dh->lrd", grad_value, value_weight, preferred_element_type=jnp.float32
            )
        ).astype(jnp.bfloat16),
        "tensor",
        scatter_dimension=0,
        tiled=True,
    ).astype(jnp.float32)
    grad_x_norm, grad_gain_one = undo_one(grad_xn_one)
    grad_layer_in = grad_hres + grad_x_norm
    part_q, part_k, part_v, part_o, part_g, part_u, part_d = (
        lax.psum_scatter(
            grad_query_w.astype(jnp.bfloat16), "dp", scatter_dimension=0, tiled=True
        ).astype(jnp.float32),
        lax.psum_scatter(
            grad_key_w.astype(jnp.bfloat16), "dp", scatter_dimension=0, tiled=True
        ).astype(jnp.float32),
        lax.psum_scatter(
            grad_value_w.astype(jnp.bfloat16), "dp", scatter_dimension=0, tiled=True
        ).astype(jnp.float32),
        lax.psum_scatter(
            grad_out_w.astype(jnp.bfloat16), "dp", scatter_dimension=1, tiled=True
        ).astype(jnp.float32),
        lax.psum_scatter(
            grad_gate_w.astype(jnp.bfloat16), "dp", scatter_dimension=0, tiled=True
        ).astype(jnp.float32),
        lax.psum_scatter(
            grad_up_w.astype(jnp.bfloat16), "dp", scatter_dimension=0, tiled=True
        ).astype(jnp.float32),
        lax.psum_scatter(
            grad_down.astype(jnp.bfloat16), "dp", scatter_dimension=1, tiled=True
        ).astype(jnp.float32),
    )
    piece_q, piece_k, piece_v, piece_o, piece_g, piece_u, piece_d = (
        lax.psum_scatter(
            part_q.astype(jnp.bfloat16), "seq", scatter_dimension=1, tiled=True
        ).astype(jnp.float32),
        lax.psum_scatter(
            part_k.astype(jnp.bfloat16), "seq", scatter_dimension=1, tiled=True
        ).astype(jnp.float32),
        lax.psum_scatter(
            part_v.astype(jnp.bfloat16), "seq", scatter_dimension=1, tiled=True
        ).astype(jnp.float32),
        lax.psum_scatter(
            part_o.astype(jnp.bfloat16), "seq", scatter_dimension=0, tiled=True
        ).astype(jnp.float32),
        lax.psum_scatter(
            part_g.astype(jnp.bfloat16), "seq", scatter_dimension=1, tiled=True
        ).astype(jnp.float32),
        lax.psum_scatter(
            part_u.astype(jnp.bfloat16), "seq", scatter_dimension=1, tiled=True
        ).astype(jnp.float32),
        lax.psum_scatter(
            part_d.astype(jnp.bfloat16), "seq", scatter_dimension=0, tiled=True
        ).astype(jnp.float32),
    )
    sum_q, sum_k, sum_v, sum_o, sum_g, sum_u, sum_d = (
        lax.all_gather(piece_q.astype(jnp.bfloat16), "seq", axis=1, tiled=True).astype(
            piece_q.dtype
        ),
        lax.all_gather(piece_k.astype(jnp.bfloat16), "seq", axis=1, tiled=True).astype(
            piece_k.dtype
        ),
        lax.all_gather(piece_v.astype(jnp.bfloat16), "seq", axis=1, tiled=True).astype(
            piece_v.dtype
        ),
        lax.all_gather(piece_o.astype(jnp.bfloat16), "seq", axis=0, tiled=True).astype(
            piece_o.dtype
        ),
        lax.all_gather(piece_g.astype(jnp.bfloat16), "seq", axis=1, tiled=True).astype(
            piece_g.dtype
        ),
        lax.all_gather(piece_u.astype(jnp.bfloat16), "seq", axis=1, tiled=True).astype(
            piece_u.dtype
        ),
        lax.all_gather(piece_d.astype(jnp.bfloat16), "seq", axis=0, tiled=True).astype(
            piece_d.dtype
        ),
    )
    bias_full = jnp.zeros((buckets_all, heads * lax.axis_size("tensor")), jnp.float32)
    bias_full = lax.dynamic_update_slice(
        bias_full, grad_bias.T, (jnp.int32(0), lax.axis_index("tensor") * heads)
    )
    gain_one_sum, gain_two_sum, bias_sum = lax.psum(
        (grad_gain_one, grad_gain_two, bias_full), ("dp", "seq", "tensor")
    )
    return (
        out_y,
        grad_layer_in,
        gain_one_sum,
        sum_q,
        sum_k,
        sum_v,
        bias_sum,
        sum_o,
        gain_two_sum,
        sum_g,
        sum_u,
        sum_d,
    )


def solution(mesh):
    placed = (
        P("tensor", ("dp", "seq"), None),
        P("tensor", ("dp", "seq"), None),
        P(("dp", "seq"), None),
        P(("dp", "seq")),
        P(),
        P(None, "tensor"),
        P(None, "tensor"),
        P(None, "tensor"),
        P(None, "tensor"),
        P("tensor", None),
        P(),
        P(None, "tensor"),
        P(None, "tensor"),
        P("tensor", None),
    )
    return jax.shard_map(
        local,
        mesh=mesh,
        in_specs=placed,
        out_specs=(
            P("tensor", ("dp", "seq"), None),
            P("tensor", ("dp", "seq"), None),
            P(),
            P("dp", "tensor"),
            P("dp", "tensor"),
            P("dp", "tensor"),
            P(),
            P("tensor", "dp"),
            P(),
            P("dp", "tensor"),
            P("dp", "tensor"),
            P("tensor", "dp"),
        ),
        check_vma=False,
    )
```

profile of v0, /device:TPU:0, one launch (start us, length us, event | category | flops | bytes accessed | tf_op | source)
XLA Modules:
  0.0 1137.1 jit_solution(7597752662665482507)
XLA Ops:
  15.9 21.9 %fusion.3 = f32[512,1024,3]{0,2,1:T(4,128)} fusion(s32[512,1024]{0,1:T(8,128)S(1)} %fusion.82, f32[32,3]{0,1:T(4,128)S(1)} %copy-done.41), kind=kOutput, calls=%fused_computation.5 | convolution fusion | flops 620756992 | bytes 8388992 | tf_op jit(solution)/shard_map/qkb,bh->hqk/dot_general | solution.py:81
  50.2 22.2 %fusion.1 = f32[512,1024,3]{0,2,1:T(4,128)} fusion(s32[512,1024]{0,1:T(8,128)S(1)} %fusion.83, f32[32,3]{0,1:T(4,128)S(1)} %copy-done.41), kind=kOutput, calls=%fused_computation.2 | convolution fusion | flops 620756992 | bytes 8388992 | tf_op jit(solution)/shard_map/qkb,bh->hqk/dot_general | solution.py:81
  106.2 76.4 %reduce-scatter.33.cloned.1.call-done = f32[512,1,1472]{0,2,1:T(8,128)} async-done(((f32[1024,1,1472]{0,2,1:T(8,128)}), f32[512,1,1472]{0,2,1:T(8,128)}) %reduce-scatter.33.cloned.1.call-update) | async-done | bytes 3014672 | tf_op jit(solution)/shard_map/reduce_scatter | solution.py:111
  189.8 42.0 %all-gather.10.cloned.1.call-done = bf16[1024,1,1472]{0,2,1:T(8,128)(2,1)} async-done(((bf16[512,1,1472]{0,2,1:T(8,128)(2,1)}), bf16[1024,1,1472]{0,2,1:T(8,128)(2,1)}) %all-gather.10.cloned.1.call-update) | async-done | bytes 3014672 | tf_op jit(solution)/shard_map/all_gather | solution.py:118
  231.8 19.8 %fusion.53 = f32[1024,1792]{1,0:T(8,128)} fusion(bf16[1472,1792]{1,0:T(8,128)(2,1)} %param.26, bf16[1024,1,1472]{0,2,1:T(8,128)(2,1)} %all-gather.10.cloned.1.call-done), kind=kOutput, calls=%fused_computation.90 | convolution fusion | flops 5402263552 | bytes 15630336 | tf_op jit(solution)/shard_map/lrd,df->lrf/dot_general | solution.py:120
  262.2 15.2 %all-gather.12.cloned.1.call-done = bf16[1024,1,1472]{0,2,1:T(8,128)(2,1)} async-done(((bf16[512,1,1472]{0,2,1:T(8,128)(2,1)}), bf16[1024,1,1472]{0,2,1:T(8,128)(2,1)}) %all-gather.12.cloned.1.call-update) | async-done | bytes 3014672 | tf_op jit(solution)/shard_map/all_gather | solution.py:138
  277.3 19.5 %multiply_convert_fusion = (bf16[1024,1792]{1,0:T(8,128)(2,1)S(1)}, bf16[1024,1792]{1,0:T(8,128)(2,1)S(1)}, bf16[1024,1792]{1,0:T(8,128)(2,1)}) fusion(f32[1024,1792]{1,0:T(8,128)} %fusion.55, f32[1024,1792]{1,0:T(8,128)} %fusion.53, bf16[1792,1472]{0,1:T(8,128)(2,1)} %param.27, bf16[1024,1,1472]{0,2,1:T(8,128)(2,1)} %all-gather.12.cloned.1.call-done), kind=kOutput, calls=%fused_computation.22 | convolution fusion | flops 5449973760 | bytes 33980416 | tf_op jit(solution)/shard_map/lrd,fd->lrf/dot_general | solution.py:140
  316.6 42.0 %reduce-scatter.37.cloned.1.call-done = bf16[512,1,1472]{0,2,1:T(8,128)(2,1)} async-done(((bf16[1024,1,1472]{0,2,1:T(8,128)(2,1)}), bf16[512,1,1472]{0,2,1:T(8,128)(2,1)}) %reduce-scatter.37.cloned.1.call-update) | async-done | bytes 1507344 | tf_op jit(solution)/shard_map/reduce_scatter | solution.py:150
  462.6 41.9 %reduce-scatter.53.cloned.1.call-done = bf16[1792,368]{0,1:T(8,128)(2,1)} async-done(((bf16[1792,1472]{0,1:T(8,128)(2,1)}), bf16[1792,368]{0,1:T(8,128)(2,1)}) %reduce-scatter.53.cloned.1.call-update) | async-done | bytes 1318928 | tf_op jit(solution)/shard_map/reduce_scatter | solution.py:245
  507.2 94.6 %reduce-scatter.51.cloned.1.call-done = bf16[368,1792]{1,0:T(8,128)(2,1)} async-done(((bf16[1472,1792]{1,0:T(8,128)(2,1)}), bf16[368,1792]{1,0:T(8,128)(2,1)}) %reduce-scatter.51.cloned.1.call-update) | async-done | bytes 1318928 | tf_op jit(solution)/shard_map/reduce_scatter | solution.py:242
  604.3 94.6 %reduce-scatter.49.cloned.1.call-done = bf16[368,1792]{1,0:T(8,128)(2,1)} async-done(((bf16[1472,1792]{1,0:T(8,128)(2,1)}), bf16[368,1792]{1,0:T(8,128)(2,1)}) %reduce-scatter.49.cloned.1.call-update) | async-done | bytes 1318928 | tf_op jit(solution)/shard_map/reduce_scatter | solution.py:239
  701.4 23.1 %reduce-scatter.61.cloned.1.call-done = bf16[368,192]{1,0:T(8,128)(2,1)} async-done(((bf16[1472,192]{1,0:T(8,128)(2,1)}), bf16[368,192]{1,0:T(8,128)(2,1)}) %reduce-scatter.61.cloned.1.call-update) | async-done | bytes 141328
  726.4 22.7 %reduce-scatter.59.cloned.1.call-done = bf16[368,192]{1,0:T(8,128)(2,1)} async-done(((bf16[1472,192]{1,0:T(8,128)(2,1)}), bf16[368,192]{1,0:T(8,128)(2,1)}) %reduce-scatter.59.cloned.1.call-update) | async-done | bytes 141328
  754.5 18.9 %reduce-scatter.57.cloned.1.call-done = bf16[368,192]{1,0:T(8,128)(2,1)} async-done(((bf16[1472,192]{1,0:T(8,128)(2,1)}), bf16[368,192]{1,0:T(8,128)(2,1)}) %reduce-scatter.57.cloned.1.call-update) | async-done | bytes 141328
  778.8 19.1 %reduce-scatter.55.cloned.1.call-done = bf16[368,192]{1,0:T(8,128)(2,1)} async-done(((bf16[1472,192]{1,0:T(8,128)(2,1)}), bf16[368,192]{1,0:T(8,128)(2,1)}) %reduce-scatter.55.cloned.1.call-update) | async-done | bytes 141328
  826.4 30.1 %reduce-scatter.65.cloned.1.call-done = bf16[448,368]{1,0:T(8,128)(2,1)} async-done(((bf16[1792,368]{1,0:T(8,128)(2,1)}), bf16[448,368]{1,0:T(8,128)(2,1)}) %reduce-scatter.65.cloned.1.call-update) | async-done | bytes 329744
  915.5 16.3 %reduce-scatter.45.cloned.1.call-done = bf16[368,48]{0,1:T(8,128)(2,1)} async-done(((bf16[368,192]{0,1:T(8,128)(2,1)}), bf16[368,48]{0,1:T(8,128)(2,1)}) %reduce-scatter.45.cloned.1.call-update) | async-done | bytes 35344 | tf_op jit(solution)/shard_map/reduce_scatter | solution.py:256
  938.2 16.4 %reduce-scatter.43.cloned.1.call-done = bf16[368,48]{0,1:T(8,128)(2,1)} async-done(((bf16[368,192]{0,1:T(8,128)(2,1)}), bf16[368,48]{0,1:T(8,128)(2,1)}) %reduce-scatter.43.cloned.1.call-update) | async-done | bytes 35344 | tf_op jit(solution)/shard_map/reduce_scatter | solution.py:253
  961.0 16.3 %reduce-scatter.41.cloned.1.call-done = bf16[368,48]{0,1:T(8,128)(2,1)} async-done(((bf16[368,192]{0,1:T(8,128)(2,1)}), bf16[368,48]{0,1:T(8,128)(2,1)}) %reduce-scatter.41.cloned.1.call-update) | async-done | bytes 35344 | tf_op jit(solution)/shard_map/reduce_scatter | solution.py:250
  983.9 37.7 %reduce-scatter.39.cloned.1.call-done = bf16[512,1,1472]{0,2,1:T(8,128)(2,1)} async-done(((bf16[1024,1,1472]{0,2,1:T(8,128)(2,1)}), bf16[512,1,1472]{0,2,1:T(8,128)(2,1)}) %reduce-scatter.39.cloned.1.call-update) | async-done | bytes 1507344 | tf_op jit(solution)/shard_map/reduce_scatter | solution.py:212
  1024.4 40.3 %all-reduce = (f32[1472]{0:T(1024)}, f32[32,6]{0,1:T(8,128)}, f32[1472]{0:T(1024)}) all-reduce(f32[1472]{0:T(1024)S(1)} %get-tuple-element.38, f32[32,6]{0,1:T(8,128)S(1)} %dynamic_update_slice.3, f32[1472]{0:T(1024)S(1)} %get-tuple-element.36), channel_id=1, replica_groups=mesh['dp'=4,'seq'=4,'tensor'=2] {'dp','seq','tensor'}, use_global_device_ids=true, to_apply=%region_17.18 | all-reduce | flops 3136 | bytes 25088 | tf_op jit(solution)/shard_map/psum | solution.py:299
  1072.9 14.2 %all-gather.20.cloned.1.call-done = bf16[1792,368]{1,0:T(8,128)(2,1)} async-done(((bf16[448,368]{1,0:T(8,128)(2,1)}), bf16[1792,368]{1,0:T(8,128)(2,1)}) %all-gather.20.cloned.1.call-update) | async-done | bytes 1318928 | tf_op jit(solution)/shard_map/all_gather | solution.py:291
  1089.9 17.2 %all-gather.18.cloned.1.call-done = bf16[368,1792]{0,1:T(8,128)(2,1)} async-done(((bf16[368,448]{0,1:T(8,128)(2,1)}), bf16[368,1792]{0,1:T(8,128)(2,1)}) %all-gather.18.cloned.1.call-update) | async-done | bytes 1318928 | tf_op jit(solution)/shard_map/all_gather | solution.py:288
  1110.0 17.4 %all-gather.16.cloned.1.call-done = bf16[368,1792]{0,1:T(8,128)(2,1)} async-done(((bf16[368,448]{0,1:T(8,128)(2,1)}), bf16[368,1792]{0,1:T(8,128)(2,1)}) %all-gather.16.cloned.1.call-update) | async-done | bytes 1318928 | tf_op jit(solution)/shard_map/all_gather | solution.py:285
  (257 shorter events, 341.8 us)
Async XLA Ops:
  13.9 168.7 %reduce-scatter.33.cloned.1.call-start = ((), (), s32[]{:S(2)}) async-start(), calls=%async_computation.19 | async-start | bytes 9043968 | tf_op jit(solution)/shard_map/reduce_scatter | solution.py:111
  105.6 126.2 %all-gather.10.cloned.1.call-start = ((), (), s32[]{:S(2)}) async-start(), calls=%async_computation.20 | async-start | bytes 4521984 | tf_op jit(solution)/shard_map/all_gather | solution.py:118
  188.2 89.2 %all-gather.12.cloned.1.call-start = ((), (), s32[]{:S(2)}) async-start(), calls=%async_computation.22 | async-start | bytes 4521984 | tf_op jit(solution)/shard_map/all_gather | solution.py:138
  189.7 168.9 %reduce-scatter.37.cloned.1.call-start = ((), (), s32[]{:S(2)}) async-start(), calls=%async_computation.23 | async-start | bytes 4521984 | tf_op jit(solution)/shard_map/reduce_scatter | solution.py:150
  316.5 91.4 %all-gather.14.cloned.1.call-start = ((), (), s32[]{:S(2)}) async-start(), calls=%async_computation.24 | async-start | bytes 4521984 | tf_op jit(solution)/shard_map/all_gather | solution.py:161
  364.3 140.2 %reduce-scatter.53.cloned.1.call-start = ((), (), s32[]{:S(2)}) async-start(), calls=%async_computation.34 | async-start | bytes 6594560 | tf_op jit(solution)/shard_map/reduce_scatter | solution.py:245
  374.3 227.4 %reduce-scatter.51.cloned.1.call-start = ((), (), s32[]{:S(2)}) async-start(), calls=%async_computation.32 | async-start | bytes 6594560 | tf_op jit(solution)/shard_map/reduce_scatter | solution.py:242
  384.4 314.5 %reduce-scatter.49.cloned.1.call-start = ((), (), s32[]{:S(2)}) async-start(), calls=%async_computation.30 | async-start | bytes 6594560 | tf_op jit(solution)/shard_map/reduce_scatter | solution.py:239
  394.8 329.8 %reduce-scatter.61.cloned.1.call-start = ((), (), s32[]{:S(2)}) async-start(), calls=%async_computation.39 | async-start | bytes 942080
  414.8 334.3 %reduce-scatter.59.cloned.1.call-start = ((), (), s32[]{:S(2)}) async-start(), calls=%async_computation.38 | async-start | bytes 942080
  439.7 333.7 %reduce-scatter.57.cloned.1.call-start = ((), (), s32[]{:S(2)}) async-start(), calls=%async_computation.37 | async-start | bytes 942080
  456.0 341.8 %reduce-scatter.55.cloned.1.call-start = ((), (), s32[]{:S(2)}) async-start(), calls=%async_computation.36 | async-start | bytes 942080
  462.6 363.8 %reduce-scatter.67.cloned.1.call-start = ((), (), s32[]{:S(2)}) async-start(), calls=%async_computation.42 | async-start | bytes 1720320 | tf_op jit(solution)/shard_map/reduce_scatter | solution.py:268
  507.1 349.4 %reduce-scatter.65.cloned.1.call-start = ((), (), s32[]{:S(2)}) async-start(), calls=%async_computation.41 | async-start | bytes 1720320
  604.2 282.2 %reduce-scatter.63.cloned.1.call-start = ((), (), s32[]{:S(2)}) async-start(), calls=%async_computation.40 | async-start | bytes 1720320
  701.4 207.7 %reduce-scatter.47.cloned.1.call-start = ((), (), s32[]{:S(2)}) async-start(), calls=%async_computation.29 | async-start | bytes 184320 | tf_op jit(solution)/shard_map/reduce_scatter | solution.py:259
  726.3 205.5 %reduce-scatter.45.cloned.1.call-start = ((), (), s32[]{:S(2)}) async-start(), calls=%async_computation.28 | async-start | bytes 184320 | tf_op jit(solution)/shard_map/reduce_scatter | solution.py:256
  750.8 203.8 %reduce-scatter.43.cloned.1.call-start = ((), (), s32[]{:S(2)}) async-start(), calls=%async_computation.27 | async-start | bytes 184320 | tf_op jit(solution)/shard_map/reduce_scatter | solution.py:253
  775.1 202.2 %reduce-scatter.41.cloned.1.call-start = ((), (), s32[]{:S(2)}) async-start(), calls=%async_computation.26 | async-start | bytes 184320 | tf_op jit(solution)/shard_map/reduce_scatter | solution.py:250
  799.6 222.0 %reduce-scatter.39.cloned.1.call-start = ((), (), s32[]{:S(2)}) async-start(), calls=%async_computation.25 | async-start | bytes 4521984 | tf_op jit(solution)/shard_map/reduce_scatter | solution.py:212
  806.8 260.2 %reduce-scatter.35.cloned.1.call-start = ((), (), s32[]{:S(2)}) async-start(), calls=%async_computation.21 | async-start | bytes 4521984 | tf_op jit(solution)/shard_map/reduce_scatter | solution.py:126
  817.1 269.9 %all-gather.20.cloned.1.call-start = ((), (), s32[]{:S(2)}) async-start(), calls=%async_computation.35 | async-start | bytes 1720320 | tf_op jit(solution)/shard_map/all_gather | solution.py:291
  826.4 280.7 %all-gather.18.cloned.1.call-start = ((), (), s32[]{:S(2)}) async-start(), calls=%async_computation.33 | async-start | bytes 1720320 | tf_op jit(solution)/shard_map/all_gather | solution.py:288
  856.5 270.8 %all-gather.16.cloned.1.call-start = ((), (), s32[]{:S(2)}) async-start(), calls=%async_computation.31 | async-start | bytes 1720320 | tf_op jit(solution)/shard_map/all_gather | solution.py:285
  (52 other events, 1232.3 us)
Sparse Core Ops, SparseCore 0:
  14.0 46.1 all-gather.7
  105.7 76.8 reduce-scatter.32
  188.3 43.4 all-gather.9
  233.8 43.4 all-gather.11
  316.6 41.8 reduce-scatter.36
  364.5 43.4 all-gather.13
  410.3 94.2 reduce-scatter.52
  506.9 94.7 reduce-scatter.50
  604.0 94.7 reduce-scatter.48
  701.0 23.5 reduce-scatter.60
  726.9 22.1 reduce-scatter.58
  751.2 22.1 reduce-scatter.56
  775.7 22.1 reduce-scatter.54
  800.2 26.0 reduce-scatter.66
  829.5 26.9 reduce-scatter.64
  859.5 26.9 reduce-scatter.62
  889.5 19.5 reduce-scatter.46
  912.1 19.6 reduce-scatter.44
  934.9 19.6 reduce-scatter.42
  957.6 19.6 reduce-scatter.40
  979.6 41.9 reduce-scatter.38
  1023.8 43.1 reduce-scatter.34
  1088.5 18.5 all-gather.17
  1108.7 18.5 all-gather.15
  (1 shorter events, 18.3 us)
where the time goes:
time: 1150 us; the launch traced here: 1140 us
  waiting for transfers between devices  693 us (60%)
  matrix products  245 us (21%)
  local copies, waits for them, and re-layouts  76.7 us (7%)
  blocking collectives  63.2 us (5%)
  other arithmetic  41.9 us (4%)
  between operations  15.9 us (1%)
    unnamed x31, waiting for transfers between devices  116 us
    reduce_scatter x1, waiting for transfers between devices, local(): lax.psum_scatter(grad_gate_w.astype(jnp.bfloat16), 'dp', scatter_dimensio...  94.6 us
    reduce_scatter x1, waiting for transfers between devices, local(): lax.psum_scatter(grad_up_w.astype(jnp.bfloat16), 'dp', scatter_dimension=...  94.6 us
    reduce_scatter x1, waiting for transfers between devices, local(): lax.psum_scatter(jnp.einsum('lrh,hd->lrd', part, output_weight, preferred...  76.4 us
    dot_general x2, matrix products, block_scores(): jnp.einsum('qkb,bh->hqk', picks.astype(jnp.float32), position_bias, preci...  44.1 us
    unnamed x116, local copies, waits for them, and re-layouts  42.9 us
    all_gather x1, waiting for transfers between devices, local(): lax.all_gather(norm_two.astype(jnp.bfloat16), 'tensor', axis=0, tiled=True)  42 us
    reduce_scatter x1, waiting for transfers between devices, local(): lax.psum_scatter((jnp.einsum('lrf,df->lrd', grad_gate, gate_weight, prefe...  42 us
  transfers between devices with their start and end apart: 25, of which 24 were waited for; matrix products, arithmetic and copies ran while one was open for 24% of the time, Pallas kernels for 0%

commit v1 on v0

v1 whole, which is shorter than its diff:
```python
import functools
import math

import jax
import jax.numpy as jnp
from jax import lax
from jax.experimental import pallas as pl
from jax.experimental.pallas import tpu as pltpu
from jax.sharding import PartitionSpec as P

steps_at = (1, 2, 3, 4, 5, 6, 7, 8, 12, 16, 23, 32, 46, 64, 91)
eps_norm = 1e-06
masked_score = -1e30
q_block = 256
band_half = 128
low = jnp.bfloat16
wide = jnp.float32


def dot(a, b, ca, cb):
    return lax.dot_general(a, b, (((ca,), (cb,)), ((), ())), preferred_element_type=wide)


def attn_fwd_kernel(length, bias_ref, q_ref, k_ref, v_ref, seg_k_ref, seg_q_ref, p_ref, o_ref, table):
    block = pl.program_id(0)
    head = pl.program_id(1)
    reach = length - q_block

    @pl.when(block == 0)
    def _():
        table[head, : reach - band_half, :] = jnp.full((reach - band_half, q_block), bias_ref[15, head], wide)
        tail = length + reach - (reach + q_block + band_half)
        table[head, reach + q_block + band_half :, :] = jnp.full((tail, q_block), bias_ref[31, head], wide)
        rows = q_block + 2 * band_half
        d = (
            lax.broadcasted_iota(jnp.int32, (rows, q_block), 0)
            - lax.broadcasted_iota(jnp.int32, (rows, q_block), 1)
            - band_half
        )
        n = jnp.abs(d)
        before = jnp.full((rows, q_block), bias_ref[0, head], wide)
        after = jnp.full((rows, q_block), bias_ref[16, head], wide)
        for number, step in enumerate(steps_at):
            reached = n >= step
            before = jnp.where(reached, bias_ref[number + 1, head], before)
            after = jnp.where(reached, bias_ref[number + 17, head], after)
        table[head, reach - band_half : reach + q_block + band_half, :] = jnp.where(d > 0, after, before)

    first = pl.multiple_of(reach - block * q_block, q_block)
    scores = dot(k_ref[...], q_ref[...], 0, 0) + table[head, pl.ds(first, length), :]
    seg_k = jnp.concatenate([seg_k_ref[...]] * (q_block // 128), axis=1)
    scores = jnp.where(seg_k == seg_q_ref[...], scores, masked_score)
    raised = jnp.exp(scores - jnp.max(scores, axis=0, keepdims=True))
    probs = (raised * (1.0 / jnp.sum(raised, axis=0, keepdims=True))).astype(low)
    p_ref[0] = probs
    o_ref[...] = dot(v_ref[...], probs, 1, 0).astype(low)


def attn_forward(qkv, seg, bias):
    width, length = qkv.shape
    heads = bias.shape[1]
    dim = width // (3 * heads)
    seg_k = jnp.broadcast_to(seg[:, None], (length, 128))
    seg_q = seg[None, :]
    blocks = length // q_block
    return pl.pallas_call(
        functools.partial(attn_fwd_kernel, length),
        grid=(blocks, heads),
        in_specs=[
            pl.BlockSpec(memory_space=pltpu.SMEM),
            pl.BlockSpec((dim, q_block), lambda b, h: (h, b)),
            pl.BlockSpec((dim, length), lambda b, h: (heads + h, 0)),
            pl.BlockSpec((dim, length), lambda b, h: (2 * heads + h, 0)),
            pl.BlockSpec((length, 128), lambda b, h: (0, 0)),
            pl.BlockSpec((1, q_block), lambda b, h: (0, b)),
        ],
        out_specs=[
            pl.BlockSpec((1, length, q_block), lambda b, h: (h, 0, b)),
            pl.BlockSpec((dim, q_block), lambda b, h: (h, b)),
        ],
        out_shape=[
            jax.ShapeDtypeStruct((heads, length, length), low),
            jax.ShapeDtypeStruct((heads * dim, length), low),
        ],
        scratch_shapes=[pltpu.VMEM((heads, 2 * length - q_block, q_block), wide)],
        compiler_params=pltpu.CompilerParams(vmem_limit_bytes=48 << 20),
        cost_estimate=pl.CostEstimate(
            flops=4 * heads * length * length * dim * 4,
            bytes_accessed=2 * heads * length * length + 8 * width * length,
            transcendentals=heads * length * length,
        ),
        name="attn_forward",
    )(bias, qkv, qkv, qkv, seg_k, seg_q)


def attn_bwd_kernel(length, q_ref, k_ref, v_ref, go_ref, o_ref, p_ref, gq_ref, gk_ref, gv_ref, gb_ref, k_acc, v_acc, sums):
    block = pl.program_id(1)
    reach = length - q_block

    @pl.when(block == 0)
    def _():
        k_acc[...] = jnp.zeros_like(k_acc)
        v_acc[...] = jnp.zeros_like(v_acc)
        sums[...] = jnp.zeros_like(sums)

    probs = p_ref[0]
    go = go_ref[...]
    inner = jnp.sum(go.astype(wide) * o_ref[...].astype(wide), axis=0, keepdims=True)
    scores = probs.astype(wide) * (dot(v_ref[...], go, 0, 0) - inner)
    first = pl.multiple_of(reach - block * q_block, q_block)
    sums[pl.ds(first, length), :] += scores
    scores = scores.astype(low)
    gq_ref[...] = dot(k_ref[...], scores, 1, 0).astype(low)
    k_acc[...] += dot(q_ref[...], scores, 1, 1)
    v_acc[...] += dot(go, probs, 1, 1)

    @pl.when(block == pl.num_programs(1) - 1)
    def _():
        gk_ref[...] = k_acc[...].astype(low)
        gv_ref[...] = v_acc[...].astype(low)
        rows = q_block + 2 * band_half
        d = (
            lax.broadcasted_iota(jnp.int32, (rows, q_block), 0)
            - lax.broadcasted_iota(jnp.int32, (rows, q_block), 1)
            - band_half
        )
        n = jnp.abs(d)
        near = sums[reach - band_half : reach + q_block + band_half, :]
        far_before = jnp.sum(sums[: reach - band_half, :], axis=0, keepdims=True)
        far_after = jnp.sum(sums[reach + q_block + band_half :, :], axis=0, keepdims=True)
        bucket = jnp.zeros((rows, q_block), jnp.int32)
        for step in steps_at:
            bucket = bucket + jnp.where(n >= step, 1, 0)
        bucket = bucket + jnp.where(d > 0, 16, 0)
        for b in range(32):
            total = jnp.sum(jnp.where(bucket == b, near, 0.0), axis=0, keepdims=True)
            if b == 15:
                total = total + far_before
            if b == 31:
                total = total + far_after
            gb_ref[0, b : b + 1, :] = total


def attn_backward(qkv, grad_mixed, mixed, probs):
    width, length = qkv.shape
    heads = probs.shape[0]
    dim = width // (3 * heads)
    blocks = length // q_block
    half = pl.BlockSpec((dim, q_block), lambda h, b: (h, b))
    whole = pl.BlockSpec((dim, length), lambda h, b: (h, 0))
    gq, gk, gv, gb = pl.pallas_call(
        functools.partial(attn_bwd_kernel, length),
        grid=(heads, blocks),
        in_specs=[
            half,
            pl.BlockSpec((dim, length), lambda h, b: (heads + h, 0)),
            pl.BlockSpec((dim, length), lambda h, b: (2 * heads + h, 0)),
            half,
            half,
            pl.BlockSpec((1, length, q_block), lambda h, b: (h, 0, b)),
        ],
        out_specs=[half, whole, whole, pl.BlockSpec((1, 32, q_block), lambda h, b: (h, 0, 0))],
        out_shape=[
            jax.ShapeDtypeStruct((heads * dim, length), low),
            jax.ShapeDtypeStruct((heads * dim, length), low),
            jax.ShapeDtypeStruct((heads * dim, length), low),
            jax.ShapeDtypeStruct((heads, 32, q_block), wide),
        ],
        scratch_shapes=[
            pltpu.VMEM((dim, length), wide),
            pltpu.VMEM((dim, length), wide),
            pltpu.VMEM((2 * length - q_block, q_block), wide),
        ],
        compiler_params=pltpu.CompilerParams(vmem_limit_bytes=48 << 20),
        cost_estimate=pl.CostEstimate(
            flops=8 * heads * length * length * dim * 4,
            bytes_accessed=2 * heads * length * length + 16 * width * length,
            transcendentals=0,
        ),
        name="attn_backward",
    )(qkv, qkv, qkv, grad_mixed, mixed, probs)
    return jnp.concatenate([gq, gk, gv], axis=0), jnp.sum(gb, axis=2).T


def ffn_kernel(*refs):
    (x_ref, g_ref, gate_w, up_w, down_w), refs = refs[:5], refs[-9:]
    hid_ref, gg_ref, gu_ref, out_ref, gx_ref, xs, gs, out_acc, gx_acc = refs
    step = pl.program_id(0)

    @pl.when(step == 0)
    def _():
        xs[...] = x_ref[...].T
        gs[...] = g_ref[...].T
        out_acc[...] = jnp.zeros_like(out_acc)
        gx_acc[...] = jnp.zeros_like(gx_acc)

    gate = dot(xs[...], gate_w[...], 1, 0)
    up = dot(xs[...], up_w[...], 1, 0)
    grad = dot(gs[...], down_w[...], 1, 0)
    c = math.sqrt(2.0 / math.pi)
    square = gate * gate
    t = jnp.tanh(c * gate * (1.0 + 0.044715 * square))
    half = 0.5 * (1.0 + t)
    gelu = gate * half
    slope = half + 0.5 * gate * (1.0 - t * t) * (c * (1.0 + 3 * 0.044715 * square))
    hid = (gelu * up).astype(low)
    gg = (grad * up * slope).astype(low)
    gu = (grad * gelu).astype(low)
    hid_ref[...] = hid
    gg_ref[...] = gg
    gu_ref[...] = gu
    out_acc[...] += dot(down_w[...], hid, 1, 1)
    gx_acc[...] += dot(gate_w[...], gg, 1, 1) + dot(up_w[...], gu, 1, 1)

    @pl.when(step == pl.num_programs(0) - 1)
    def _():
        out_ref[...] = out_acc[...].astype(out_ref.dtype)
        gx_ref[...] = gx_acc[...].astype(gx_ref.dtype)


def ffn(x, g, gate_w, up_w, down_w, kept, slot, slots, kind):
    width, tokens = x.shape
    hidden = gate_w.shape[1]
    tile = 256
    full = pl.BlockSpec((width, tokens), lambda j: (0, 0), pipeline_mode=pl.Buffered(1))
    weight = pl.BlockSpec((width, tile), lambda j: (0, j))
    act = pl.BlockSpec((tokens, tile), lambda j: (slot, j))
    act_shape = jax.ShapeDtypeStruct((slots * tokens, hidden), low)
    args = [x, g, gate_w, up_w, down_w]
    specs = [full, full, weight, weight, weight]
    alias = {}
    if kept is not None:
        args += list(kept)
        specs += [pl.BlockSpec(memory_space=pl.ANY)] * 3
        alias = {5: 0, 6: 1, 7: 2}
    hid, gg, gu, out, gx = pl.pallas_call(
        ffn_kernel,
        grid=(hidden // tile,),
        in_specs=specs,
        out_specs=[act, act, act, full, full],
        out_shape=[act_shape, act_shape, act_shape]
        + [jax.ShapeDtypeStruct((width, tokens), kind)] * 2,
        scratch_shapes=[
            pltpu.VMEM((tokens, width), low),
            pltpu.VMEM((tokens, width), low),
            pltpu.VMEM((width, tokens), wide),
            pltpu.VMEM((width, tokens), wide),
        ],
        input_output_aliases=alias,
        compiler_params=pltpu.CompilerParams(vmem_limit_bytes=56 << 20),
        cost_estimate=pl.CostEstimate(
            flops=12 * tokens * width * hidden,
            bytes_accessed=6 * width * hidden + 8 * width * tokens + 6 * tokens * hidden,
            transcendentals=tokens * hidden,
        ),
        name="ffn_both_ways",
    )(*args)
    return (hid, gg, gu), out, gx


def norm_of(values, gain):
    scale = lax.rsqrt(jnp.mean(values * values, axis=0, keepdims=True) + eps_norm)
    return values * scale * gain, scale


def norm_back(values, scale, gain, grad):
    normed = values * scale
    pushed = gain * grad
    mean = jnp.mean(normed * pushed, axis=0, keepdims=True)
    return scale * (pushed - normed * mean), jnp.sum(grad * normed, axis=1)


class Moves:
    def __init__(self, mesh):
        self.nz = mesh.shape["dp"]
        self.nseq = mesh.shape["seq"]
        self.ny = mesh.shape["tensor"]
        self.nx = self.nseq // 2
        both = [(m, c, y) for m in range(self.nx) for c in range(2) for y in range(2)]
        at = lambda m, c, y: (m * 2 + c) * 2 + y
        self.swap_pairs = [(at(m, c, y), at(m, y, c)) for m, c, y in both]
        self.second_pairs = [(at(m, c, y), at(m, y, 1 - c)) for m, c, y in both]
        self.back_pairs = [(b, a) for a, b in self.second_pairs]
        self.core_pairs = [(m * 2 + c, m * 2 + 1 - c) for m in range(self.nx) for c in range(2)]
        self.ring_x = [(m * 2 + c, (m + 1) % self.nx * 2 + c) for m in range(self.nx) for c in range(2)]
        self.ring_z = [(z, (z + 1) % self.nz) for z in range(self.nz)]

    def swap(self, a):
        return lax.ppermute(a, ("seq", "tensor"), self.swap_pairs)

    def second(self, a):
        return lax.ppermute(a, ("seq", "tensor"), self.second_pairs)

    def back(self, a):
        return lax.ppermute(a, ("seq", "tensor"), self.back_pairs)

    def core(self, a):
        return lax.ppermute(a, "seq", self.core_pairs)

    def over_y(self, a):
        return lax.ppermute(a, "tensor", [(0, 1), (1, 0)])

    def ring(self, take, me, n, axis, pairs):
        if n == 1:
            return take(me)
        held = take((me + n - 1) % n)
        for t in range(1, n):
            got = lax.ppermute(held.astype(low), axis, pairs)
            held = got.astype(wide) + take((me + 2 * n - 1 - t) % n).astype(wide)
        return held.astype(low)

    def over_x_then_z(self, a, m, z):
        a = self.ring(lambda i: lax.dynamic_index_in_dim(a, i, 1, False), m, self.nx, "seq", self.ring_x)
        return self.ring(lambda i: lax.dynamic_index_in_dim(a, i, 0, False), z, self.nz, "dp", self.ring_z)

    def over_z_then_x(self, a, m, z):
        a = self.ring(lambda i: lax.dynamic_index_in_dim(a, i, 0, False), z, self.nz, "dp", self.ring_z)
        return self.ring(lambda i: lax.dynamic_index_in_dim(a, i, 0, False), m, self.nx, "seq", self.ring_x)

    def gather_x_core(self, piece, m, c):
        rows, columns = piece.shape
        if self.nx == 2:
            over = lax.ppermute(piece, "seq", self.ring_x)
            here = jnp.where(m == 0, jnp.concatenate([piece, over], 0), jnp.concatenate([over, piece], 0))
            there = self.core(here)
            return jnp.where(
                c == 0, jnp.concatenate([here, there], 1), jnp.concatenate([there, here], 1)
            )
        got = lax.all_gather(piece, "seq").reshape(self.nx, 2, rows, columns)
        return got.transpose(0, 2, 1, 3).reshape(self.nx * rows, 2 * columns)


def segment_ids(lengths, valid, length):
    ends = jnp.sum(jnp.where(jnp.arange(4)[None, :] <= jnp.arange(4)[:, None], lengths[None, :], 0), axis=1)
    where_at = jnp.arange(length, dtype=jnp.int32)
    counted = jnp.sum((where_at[:, None] >= ends[None, :]).astype(jnp.int32), axis=1)
    return jnp.where(where_at < valid, counted, 4)


def local(
    mesh,
    layer_in,
    out_grad,
    doc_lengths,
    valid_length,
    gain_attn,
    query_weight,
    key_weight,
    value_weight,
    position_bias,
    output_weight,
    gain_ffn,
    gate_weight,
    up_weight,
    down_weight,
):
    moves = Moves(mesh)
    half_len, _, width = layer_in.shape
    length = 2 * half_len
    heads = position_bias.shape[1]
    inner_width = query_weight.shape[1]
    s = lax.axis_index("seq")
    y = lax.axis_index("tensor")
    z = lax.axis_index("dp")
    c = s % 2
    m = s // 2

    x_in = moves.swap(layer_in.reshape(half_len, width).T)
    qkv_w = jnp.concatenate([query_weight.T, key_weight.T, value_weight.T], axis=0)
    qkv_w = moves.swap(qkv_w)
    facts = moves.swap(jnp.concatenate([doc_lengths[0], valid_length]))
    bias = moves.swap(position_bias)
    out_w = moves.swap(output_weight)
    positions = y * half_len + jnp.arange(half_len, dtype=jnp.int32)
    g_in = jnp.where((positions < valid_length[0])[None, :], out_grad.reshape(half_len, width).T, 0)
    g_in = g_in.astype(low)
    g_own = moves.swap(g_in)
    g_oth = moves.second(g_in)
    segment = segment_ids(facts[:4], facts[4], length)
    gain_one = gain_attn.astype(wide)[:, None]
    gain_two = gain_ffn.astype(wide)[:, None]

    def both_halves(own):
        other = moves.core(own)
        return jnp.where(
            c == 0, jnp.concatenate([own, other], 1), jnp.concatenate([other, own], 1)
        )

    def my_half(a):
        return lax.dynamic_slice_in_dim(a, c * half_len, half_len, 1)

    def other_half(a):
        return lax.dynamic_slice_in_dim(a, (1 - c) * half_len, half_len, 1)

    x_wide = x_in.astype(wide)
    normed, scale_one = norm_of(x_wide, gain_one)
    xn_one = both_halves(normed.astype(low))
    qkv = dot(qkv_w, xn_one, 1, 0).astype(low)
    probs, mixed = attn_forward(qkv, segment, bias)
    sent = dot(out_w, other_half(mixed), 0, 0).astype(low)
    hres = x_wide + dot(out_w, my_half(mixed), 0, 0) + moves.core(sent).astype(wide)

    normed, scale_two = norm_of(hres, gain_two)
    xn_own = normed.astype(low)
    xn_oth = moves.over_y(xn_own)
    down_t = down_weight.T
    kept, out_own, gx_own = ffn(xn_own, g_own, gate_weight, up_weight, down_t, None, 0, 2, wide)
    kept, out_oth, gx_oth = ffn(xn_oth, g_oth, gate_weight, up_weight, down_t, kept, 1, 2, low)
    hid, grad_gate, grad_up = kept
    gx = gx_own + moves.over_y(gx_oth).astype(wide)
    out_y = moves.swap((hres + out_own).astype(low)).astype(wide) + moves.back(out_oth).astype(wide)
    out_y = out_y.astype(low)

    def ffn_weight_grad(left_own, left_oth, right, x_first):
        left = jnp.concatenate([left_own, left_oth], axis=1)
        columns = right.shape[1] // 2
        send = dot(left, lax.dynamic_slice_in_dim(right, (1 - c) * columns, columns, 1), 1, 0)
        got = moves.core(send.astype(low))
        keep = dot(left, lax.dynamic_slice_in_dim(right, c * columns, columns, 1), 1, 0)
        total = (keep + got.astype(wide)).astype(low)
        total = total.reshape(moves.nz, moves.nx, -1, columns)
        piece = (moves.over_x_then_z if x_first else moves.over_z_then_x)(total, m, z)
        return moves.gather_x_core(piece, m, c).astype(wide)

    sum_d = ffn_weight_grad(g_own, g_oth, hid, False)
    sum_g = ffn_weight_grad(xn_own, xn_oth, grad_gate, True)
    sum_u = ffn_weight_grad(xn_own, xn_oth, grad_up, True)

    back, grad_gain_two = norm_back(hres, scale_two, gain_two, gx)
    grad_hres = g_own.astype(wide) + back
    branch = both_halves(grad_hres.astype(low))

    grad_mixed = dot(out_w, branch, 1, 0).astype(low)
    grad_qkv, grad_bias = attn_backward(qkv, grad_mixed, mixed, probs)
    grad_attn_w = jnp.concatenate(
        [dot(xn_one, grad_qkv, 1, 1).astype(low), dot(branch, mixed, 1, 1).astype(low)], axis=1
    )
    sent = dot(qkv_w, other_half(grad_qkv), 0, 0).astype(low)
    gx = dot(qkv_w, my_half(grad_qkv), 0, 0) + moves.core(sent).astype(wide)
    back, grad_gain_one = norm_back(x_wide, scale_one, gain_one, gx)
    grad_in = moves.swap((grad_hres + back).astype(low)).astype(wide)

    columns = grad_attn_w.shape[1] // 2
    got = moves.over_y(lax.dynamic_slice_in_dim(grad_attn_w, (1 - y) * columns, columns, 1))
    total = lax.dynamic_slice_in_dim(grad_attn_w, y * columns, columns, 1).astype(wide) + got.astype(wide)
    total = total.astype(low).reshape(moves.nz, moves.nx, -1, columns)
    piece = moves.over_x_then_z(total, m, z)
    pieces = lax.all_gather(piece, ("seq", "tensor")).reshape(moves.nx, 2, 2, -1, columns)
    pieces = lax.dynamic_index_in_dim(pieces, y, 1, False)
    sums = pieces.transpose(0, 2, 1, 3).reshape(-1, 2 * columns).astype(wide)
    sum_q, sum_k, sum_v, sum_o = (
        sums[:, i * inner_width : (i + 1) * inner_width] for i in range(4)
    )

    bias_full = jnp.zeros((grad_bias.shape[0], 2 * heads), wide)
    bias_full = lax.dynamic_update_slice(bias_full, grad_bias, (jnp.int32(0), c * heads))
    gain_one_sum, gain_two_sum, bias_sum = lax.psum(
        (grad_gain_one, grad_gain_two, bias_full), ("dp", "seq", "tensor")
    )
    return (
        out_y.T.reshape(half_len, 1, width),
        grad_in.T.reshape(half_len, 1, width),
        gain_one_sum,
        sum_q,
        sum_k,
        sum_v,
        bias_sum,
        sum_o.T,
        gain_two_sum,
        sum_g,
        sum_u,
        sum_d.T,
    )


def solution(mesh):
    rows = P("tensor", ("dp", "seq"), None)
    columns = P(None, "tensor")
    return jax.shard_map(
        functools.partial(local, mesh),
        mesh=mesh,
        in_specs=(
            rows,
            rows,
            P(("dp", "seq"), None),
            P(("dp", "seq")),
            P(),
            columns,
            columns,
            columns,
            columns,
            P("tensor", None),
            P(),
            columns,
            columns,
            P("tensor", None),
        ),
        out_specs=(
            rows,
            rows,
            P(),
            P("dp", "tensor"),
            P("dp", "tensor"),
            P("dp", "tensor"),
            P(),
            P("tensor", "dp"),
            P(),
            P("dp", "tensor"),
            P("dp", "tensor"),
            P("tensor", "dp"),
        ),
        check_vma=False,
    )
```

time: 1150 us -> 489 us (0.43)
  waiting for transfers between devices: 693 us -> 108 us
  matrix products: 245 us -> 58.3 us
  starting transfers between devices: 1.03 us -> 117 us
  Pallas kernels: 0 us -> 88.4 us
  local copies, waits for them, and re-layouts: 76.7 us -> 14 us
  blocking collectives: 63.2 us -> 37.8 us
    reduce_scatter x12 -> x0, waiting for transfers between devices: 458 us -> none  [the longest x1 94.6 us: local(): lax.psum_scatter(grad_gate_w.astype(jnp.bfloat16), 'dp', scatter_dimensio...]
    dot_general x37 -> x14, matrix products: 245 us -> 58.3 us  [dot(): lax.dot_general(a, b, (((ca,), (cb,)), ((), ())), preferred_element_type=...]
    all_gather x7 -> x1, waiting for transfers between devices: 119 us -> 0.01 us  [local(): lax.all_gather(piece, ('seq', 'tensor'))]
    ppermute x0 -> x42, starting transfers between devices: none -> 117 us  [the longest x8 58.1 us: swap(): return lax.ppermute(a, ('seq', 'tensor'), self.swap_pairs)]
    unnamed x31 -> x1, waiting for transfers between devices: 116 us -> 0.02 us
    ppermute x0 -> x42, waiting for transfers between devices: none -> 108 us  [the longest x16 79 us: ring(): got = lax.ppermute(held.astype(low), axis, pairs)]
    pallas_call x0 -> x4, Pallas kernels: none -> 88.4 us  [the longest x2 53.1 us: ffn(): pl.pallas_call(ffn_kernel, grid=(hidden // tile,), in_specs=specs, out_sp...]
    unnamed x116 -> x61, local copies, waits for them, and re-layouts: 42.9 us -> 6.97 us
  transfers between devices with their start and end apart: 25 -> 43, of which waited for: 24 -> 14; matrix products, arithmetic and copies ran while one was open for 24% -> 22% of each run, Pallas kernels for 0% -> 13%
where the time goes in v1:
time: 489 us; the launch traced here: 481 us
  starting transfers between devices  117 us (24%)
  waiting for transfers between devices  108 us (22%)
  Pallas kernels  88.4 us (18%)
  matrix products  58.3 us (12%)
  other arithmetic  42.2 us (9%)
  blocking collectives  37.8 us (8%)
  between operations  15.7 us (3%)
  local copies, waits for them, and re-layouts  14 us (3%)
    ppermute x16, waiting for transfers between devices, ring(): got = lax.ppermute(held.astype(low), axis, pairs)  79 us
    dot_general x14, matrix products, dot(): lax.dot_general(a, b, (((ca,), (cb,)), ((), ())), preferred_element_type=...  58.3 us
    ppermute x8, starting transfers between devices, swap(): return lax.ppermute(a, ('seq', 'tensor'), self.swap_pairs)  58.1 us
    pallas_call x2, Pallas kernels, ffn(): pl.pallas_call(ffn_kernel, grid=(hidden // tile,), in_specs=specs, out_sp...  53.1 us
    ppermute x10, starting transfers between devices, core(): return lax.ppermute(a, 'seq', self.core_pairs)  41.3 us
    psum x1, blocking collectives, local(): lax.psum((grad_gain_one, grad_gain_two, bias_full), ('dp', 'seq', 'tensor'))  37.8 us
    ppermute x3, waiting for transfers between devices, over_y(): return lax.ppermute(a, 'tensor', [(0, 1), (1, 0)])  28.5 us
    pallas_call x1, Pallas kernels, attn_backward(): pl.pallas_call(functools.partial(attn_bwd_kernel, length), grid=(heads, b...  20.6 us
  transfers between devices with their start and end apart: 43, of which 14 were waited for; matrix products, arithmetic and copies ran while one was open for 22% of the time, Pallas kernels for 13%

profile of v1, /device:TPU:0, one launch (start us, length us, event | category | flops | bytes accessed | tf_op | source)
XLA Modules:
  0.0 481.1 jit_solution(17813699113871608203)
XLA Ops:
  12.0 14.9 %collective-permute-start.2 = (bf16[576,1472]{1,0:T(8,128)(2,1)}, bf16[576,1472]{1,0:T(8,128)(2,1)}, u32[]{:S(2)}, u32[]{:S(2)}) collective-permute-start(bf16[576,1472]{1,0:T(8,128)(2,1)} %pad_maximum_fusion.1), channel_id=1, source_target_pairs={{0,0},{1,2},{2,1},{3,3},{4,4},{5,6},{6,5},{7,7},{8,8},{9,10},{10,9... | collective-permute-start | bytes 5087240 | tf_op jit(solution)/shard_map/ppermute | solution.py:289
  33.7 12.7 %collective-permute-start.7 = (bf16[1472,512]{1,0:T(8,128)(2,1)}, bf16[1472,512]{1,0:T(8,128)(2,1)}, u32[]{:S(2)}, u32[]{:S(2)}) collective-permute-start(bf16[1472,512]{1,0:T(8,128)(2,1)} %fusion.23), channel_id=1, source_target_pairs={{0,0},{1,2},{2,1},{3,3},{4,4},{5,6},{6,5},{7,7},{8,8},{9,10},{10,9... | collective-permute-start | bytes 4521992 | tf_op jit(solution)/shard_map/ppermute | solution.py:289
  51.8 5.4 %convolution_convert_fusion.7.q_ref.k_ref.v_ref = bf16[576,1024]{1,0:T(8,128)(2,1)S(1)} fusion(bf16[576,1472]{1,0:T(8,128)(2,1)} %collective-permute-done.2, bf16[1472,512]{1,0:T(8,128)(2,1)} %collective-permute-done.3, bf16[1472,512]{1,0:T(8,128)(2,1)} %fusion.5, pred[]{:T(512)S(6)} %eq.38), kind=kOutput, calls=%fused_computation.58 | convolution fusion | flops 1750597632 | bytes 5890049 | tf_op jit(solution)/shard_map/dot_general | solution.py:21
  57.4 14.8 %attn_forward.1 = (bf16[3,1024,1024]{2,1,0:T(8,128)(2,1)}, bf16[192,1024]{1,0:T(8,128)(2,1)S(1)}) custom-call(f32[32,3]{1,0:T(8,128)S(1)} %collective-permute-done.1.bias_ref, bf16[576,1024]{1,0:T(8,128)(2,1)S(1)} %convolution_convert_fusion.7.q_ref.k_ref.v_ref, bf16[576,1024]{1,0:T(8,128)(2,1)S(1)} %convolution_convert_fusion.7.q_ref.k_ref.v_ref, ...), custom_call_target="tpu_custom_call" | custom-call | flops 3221225472 | bytes 11010048 | tf_op jit(solution)/shard_map/attn_forward/pallas_call | solution.py:66
  74.7 37.1 %collective-permute-start.6 = (bf16[1472,512]{1,0:T(8,128)(2,1)}, bf16[1472,512]{1,0:T(8,128)(2,1)}, u32[]{:S(2)}, u32[]{:S(2)}) collective-permute-start(bf16[1472,512]{1,0:T(8,128)(2,1)} %fusion.13), channel_id=1, source_target_pairs={{0,2},{2,0},{4,6},{6,4},{1,3},{3,1},{5,7},{7,5},{8,10},{10,8},{12,... | collective-permute-start | bytes 4521992 | tf_op jit(solution)/shard_map/ppermute | solution.py:298
  120.5 27.0 %ffn_both_ways.2 = (bf16[1024,1792]{1,0:T(8,128)(2,1)}, bf16[1024,1792]{1,0:T(8,128)(2,1)}, bf16[1024,1792]{1,0:T(8,128)(2,1)}, f32[1472,512]{1,0:T(8,128)}, f32[1472,512]{1,0:T(8,128)}) custom-call(bf16[1472,512]{1,0:T(8,128)(2,1)} %copy-done.14, bf16[1472,512]{1,0:T(8,128)(2,1)} %collective-permute-done.7.refs_1_, bf16[1472,1792]{1,0:T(8,128)(2,1)} %refs_2_.3, ...), custom_call_target="tpu_custom_call" | custom-call | flops 16206790656 | bytes 27361280 | tf_op jit(solution)/shard_map/ffn_both_ways/pallas_call | solution.py:236
  147.5 6.7 %collective-permute-done.9.refs_0_ = bf16[1472,512]{1,0:T(8,128)(2,1)} collective-permute-done((bf16[1472,512]{1,0:T(8,128)(2,1)S(1)}, bf16[1472,512]{1,0:T(8,128)(2,1)}, u32[]{:S(2)}, u32[]{:S(2)}) %collective-permute-start.9) | collective-permute-done | bytes 1507360 | tf_op jit(solution)/shard_map/ppermute | solution.py:301
  154.3 26.1 %ffn_both_ways.3 = (bf16[1024,1792]{1,0:T(8,128)(2,1)}, bf16[1024,1792]{1,0:T(8,128)(2,1)}, bf16[1024,1792]{1,0:T(8,128)(2,1)}, bf16[1472,512]{1,0:T(8,128)(2,1)}, bf16[1472,512]{1,0:T(8,128)(2,1)}) custom-call(bf16[1472,512]{1,0:T(8,128)(2,1)} %collective-permute-done.9.refs_0_, ...), custom_call_target="tpu_custom_call", output_to_operand_aliasing={{0}: (5, {}), {1}: (6, {}), {2}: (7, {})} | custom-call | flops 16206790656 | bytes 27361280 | tf_op jit(solution)/shard_map/ffn_both_ways/pallas_call | solution.py:236
  182.2 7.3 %convolution_convert_fusion = bf16[1472,896]{1,0:T(8,128)(2,1)} fusion(bf16[1472,1024]{1,0:T(8,128)(2,1)} %copy-done.16, bf16[1024,1792]{1,0:T(8,128)(2,1)} %get-tuple-element.43, s32[]{:T(128)S(6)} %select_n.247), kind=kOutput, calls=%fused_computation.10 | convolution fusion | flops 2702450688 | bytes 7487492 | tf_op jit(solution)/shard_map/dot_general | solution.py:21
  200.8 15.1 %collective-permute-done.12 = bf16[1472,512]{1,0:T(8,128)(2,1)S(1)} collective-permute-done((bf16[1472,512]{1,0:T(8,128)(2,1)}, bf16[1472,512]{1,0:T(8,128)(2,1)S(1)}, u32[]{:S(2)}, u32[]{:S(2)}) %collective-permute-start.12) | collective-permute-done | bytes 1507360 | tf_op jit(solution)/shard_map/ppermute | solution.py:301
  221.5 12.7 %collective-permute-start.8 = (bf16[1472,512]{1,0:T(8,128)(2,1)}, bf16[1472,512]{1,0:T(8,128)(2,1)}, u32[]{:S(2)}, u32[]{:S(2)}) collective-permute-start(bf16[1472,512]{1,0:T(8,128)(2,1)} %get-tuple-element.101), channel_id=1, source_target_pairs={{0,0},{1,2},{2,1},{3,3},{4,4},{5,6},{6,5},{7,7},{8,8},{9,10},{10,9... | collective-permute-start | bytes 4521992 | tf_op jit(solution)/shard_map/ppermute | solution.py:289
  234.2 5.4 %add_convert_fusion = bf16[1472,896]{1,0:T(8,128)(2,1)S(1)} fusion(bf16[1472,896]{1,0:T(8,128)(2,1)} %collective-permute-done.35, bf16[1472,1024]{1,0:T(8,128)(2,1)S(1)} %copy-done.17, bf16[1024,1792]{1,0:T(8,128)(2,1)} %get-tuple-element.43, s32[]{:T(128)S(6)} %select_n.246), kind=kOutput, calls=%fused_computation | convolution fusion | flops 2705088512 | bytes 10125316 | tf_op jit(solution)/shard_map/dot_general | solution.py:21
  259.0 20.6 %attn_backward.1 = (bf16[192,1024]{1,0:T(8,128)(2,1)S(1)}, bf16[192,1024]{1,0:T(8,128)(2,1)S(1)}, bf16[192,1024]{1,0:T(8,128)(2,1)S(1)}, f32[3,32,256]{2,1,0:T(8,128)S(1)}) custom-call(bf16[576,1024]{1,0:T(8,128)(2,1)S(1)} %convolution_convert_fusion.7.q_ref.k_ref.v_ref, bf16[576,1024]{1,0:T(8,128)(2,1)S(1)} %convolution_convert_fusion.7.q_ref.k_ref.v_ref, ...), custom_call_target="tpu_custom_call" | custom-call | flops 6442450944 | bytes 15728640 | tf_op jit(solution)/shard_map/attn_backward/pallas_call | solution.py:151
  279.7 5.5 %convolution_convert_fusion.3 = bf16[1472,576]{1,0:T(8,128)(2,1)S(1)} fusion(bf16[576,1024]{1,0:T(8,128)(2,1)S(1)} %constant_dynamic-update-slice_fusion, bf16[1472,512]{1,0:T(8,128)(2,1)} %collective-permute-done.3, bf16[1472,512]{1,0:T(8,128)(2,1)} %fusion.5, pred[]{:T(512)S(6)} %eq.38), kind=kOutput, calls=%fused_computation.16 | convolution fusion | flops 1750855680 | bytes 5890049 | tf_op jit(solution)/shard_map/dot_general | solution.py:21
  301.9 8.7 %collective-permute-done.37 = bf16[2,184,896]{2,1,0:T(8,128)(2,1)S(1)} collective-permute-done((bf16[2,184,896]{2,1,0:T(8,128)(2,1)S(1)}, bf16[2,184,896]{2,1,0:T(8,128)(2,1)S(1)}, u32[]{:S(2)}, u32[]{:S(2)}) %collective-permute-start.37) | collective-permute-done | bytes 659488 | tf_op jit(solution)/shard_map/ppermute | solution.py:308
  310.8 6.7 %collective-permute-done.16 = bf16[1472,384]{1,0:T(8,128)(2,1)S(1)} collective-permute-done((bf16[1472,384]{1,0:T(8,128)(2,1)S(1)}, bf16[1472,384]{1,0:T(8,128)(2,1)S(1)}, u32[]{:S(2)}, u32[]{:S(2)}) %collective-permute-start.16) | collective-permute-done | bytes 1130528 | tf_op jit(solution)/shard_map/ppermute | solution.py:301
  335.6 6.5 %collective-permute-done.31 = bf16[184,896]{1,0:T(8,128)(2,1)S(1)} collective-permute-done((bf16[184,896]{1,0:T(8,128)(2,1)S(1)}, bf16[184,896]{1,0:T(8,128)(2,1)S(1)}, u32[]{:S(2)}, u32[]{:S(2)}) %collective-permute-start.31) | collective-permute-done | bytes 329760 | tf_op jit(solution)/shard_map/ppermute | solution.py:308
  342.2 7.0 %collective-permute-done.24 = bf16[184,896]{1,0:T(8,128)(2,1)S(1)} collective-permute-done((bf16[184,896]{1,0:T(8,128)(2,1)S(1)}, bf16[184,896]{1,0:T(8,128)(2,1)S(1)}, u32[]{:S(2)}, u32[]{:S(2)}) %collective-permute-start.24) | collective-permute-done | bytes 329760 | tf_op jit(solution)/shard_map/ppermute | solution.py:308
  349.5 13.8 %collective-permute-done.38 = bf16[2,184,896]{2,1,0:T(8,128)(2,1)S(1)} collective-permute-done((bf16[2,184,896]{2,1,0:T(8,128)(2,1)S(1)}, bf16[2,184,896]{2,1,0:T(8,128)(2,1)S(1)}, u32[]{:S(2)}, u32[]{:S(2)}) %collective-permute-start.38) | collective-permute-done | bytes 659488 | tf_op jit(solution)/shard_map/ppermute | solution.py:308
  363.5 15.7 %collective-permute-done.18 = bf16[184,384]{1,0:T(8,128)(2,1)S(1)} collective-permute-done((bf16[184,384]{1,0:T(8,128)(2,1)S(1)}, bf16[184,384]{1,0:T(8,128)(2,1)S(1)}, u32[]{:S(2)}, u32[]{:S(2)}) %collective-permute-start.18) | collective-permute-done | bytes 141344 | tf_op jit(solution)/shard_map/ppermute | solution.py:308
  381.6 6.1 %collective-permute-done.19 = bf16[184,384]{1,0:T(8,128)(2,1)S(1)} collective-permute-done((bf16[184,384]{1,0:T(8,128)(2,1)S(1)}, bf16[184,384]{1,0:T(8,128)(2,1)S(1)}, u32[]{:S(2)}, u32[]{:S(2)}) %collective-permute-start.19) | collective-permute-done | bytes 141344 | tf_op jit(solution)/shard_map/ppermute | solution.py:308
  389.9 6.8 %collective-permute-done.20 = bf16[184,384]{1,0:T(8,128)(2,1)S(1)} collective-permute-done((bf16[184,384]{1,0:T(8,128)(2,1)S(1)}, bf16[184,384]{1,0:T(8,128)(2,1)S(1)}, u32[]{:S(2)}, u32[]{:S(2)}) %collective-permute-start.20) | collective-permute-done | bytes 141344 | tf_op jit(solution)/shard_map/ppermute | solution.py:308
  398.9 12.7 %collective-permute-start.15 = (bf16[1472,512]{1,0:T(8,128)(2,1)}, bf16[1472,512]{1,0:T(8,128)(2,1)}, u32[]{:S(2)}, u32[]{:S(2)}) collective-permute-start(bf16[1472,512]{1,0:T(8,128)(2,1)} %fusion.10), channel_id=1, source_target_pairs={{0,0},{1,2},{2,1},{3,3},{4,4},{5,6},{6,5},{7,7},{8,8},{9,10},{10,9... | collective-permute-start | bytes 4521992 | tf_op jit(solution)/shard_map/ppermute | solution.py:289
  417.9 37.8 %all-reduce = (f32[1472]{0:T(1024)}, f32[32,6]{0,1:T(8,128)}, f32[1472]{0:T(1024)}) all-reduce(f32[1472]{0:T(1024)S(1)} %get-tuple-element.94, f32[32,6]{0,1:T(8,128)S(1)} %dynamic_update_slice.3, f32[1472]{0:T(1024)S(1)} %get-tuple-element.92), channel_id=1, replica_groups=mesh['dp'=4,'seq'=4,'tensor'=2] {'dp','seq','tensor'}, use_global_device_ids=true, to_apply=%region_7.8 | all-reduce | flops 3136 | bytes 25088 | tf_op jit(solution)/shard_map/psum | solution.py:457
  (207 shorter events, 132.5 us)
Async XLA Ops:
  7.2 461.3 %all-gather.3.cloned.1.call-start = ((), (), s32[]{:S(2)}) async-start(), calls=%async_computation | async-start | bytes 1271808 | tf_op jit(solution)/shard_map/all_gather | solution.py:448
  12.0 38.0 %collective-permute-start.2 = (bf16[576,1472]{1,0:T(8,128)(2,1)}, bf16[576,1472]{1,0:T(8,128)(2,1)}, u32[]{:S(2)}, u32[]{:S(2)}) collective-permute-start(bf16[576,1472]{1,0:T(8,128)(2,1)} %pad_maximum_fusion.1), channel_id=1, source_target_pairs={{0,0},{1,2},{2,1},{3,3},{4,4},{5,6},{6,5},{7,7},{8,8},{9,10},{10,9... | collective-permute-start | bytes 5087240 | tf_op jit(solution)/shard_map/ppermute | solution.py:289
  33.7 78.2 %collective-permute-start.7 = (bf16[1472,512]{1,0:T(8,128)(2,1)}, bf16[1472,512]{1,0:T(8,128)(2,1)}, u32[]{:S(2)}, u32[]{:S(2)}) collective-permute-start(bf16[1472,512]{1,0:T(8,128)(2,1)} %fusion.23), channel_id=1, source_target_pairs={{0,0},{1,2},{2,1},{3,3},{4,4},{5,6},{6,5},{7,7},{8,8},{9,10},{10,9... | collective-permute-start | bytes 4521992 | tf_op jit(solution)/shard_map/ppermute | solution.py:289
  46.4 67.1 %collective-permute-start.10 = (bf16[1472,512]{1,0:T(8,128)(2,1)}, bf16[1472,512]{1,0:T(8,128)(2,1)}, u32[]{:S(2)}, u32[]{:S(2)}) collective-permute-start(bf16[1472,512]{1,0:T(8,128)(2,1)} %fusion.23), channel_id=1, source_target_pairs={{0,1},{1,3},{2,0},{3,2},{4,5},{5,7},{6,4},{7,6},{8,9},{9,11},{10,8... | collective-permute-start | bytes 4521992 | tf_op jit(solution)/shard_map/ppermute | solution.py:292
  74.7 40.4 %collective-permute-start.6 = (bf16[1472,512]{1,0:T(8,128)(2,1)}, bf16[1472,512]{1,0:T(8,128)(2,1)}, u32[]{:S(2)}, u32[]{:S(2)}) collective-permute-start(bf16[1472,512]{1,0:T(8,128)(2,1)} %fusion.13), channel_id=1, source_target_pairs={{0,2},{2,0},{4,6},{6,4},{1,3},{3,1},{5,7},{7,5},{8,10},{10,8},{12,... | collective-permute-start | bytes 4521992 | tf_op jit(solution)/shard_map/ppermute | solution.py:298
  118.8 35.5 %collective-permute-start.9 = (bf16[1472,512]{1,0:T(8,128)(2,1)S(1)}, bf16[1472,512]{1,0:T(8,128)(2,1)}, u32[]{:S(2)}, u32[]{:S(2)}) collective-permute-start(bf16[1472,512]{1,0:T(8,128)(2,1)S(1)} %multiply_convert_fusion.refs_0_), channel_id=1, source_target_pairs={{0,1},{1,0},{2,3},{3,2},{4,5},{5,4},{6,7},{7,6},{8,9},{9,8},{10,11... | collective-permute-start | bytes 4521992 | tf_op jit(solution)/shard_map/ppermute | solution.py:301
  180.4 35.5 %collective-permute-start.12 = (bf16[1472,512]{1,0:T(8,128)(2,1)}, bf16[1472,512]{1,0:T(8,128)(2,1)S(1)}, u32[]{:S(2)}, u32[]{:S(2)}) collective-permute-start(bf16[1472,512]{1,0:T(8,128)(2,1)} %get-tuple-element.35), channel_id=1, source_target_pairs={{0,1},{1,0},{2,3},{3,2},{4,5},{5,4},{6,7},{7,6},{8,9},{9,8},{10,11... | collective-permute-start | bytes 4521992 | tf_op jit(solution)/shard_map/ppermute | solution.py:301
  189.5 32.0 %collective-permute-start.35 = (bf16[1472,896]{1,0:T(8,128)(2,1)}, bf16[1472,896]{1,0:T(8,128)(2,1)}, u32[]{:S(2)}, u32[]{:S(2)}) collective-permute-start(bf16[1472,896]{1,0:T(8,128)(2,1)} %convolution_convert_fusion), channel_id=1, source_target_pairs={{0,2},{2,0},{4,6},{6,4},{1,3},{3,1},{5,7},{7,5},{8,10},{10,8},{12,... | collective-permute-start | bytes 7913480 | tf_op jit(solution)/shard_map/ppermute | solution.py:298
  194.6 46.1 %collective-permute-start.28 = (bf16[1472,896]{1,0:T(8,128)(2,1)S(1)}, bf16[1472,896]{1,0:T(8,128)(2,1)S(1)}, u32[]{:S(2)}, u32[]{:S(2)}) collective-permute-start(bf16[1472,896]{1,0:T(8,128)(2,1)S(1)} %convolution_convert_fusion.1), channel_id=1, source_target_pairs={{0,2},{2,0},{4,6},{6,4},{1,3},{3,1},{5,7},{7,5},{8,10},{10,8},{12,... | collective-permute-start | bytes 7913480 | tf_op jit(solution)/shard_map/ppermute | solution.py:298
  200.2 49.1 %collective-permute-start.21 = (bf16[1472,896]{1,0:T(8,128)(2,1)S(1)}, bf16[1472,896]{1,0:T(8,128)(2,1)S(1)}, u32[]{:S(2)}, u32[]{:S(2)}) collective-permute-start(bf16[1472,896]{1,0:T(8,128)(2,1)S(1)} %convolution_convert_fusion.2), channel_id=1, source_target_pairs={{0,2},{2,0},{4,6},{6,4},{1,3},{3,1},{5,7},{7,5},{8,10},{10,8},{12,... | collective-permute-start | bytes 7913480 | tf_op jit(solution)/shard_map/ppermute | solution.py:298
  200.3 213.8 %collective-permute-start.11 = (bf16[1472,512]{1,0:T(8,128)(2,1)}, bf16[1472,512]{1,0:T(8,128)(2,1)}, u32[]{:S(2)}, u32[]{:S(2)}) collective-permute-start(bf16[1472,512]{1,0:T(8,128)(2,1)} %get-tuple-element.33), channel_id=1, source_target_pairs={{1,0},{3,1},{0,2},{2,3},{5,4},{7,5},{4,6},{6,7},{9,8},{11,9},{8,10... | collective-permute-start | bytes 4521992 | tf_op jit(solution)/shard_map/ppermute | solution.py:295
  221.5 35.9 %collective-permute-start.13 = (bf16[1472,512]{1,0:T(8,128)(2,1)S(1)}, bf16[1472,512]{1,0:T(8,128)(2,1)S(1)}, u32[]{:S(2)}, u32[]{:S(2)}) collective-permute-start(bf16[1472,512]{1,0:T(8,128)(2,1)S(1)} %get-tuple-element.99), channel_id=1, source_target_pairs={{0,2},{2,0},{4,6},{6,4},{1,3},{3,1},{5,7},{7,5},{8,10},{10,8},{12,... | collective-permute-start | bytes 4521992 | tf_op jit(solution)/shard_map/ppermute | solution.py:298
  221.5 192.7 %collective-permute-start.8 = (bf16[1472,512]{1,0:T(8,128)(2,1)}, bf16[1472,512]{1,0:T(8,128)(2,1)}, u32[]{:S(2)}, u32[]{:S(2)}) collective-permute-start(bf16[1472,512]{1,0:T(8,128)(2,1)} %get-tuple-element.101), channel_id=1, source_target_pairs={{0,0},{1,2},{2,1},{3,3},{4,4},{5,6},{6,5},{7,7},{8,8},{9,10},{10,9... | collective-permute-start | bytes 4521992 | tf_op jit(solution)/shard_map/ppermute | solution.py:289
  240.7 49.6 %collective-permute-start.36 = (bf16[2,184,896]{2,1,0:T(8,128)(2,1)}, bf16[2,184,896]{2,1,0:T(8,128)(2,1)}, u32[]{:S(2)}, u32[]{:S(2)}) collective-permute-start(bf16[2,184,896]{2,1,0:T(8,128)(2,1)} %dynamic-slice_bitcast_fusion.2), channel_id=1, source_target_pairs={{0,8},{8,16},{16,24},{24,0},{1,9},{9,17},{17,25},{25,1},{2,10},{10... | collective-permute-start | bytes 1978376 | tf_op jit(solution)/shard_map/ppermute | solution.py:308
  249.3 42.4 %collective-permute-start.29 = (bf16[4,184,896]{2,1,0:T(8,128)(2,1)}, bf16[4,184,896]{2,1,0:T(8,128)(2,1)}, u32[]{:S(2)}, u32[]{:S(2)}) collective-permute-start(bf16[4,184,896]{2,1,0:T(8,128)(2,1)} %dynamic-slice_bitcast_fusion), channel_id=1, source_target_pairs={{0,4},{2,6},{4,0},{6,2},{1,5},{3,7},{5,1},{7,3},{8,12},{10,14},{12... | collective-permute-start | bytes 3956744 | tf_op jit(solution)/shard_map/ppermute | solution.py:308
  257.4 42.8 %collective-permute-start.22 = (bf16[4,184,896]{2,1,0:T(8,128)(2,1)}, bf16[4,184,896]{2,1,0:T(8,128)(2,1)}, u32[]{:S(2)}, u32[]{:S(2)}) collective-permute-start(bf16[4,184,896]{2,1,0:T(8,128)(2,1)} %dynamic-slice_bitcast_fusion.1), channel_id=1, source_target_pairs={{0,4},{2,6},{4,0},{6,2},{1,5},{3,7},{5,1},{7,3},{8,12},{10,14},{12... | collective-permute-start | bytes 3956744 | tf_op jit(solution)/shard_map/ppermute | solution.py:308
  290.4 27.1 %collective-permute-start.16 = (bf16[1472,384]{1,0:T(8,128)(2,1)S(1)}, bf16[1472,384]{1,0:T(8,128)(2,1)S(1)}, u32[]{:S(2)}, u32[]{:S(2)}) collective-permute-start(bf16[1472,384]{1,0:T(8,128)(2,1)S(1)} %fusion.30), channel_id=1, source_target_pairs={{0,1},{1,0},{2,3},{3,2},{4,5},{5,4},{6,7},{7,6},{8,9},{9,8},{10,11... | collective-permute-start | bytes 3391496 | tf_op jit(solution)/shard_map/ppermute | solution.py:301
  300.2 29.5 %collective-permute-start.14 = (bf16[1472,512]{1,0:T(8,128)(2,1)S(1)}, bf16[1472,512]{1,0:T(8,128)(2,1)S(1)}, u32[]{:S(2)}, u32[]{:S(2)}) collective-permute-start(bf16[1472,512]{1,0:T(8,128)(2,1)S(1)} %convolution_convert_fusion.4), channel_id=1, source_target_pairs={{0,2},{2,0},{4,6},{6,4},{1,3},{3,1},{5,7},{7,5},{8,10},{10,8},{12,... | collective-permute-start | bytes 4521992 | tf_op jit(solution)/shard_map/ppermute | solution.py:298
  349.1 31.5 %collective-permute-start.32 = (bf16[184,896]{1,0:T(8,128)(2,1)S(1)}, bf16[184,896]{1,0:T(8,128)(2,1)S(1)}, u32[]{:S(2)}, u32[]{:S(2)}) collective-permute-start(bf16[184,896]{1,0:T(8,128)(2,1)S(1)} %fusion.35), channel_id=1, source_target_pairs={{0,8},{8,16},{16,24},{24,0},{1,9},{9,17},{17,25},{25,1},{2,10},{10... | collective-permute-start | bytes 989192 | tf_op jit(solution)/shard_map/ppermute | solution.py:308
  349.3 31.6 %collective-permute-start.25 = (bf16[184,896]{1,0:T(8,128)(2,1)S(1)}, bf16[184,896]{1,0:T(8,128)(2,1)S(1)}, u32[]{:S(2)}, u32[]{:S(2)}) collective-permute-start(bf16[184,896]{1,0:T(8,128)(2,1)S(1)} %fusion.38), channel_id=1, source_target_pairs={{0,8},{8,16},{16,24},{24,0},{1,9},{9,17},{17,25},{25,1},{2,10},{10... | collective-permute-start | bytes 989192 | tf_op jit(solution)/shard_map/ppermute | solution.py:308
  398.9 66.2 %collective-permute-start.15 = (bf16[1472,512]{1,0:T(8,128)(2,1)}, bf16[1472,512]{1,0:T(8,128)(2,1)}, u32[]{:S(2)}, u32[]{:S(2)}) collective-permute-start(bf16[1472,512]{1,0:T(8,128)(2,1)} %fusion.10), channel_id=1, source_target_pairs={{0,0},{1,2},{2,1},{3,3},{4,4},{5,6},{6,5},{7,7},{8,8},{9,10},{10,9... | collective-permute-start | bytes 4521992 | tf_op jit(solution)/shard_map/ppermute | solution.py:289
  411.8 43.8 %collective-permute-start.34 = (bf16[368,896]{1,0:T(8,128)(2,1)S(1)}, bf16[368,896]{1,0:T(8,128)(2,1)}, u32[]{:S(2)}, u32[]{:S(2)}) collective-permute-start(bf16[368,896]{1,0:T(8,128)(2,1)S(1)} %maximum_select_fusion.6), channel_id=1, source_target_pairs={{0,2},{2,0},{4,6},{6,4},{1,3},{3,1},{5,7},{7,5},{8,10},{10,8},{12,... | collective-permute-start | bytes 1978376 | tf_op jit(solution)/shard_map/ppermute | solution.py:298
  412.1 46.7 %collective-permute-start.27 = (bf16[368,896]{1,0:T(8,128)(2,1)S(1)}, bf16[368,896]{1,0:T(8,128)(2,1)}, u32[]{:S(2)}, u32[]{:S(2)}) collective-permute-start(bf16[368,896]{1,0:T(8,128)(2,1)S(1)} %maximum_select_fusion.5), channel_id=1, source_target_pairs={{0,2},{2,0},{4,6},{6,4},{1,3},{3,1},{5,7},{7,5},{8,10},{10,8},{12,... | collective-permute-start | bytes 1978376 | tf_op jit(solution)/shard_map/ppermute | solution.py:298
  414.2 47.8 %collective-permute-start.41 = (bf16[368,896]{1,0:T(8,128)(2,1)S(1)}, bf16[368,896]{1,0:T(8,128)(2,1)}, u32[]{:S(2)}, u32[]{:S(2)}) collective-permute-start(bf16[368,896]{1,0:T(8,128)(2,1)S(1)} %maximum_select_fusion.7), channel_id=1, source_target_pairs={{0,2},{2,0},{4,6},{6,4},{1,3},{3,1},{5,7},{7,5},{8,10},{10,8},{12,... | collective-permute-start | bytes 1978376 | tf_op jit(solution)/shard_map/ppermute | solution.py:298
  (45 other events, 640.8 us)
Sparse Core Ops, SparseCore 0:
  399.0 22.6 all-gather.2

commit v2 on v1

--- a/solution.py
+++ b/solution.py
@@ -15,10 +15,15 @@
 band_half = 128
 low = jnp.bfloat16
 wide = jnp.float32
+hint = pl.CostEstimate(flops=1000, bytes_accessed=1000, transcendentals=0)
 
 
 def dot(a, b, ca, cb):
     return lax.dot_general(a, b, (((ca,), (cb,)), ((), ())), preferred_element_type=wide)
+
+
+def after(value, *first):
+    return lax.optimization_barrier((value, *first))[0]
 
 
 def attn_fwd_kernel(length, bias_ref, q_ref, k_ref, v_ref, seg_k_ref, seg_q_ref, p_ref, o_ref, table):
@@ -84,11 +89,7 @@
         ],
         scratch_shapes=[pltpu.VMEM((heads, 2 * length - q_block, q_block), wide)],
         compiler_params=pltpu.CompilerParams(vmem_limit_bytes=48 << 20),
-        cost_estimate=pl.CostEstimate(
-            flops=4 * heads * length * length * dim * 4,
-            bytes_accessed=2 * heads * length * length + 8 * width * length,
-            transcendentals=heads * length * length,
-        ),
+        cost_estimate=hint,
         name="attn_forward",
     )(bias, qkv, qkv, qkv, seg_k, seg_q)
 
@@ -172,27 +173,63 @@
             pltpu.VMEM((2 * length - q_block, q_block), wide),
         ],
         compiler_params=pltpu.CompilerParams(vmem_limit_bytes=48 << 20),
-        cost_estimate=pl.CostEstimate(
-            flops=8 * heads * length * length * dim * 4,
-            bytes_accessed=2 * heads * length * length + 16 * width * length,
-            transcendentals=0,
-        ),
+        cost_estimate=hint,
         name="attn_backward",
     )(qkv, qkv, qkv, grad_mixed, mixed, probs)
     return jnp.concatenate([gq, gk, gv], axis=0), jnp.sum(gb, axis=2).T
 
 
-def ffn_kernel(*refs):
-    (x_ref, g_ref, gate_w, up_w, down_w), refs = refs[:5], refs[-9:]
-    hid_ref, gg_ref, gu_ref, out_ref, gx_ref, xs, gs, out_acc, gx_acc = refs
-    step = pl.program_id(0)
-
-    @pl.when(step == 0)
+def ffn_kernel(
+    x_ref, go_ref, gr_ref, gate_w, up_w, down_w,
+    hid_ref, gg_ref, gu_ref, xr_ref, out_ref, out_r_ref, gx_ref,
+    xs, gs, out_acc, gx_acc, x_in, gx_out, gx_in, sems,
+):
+    chunk = pl.program_id(0)
+    tile = pl.program_id(1)
+    size = xs.shape[0]
+    there = {"tensor": 1 - lax.axis_index("tensor")}
+    half = [pl.ds(0, size), pl.ds(size, size)]
+
+    def send_x(h):
+        return pltpu.make_async_remote_copy(
+            src_ref=x_ref.at[:, half[h]], dst_ref=x_in.at[h], send_sem=sems.at[h], recv_sem=sems.at[2 + h],
+            device_id=there, device_id_type=pl.DeviceIdType.MESH,
+        )
+
+    def send_gx(h):
+        return pltpu.make_async_remote_copy(
+            src_ref=gx_out.at[h], dst_ref=gx_in.at[h], send_sem=sems.at[4 + h], recv_sem=sems.at[6 + h],
+            device_id=there, device_id_type=pl.DeviceIdType.MESH,
+        )
+
+    @pl.when(tile == 0)
     def _():
-        xs[...] = x_ref[...].T
-        gs[...] = g_ref[...].T
         out_acc[...] = jnp.zeros_like(out_acc)
         gx_acc[...] = jnp.zeros_like(gx_acc)
+
+    @pl.when((tile == 0) & (chunk == 0))
+    def _():
+        barrier = pltpu.get_barrier_semaphore()
+        pl.semaphore_signal(barrier, inc=1, device_id=there, device_id_type=pl.DeviceIdType.MESH)
+        pl.semaphore_wait(barrier, 1)
+        send_x(0).start()
+        send_x(1).start()
+        xs[...] = x_ref[:, half[1]].T
+        gs[...] = go_ref[:, half[1]].T
+
+    for h in range(2):
+
+        @pl.when((tile == 0) & (chunk == 1 + h))
+        def _(h=h):
+            send_x(h).wait_recv()
+            xs[...] = x_in[h].T
+            gs[...] = gr_ref[:, half[h]].T
+            xr_ref[:, half[h]] = x_in[h]
+
+    @pl.when((tile == 0) & (chunk == 3))
+    def _():
+        xs[...] = x_ref[:, half[0]].T
+        gs[...] = go_ref[:, half[0]].T
 
     gate = dot(xs[...], gate_w[...], 1, 0)
     up = dot(xs[...], up_w[...], 1, 0)
@@ -200,9 +237,9 @@
     c = math.sqrt(2.0 / math.pi)
     square = gate * gate
     t = jnp.tanh(c * gate * (1.0 + 0.044715 * square))
-    half = 0.5 * (1.0 + t)
-    gelu = gate * half
-    slope = half + 0.5 * gate * (1.0 - t * t) * (c * (1.0 + 3 * 0.044715 * square))
+    part = 0.5 * (1.0 + t)
+    gelu = gate * part
+    slope = part + 0.5 * gate * (1.0 - t * t) * (c * (1.0 + 3 * 0.044715 * square))
     hid = (gelu * up).astype(low)
     gg = (grad * up * slope).astype(low)
     gu = (grad * gelu).astype(low)
@@ -212,50 +249,98 @@
     out_acc[...] += dot(down_w[...], hid, 1, 1)
     gx_acc[...] += dot(gate_w[...], gg, 1, 1) + dot(up_w[...], gu, 1, 1)
 
-    @pl.when(step == pl.num_programs(0) - 1)
+    last = tile == pl.num_programs(1) - 1
+    for at, h in ((0, 1), (3, 0)):
+
+        @pl.when(last & (chunk == at))
+        def _(h=h):
+            out_ref[:, half[h]] = out_acc[...]
+            gx_ref[:, half[h]] = gx_acc[...]
+
+    for h in range(2):
+
+        @pl.when(last & (chunk == 1 + h))
+        def _(h=h):
+            out_r_ref[:, half[h]] = out_acc[...].astype(low)
+            gx_out[h] = gx_acc[...].astype(low)
+            send_gx(h).start()
+
+    @pl.when(last & (chunk == 3))
     def _():
-        out_ref[...] = out_acc[...].astype(out_ref.dtype)
-        gx_ref[...] = gx_acc[...].astype(gx_ref.dtype)
-
-
-def ffn(x, g, gate_w, up_w, down_w, kept, slot, slots, kind):
+        for h in range(2):
+            send_gx(h).wait_recv()
+            gx_ref[:, half[h]] += gx_in[h].astype(wide)
+        for h in range(2):
+            send_x(h).wait_send()
+            send_gx(h).wait_send()
+
+
+def ffn(x, g_own, g_oth, gate_w, up_w, down_w):
     width, tokens = x.shape
     hidden = gate_w.shape[1]
-    tile = 256
-    full = pl.BlockSpec((width, tokens), lambda j: (0, 0), pipeline_mode=pl.Buffered(1))
-    weight = pl.BlockSpec((width, tile), lambda j: (0, j))
-    act = pl.BlockSpec((tokens, tile), lambda j: (slot, j))
-    act_shape = jax.ShapeDtypeStruct((slots * tokens, hidden), low)
-    args = [x, g, gate_w, up_w, down_w]
-    specs = [full, full, weight, weight, weight]
-    alias = {}
-    if kept is not None:
-        args += list(kept)
-        specs += [pl.BlockSpec(memory_space=pl.ANY)] * 3
-        alias = {5: 0, 6: 1, 7: 2}
-    hid, gg, gu, out, gx = pl.pallas_call(
+    tile, size = 256, tokens // 2
+    full = pl.BlockSpec((width, tokens), lambda s, j: (0, 0), pipeline_mode=pl.Buffered(1))
+    weight = pl.BlockSpec((width, tile), lambda s, j: (0, j))
+    act = pl.BlockSpec((size, tile), lambda s, j: ((s + 1) % 4, j))
+    act_shape = jax.ShapeDtypeStruct((2 * tokens, hidden), low)
+    tokens_of = lambda kind: jax.ShapeDtypeStruct((width, tokens), kind)
+    part = pltpu.VMEM((2, width, size), low)
+    return pl.pallas_call(
         ffn_kernel,
-        grid=(hidden // tile,),
-        in_specs=specs,
-        out_specs=[act, act, act, full, full],
-        out_shape=[act_shape, act_shape, act_shape]
-        + [jax.ShapeDtypeStruct((width, tokens), kind)] * 2,
+        grid=(4, hidden // tile),
+        in_specs=[full, full, full, weight, weight, weight],
+        out_specs=[act, act, act, full, full, full, full],
+        out_shape=[act_shape, act_shape, act_shape, tokens_of(low), tokens_of(wide), tokens_of(low), tokens_of(wide)],
         scratch_shapes=[
-            pltpu.VMEM((tokens, width), low),
-            pltpu.VMEM((tokens, width), low),
-            pltpu.VMEM((width, tokens), wide),
-            pltpu.VMEM((width, tokens), wide),
+            pltpu.VMEM((size, width), low),
+            pltpu.VMEM((size, width), low),
+            pltpu.VMEM((width, size), wide),
+            pltpu.VMEM((width, size), wide),
+            part,
+            part,
+            part,
+            pltpu.SemaphoreType.DMA((8,)),
         ],
-        input_output_aliases=alias,
-        compiler_params=pltpu.CompilerParams(vmem_limit_bytes=56 << 20),
-        cost_estimate=pl.CostEstimate(
-            flops=12 * tokens * width * hidden,
-            bytes_accessed=6 * width * hidden + 8 * width * tokens + 6 * tokens * hidden,
-            transcendentals=tokens * hidden,
+        compiler_params=pltpu.CompilerParams(vmem_limit_bytes=56 << 20, collective_id=0, has_side_effects=True),
+        cost_estimate=hint,
+        name="ffn_both_ways",
+    )(x, g_own, g_oth, gate_w, up_w, down_w)
+
+
+def weight_grad_kernel(core_ref, own_ref, oth_ref, right_ref, *refs):
+    tokens = own_ref.shape[1]
+    total = dot(own_ref[...], right_ref[:tokens, :], 1, 0) + dot(oth_ref[...], right_ref[tokens:, :], 1, 0)
+    if len(refs) == 2:
+        total = total + refs[0][...].astype(wide)
+    refs[-1][...] = total.astype(low)
+
+
+def weight_grad(own, oth, right, core, got=None):
+    width, tokens = own.shape
+    columns = right.shape[1] // 2
+    blocks = 4
+    rows = width // blocks
+    left = pl.BlockSpec((rows, tokens), lambda i, core_ref: (i, 0))
+    out = pl.BlockSpec((rows, columns), lambda i, core_ref: (i, 0))
+    args = [own, oth, right] + ([] if got is None else [got])
+    return pl.pallas_call(
+        weight_grad_kernel,
+        grid_spec=pltpu.PrefetchScalarGridSpec(
+            num_scalar_prefetch=1,
+            grid=(blocks,),
+            in_specs=[
+                left,
+                left,
+                pl.BlockSpec((2 * tokens, columns), lambda i, core_ref: (0, core_ref[0]), pipeline_mode=pl.Buffered(1)),
+            ]
+            + ([] if got is None else [out]),
+            out_specs=out,
         ),
-        name="ffn_both_ways",
-    )(*args)
-    return (hid, gg, gu), out, gx
+        out_shape=jax.ShapeDtypeStruct((width, columns), low),
+        compiler_params=pltpu.CompilerParams(vmem_limit_bytes=40 << 20),
+        cost_estimate=hint,
+        name="weight_grad",
+    )(core.reshape(1), *args)
 
 
 def norm_of(values, gain):
@@ -273,20 +358,22 @@
 class Moves:
     def __init__(self, mesh):
         self.nz = mesh.shape["dp"]
-        self.nseq = mesh.shape["seq"]
-        self.ny = mesh.shape["tensor"]
-        self.nx = self.nseq // 2
+        self.nx = mesh.shape["seq"] // 2
         both = [(m, c, y) for m in range(self.nx) for c in range(2) for y in range(2)]
         at = lambda m, c, y: (m * 2 + c) * 2 + y
-        self.swap_pairs = [(at(m, c, y), at(m, y, c)) for m, c, y in both]
+        self.swap_pairs = [(at(m, c, y), at(m, y, c)) for m, c, y in both if c != y]
         self.second_pairs = [(at(m, c, y), at(m, y, 1 - c)) for m, c, y in both]
         self.back_pairs = [(b, a) for a, b in self.second_pairs]
-        self.core_pairs = [(m * 2 + c, m * 2 + 1 - c) for m in range(self.nx) for c in range(2)]
         self.ring_x = [(m * 2 + c, (m + 1) % self.nx * 2 + c) for m in range(self.nx) for c in range(2)]
-        self.ring_z = [(z, (z + 1) % self.nz) for z in range(self.nz)]
+        self.y = lax.axis_index("tensor")
+        self.z = lax.axis_index("dp")
+        s = lax.axis_index("seq")
+        self.c = s % 2
+        self.m = s // 2
 
     def swap(self, a):
-        return lax.ppermute(a, ("seq", "tensor"), self.swap_pairs)
+        got = lax.ppermute(a, ("seq", "tensor"), self.swap_pairs)
+        return jnp.where(self.c == self.y, a, got)
 
     def second(self, a):
         return lax.ppermute(a, ("seq", "tensor"), self.second_pairs)
@@ -295,39 +382,63 @@
         return lax.ppermute(a, ("seq", "tensor"), self.back_pairs)
 
     def core(self, a):
-        return lax.ppermute(a, "seq", self.core_pairs)
+        return lax.ppermute(a, "seq", [(s, s ^ 1) for s in range(2 * self.nx)])
 
     def over_y(self, a):
         return lax.ppermute(a, "tensor", [(0, 1), (1, 0)])
 
-    def ring(self, take, me, n, axis, pairs):
-        if n == 1:
-            return take(me)
-        held = take((me + n - 1) % n)
-        for t in range(1, n):
-            got = lax.ppermute(held.astype(low), axis, pairs)
-            held = got.astype(wide) + take((me + 2 * n - 1 - t) % n).astype(wide)
-        return held.astype(low)
-
-    def over_x_then_z(self, a, m, z):
-        a = self.ring(lambda i: lax.dynamic_index_in_dim(a, i, 1, False), m, self.nx, "seq", self.ring_x)
-        return self.ring(lambda i: lax.dynamic_index_in_dim(a, i, 0, False), z, self.nz, "dp", self.ring_z)
-
-    def over_z_then_x(self, a, m, z):
-        a = self.ring(lambda i: lax.dynamic_index_in_dim(a, i, 0, False), z, self.nz, "dp", self.ring_z)
-        return self.ring(lambda i: lax.dynamic_index_in_dim(a, i, 0, False), m, self.nx, "seq", self.ring_x)
-
-    def gather_x_core(self, piece, m, c):
-        rows, columns = piece.shape
+    def over_x(self, a):
+        return lax.ppermute(a, "seq", self.ring_x)
+
+    def start_x(self, a):
+        take = lax.dynamic_index_in_dim(a, (self.m + self.nx - 1) % self.nx, 1, False)
+        return a, self.over_x(take)
+
+    def finish_x(self, a, got, *first):
+        take = lambda i: lax.dynamic_index_in_dim(a, i % self.nx, 1, False)
+        got = after(got, *first)
+        held = (got.astype(wide) + take(self.m + 2 * self.nx - 2).astype(wide)).astype(low)
+        for t in range(2, self.nx):
+            held = (self.over_x(held).astype(wide) + take(self.m + 2 * self.nx - 1 - t).astype(wide)).astype(low)
+        return held
+
+    def scatter_x(self, a):
+        take = lambda i: lax.dynamic_index_in_dim(a, i % self.nx, 1, False)
+        held = take(self.m + self.nx - 1)
+        for t in range(1, self.nx):
+            held = (self.over_x(held).astype(wide) + take(self.m + 2 * self.nx - 1 - t).astype(wide)).astype(low)
+        return held
+
+    def scatter_z(self, a):
+        return lax.psum_scatter(a, "dp", scatter_dimension=0, tiled=True)
+
+    def gather_x(self, piece):
         if self.nx == 2:
-            over = lax.ppermute(piece, "seq", self.ring_x)
-            here = jnp.where(m == 0, jnp.concatenate([piece, over], 0), jnp.concatenate([over, piece], 0))
-            there = self.core(here)
+            over = self.over_x(piece)
             return jnp.where(
-                c == 0, jnp.concatenate([here, there], 1), jnp.concatenate([there, here], 1)
+                self.m == 0, jnp.concatenate([piece, over], 0), jnp.concatenate([over, piece], 0)
             )
-        got = lax.all_gather(piece, "seq").reshape(self.nx, 2, rows, columns)
-        return got.transpose(0, 2, 1, 3).reshape(self.nx * rows, 2 * columns)
+        groups = [[m * 2 + c for m in range(self.nx)] for c in range(2)]
+        return lax.all_gather(piece, "seq", axis=0, tiled=True, axis_index_groups=groups)
+
+    def gather_core(self, piece):
+        there = self.core(piece)
+        return jnp.where(
+            self.c == 0, jnp.concatenate([piece, there], 1), jnp.concatenate([there, piece], 1)
+        )
+
+    def sum_everywhere(self, a):
+        a = a + self.core(a)
+        a = a + self.over_y(a)
+        step = 1
+        while step < self.nx:
+            a = a + lax.ppermute(a, "seq", [(s, s ^ (2 * step)) for s in range(2 * self.nx)])
+            step *= 2
+        step = 1
+        while step < self.nz:
+            a = a + lax.ppermute(a, "dp", [(z, z ^ step) for z in range(self.nz)])
+            step *= 2
+        return a
 
 
 def segment_ids(lengths, valid, length):
@@ -359,21 +470,19 @@
     length = 2 * half_len
     heads = position_bias.shape[1]
     inner_width = query_weight.shape[1]
-    s = lax.axis_index("seq")
-    y = lax.axis_index("tensor")
-    z = lax.axis_index("dp")
-    c = s % 2
-    m = s // 2
-
+    y, c, m = moves.y, moves.c, moves.m
+
+    facts = jnp.concatenate([doc_lengths[0].astype(wide), valid_length.astype(wide), position_bias.reshape(-1)])
+    facts = moves.swap(facts)
+    bias = facts[5:].reshape(position_bias.shape)
+    facts = facts[:5].astype(jnp.int32)
     x_in = moves.swap(layer_in.reshape(half_len, width).T)
     qkv_w = jnp.concatenate([query_weight.T, key_weight.T, value_weight.T], axis=0)
     qkv_w = moves.swap(qkv_w)
-    facts = moves.swap(jnp.concatenate([doc_lengths[0], valid_length]))
-    bias = moves.swap(position_bias)
-    out_w = moves.swap(output_weight)
     positions = y * half_len + jnp.arange(half_len, dtype=jnp.int32)
     g_in = jnp.where((positions < valid_length[0])[None, :], out_grad.reshape(half_len, width).T, 0)
-    g_in = g_in.astype(low)
+    g_in, out_w, x_in, facts = lax.optimization_barrier((g_in.astype(low), output_weight, x_in, facts))
+    out_w = moves.swap(out_w)
     g_own = moves.swap(g_in)
     g_oth = moves.second(g_in)
     segment = segment_ids(facts[:4], facts[4], length)
@@ -402,29 +511,25 @@
 
     normed, scale_two = norm_of(hres, gain_two)
     xn_own = normed.astype(low)
-    xn_oth = moves.over_y(xn_own)
-    down_t = down_weight.T
-    kept, out_own, gx_own = ffn(xn_own, g_own, gate_weight, up_weight, down_t, None, 0, 2, wide)
-    kept, out_oth, gx_oth = ffn(xn_oth, g_oth, gate_weight, up_weight, down_t, kept, 1, 2, low)
-    hid, grad_gate, grad_up = kept
-    gx = gx_own + moves.over_y(gx_oth).astype(wide)
+    hid, grad_gate, grad_up, xn_oth, out_own, out_oth, gx = ffn(
+        xn_own, g_own, g_oth, gate_weight, up_weight, down_weight.T
+    )
+
+    columns = hid.shape[1] // 2
+    send_d = weight_grad(g_own, g_oth, hid, 1 - c)
+    got_d = moves.core(send_d)
+    send_g = weight_grad(xn_own, xn_oth, after(grad_gate, send_d), 1 - c)
+    got_g = moves.core(send_g)
+    send_u = weight_grad(xn_own, xn_oth, after(grad_up, send_g), 1 - c)
+    got_u = moves.core(send_u)
+    total_d = weight_grad(g_own, g_oth, after(hid, send_u), c, got_d)
+    total_g = weight_grad(xn_own, xn_oth, after(grad_gate, total_d), c, got_g)
+    total_u = weight_grad(xn_own, xn_oth, after(grad_up, total_g), c, got_u)
+    part_d = moves.scatter_z(total_d)
+    x_sent = [moves.start_x(t.reshape(moves.nz, moves.nx, -1, columns)) for t in (total_g, total_u)]
+
+    gx = after(gx, total_u)
     out_y = moves.swap((hres + out_own).astype(low)).astype(wide) + moves.back(out_oth).astype(wide)
-    out_y = out_y.astype(low)
-
-    def ffn_weight_grad(left_own, left_oth, right, x_first):
-        left = jnp.concatenate([left_own, left_oth], axis=1)
-        columns = right.shape[1] // 2
-        send = dot(left, lax.dynamic_slice_in_dim(right, (1 - c) * columns, columns, 1), 1, 0)
-        got = moves.core(send.astype(low))
-        keep = dot(left, lax.dynamic_slice_in_dim(right, c * columns, columns, 1), 1, 0)
-        total = (keep + got.astype(wide)).astype(low)
-        total = total.reshape(moves.nz, moves.nx, -1, columns)
-        piece = (moves.over_x_then_z if x_first else moves.over_z_then_x)(total, m, z)
-        return moves.gather_x_core(piece, m, c).astype(wide)
-
-    sum_d = ffn_weight_grad(g_own, g_oth, hid, False)
-    sum_g = ffn_weight_grad(xn_own, xn_oth, grad_gate, True)
-    sum_u = ffn_weight_grad(xn_own, xn_oth, grad_up, True)
 
     back, grad_gain_two = norm_back(hres, scale_two, gain_two, gx)
     grad_hres = g_own.astype(wide) + back
@@ -432,33 +537,55 @@
 
     grad_mixed = dot(out_w, branch, 1, 0).astype(low)
     grad_qkv, grad_bias = attn_backward(qkv, grad_mixed, mixed, probs)
+
+    part_g = moves.finish_x(*x_sent[0], grad_qkv).reshape(-1, columns)
+    sent = dot(qkv_w, other_half(after(grad_qkv, part_g)), 0, 0).astype(low)
+    part_g = moves.scatter_z(part_g)
+    got_x = moves.core(sent)
     grad_attn_w = jnp.concatenate(
-        [dot(xn_one, grad_qkv, 1, 1).astype(low), dot(branch, mixed, 1, 1).astype(low)], axis=1
+        [dot(xn_one, after(grad_qkv, sent), 1, 1).astype(low), dot(branch, mixed, 1, 1).astype(low)], axis=1
     )
-    sent = dot(qkv_w, other_half(grad_qkv), 0, 0).astype(low)
-    gx = dot(qkv_w, my_half(grad_qkv), 0, 0) + moves.core(sent).astype(wide)
+    gx = dot(qkv_w, my_half(after(grad_qkv, grad_attn_w)), 0, 0) + got_x.astype(wide)
     back, grad_gain_one = norm_back(x_wide, scale_one, gain_one, gx)
-    grad_in = moves.swap((grad_hres + back).astype(low)).astype(wide)
-
-    columns = grad_attn_w.shape[1] // 2
-    got = moves.over_y(lax.dynamic_slice_in_dim(grad_attn_w, (1 - y) * columns, columns, 1))
-    total = lax.dynamic_slice_in_dim(grad_attn_w, y * columns, columns, 1).astype(wide) + got.astype(wide)
-    total = total.astype(low).reshape(moves.nz, moves.nx, -1, columns)
-    piece = moves.over_x_then_z(total, m, z)
-    pieces = lax.all_gather(piece, ("seq", "tensor")).reshape(moves.nx, 2, 2, -1, columns)
-    pieces = lax.dynamic_index_in_dim(pieces, y, 1, False)
-    sums = pieces.transpose(0, 2, 1, 3).reshape(-1, 2 * columns).astype(wide)
+    grad_in = (grad_hres + back).astype(low)
+    part_u = moves.scatter_z(moves.finish_x(*x_sent[1], grad_in).reshape(-1, columns))
+
+    a_columns = grad_attn_w.shape[1] // 2
+    chunks = grad_attn_w.reshape(moves.nz, moves.nx, -1, 2 * a_columns)
+
+    def scatter_y(a):
+        got = moves.over_y(lax.dynamic_slice_in_dim(a, (1 - y) * a_columns, a_columns, a.ndim - 1))
+        kept = lax.dynamic_slice_in_dim(a, y * a_columns, a_columns, a.ndim - 1)
+        return (kept.astype(wide) + got.astype(wide)).astype(low)
+
+    half_z = moves.nz // 2
+    part = jnp.concatenate(
+        [moves.scatter_x(scatter_y(chunks[:half_z])), scatter_y(moves.scatter_x(chunks[half_z:]))], 0
+    )
+    piece = moves.gather_x(moves.scatter_z(part.reshape(-1, a_columns)))
+    there = moves.over_y(piece)
+    group = jnp.where(y == 0, jnp.concatenate([piece, there], 1), jnp.concatenate([there, piece], 1))
+    sums = jnp.where(c == y, group, moves.core(group)).astype(wide)
     sum_q, sum_k, sum_v, sum_o = (
         sums[:, i * inner_width : (i + 1) * inner_width] for i in range(4)
     )
+    grad_in = moves.swap(grad_in).astype(wide)
+
+    if moves.nx == 2:
+        part_d = (part_d.astype(wide) + moves.over_x(part_d).astype(wide)).astype(low)
+    else:
+        part_d = moves.gather_x(moves.scatter_x(part_d.reshape(1, moves.nx, -1, columns))[0])
+    sum_d = moves.gather_core(part_d).astype(wide)
+    sum_g = moves.gather_core(moves.gather_x(part_g)).astype(wide)
+    sum_u = moves.gather_core(moves.gather_x(part_u)).astype(wide)
 
     bias_full = jnp.zeros((grad_bias.shape[0], 2 * heads), wide)
     bias_full = lax.dynamic_update_slice(bias_full, grad_bias, (jnp.int32(0), c * heads))
-    gain_one_sum, gain_two_sum, bias_sum = lax.psum(
-        (grad_gain_one, grad_gain_two, bias_full), ("dp", "seq", "tensor")
-    )
+    early = moves.sum_everywhere(jnp.concatenate([grad_gain_two, bias_full.reshape(-1)]))
+    gain_two_sum, bias_sum = early[:width], early[width:].reshape(bias_full.shape)
+    gain_one_sum = moves.sum_everywhere(grad_gain_one)
     return (
-        out_y.T.reshape(half_len, 1, width),
+        out_y.astype(low).T.reshape(half_len, 1, width),
         grad_in.T.reshape(half_len, 1, width),
         gain_one_sum,
         sum_q,

time: 489 us -> 471 us (0.963)
  Pallas kernels: 88.4 us -> 140 us
  starting transfers between devices: 117 us -> 74.4 us
  blocking collectives: 37.8 us -> 0 us
  matrix products: 58.3 us -> 26.1 us
  waiting for transfers between devices: 108 us -> 128 us
  local copies, waits for them, and re-layouts: 14 us -> 33.9 us
  other arithmetic: 42.2 us -> 48.3 us
    pallas_call x2 -> x7, Pallas kernels: 53.1 us -> 105 us  [the longest x1 74.5 us: ffn(): pl.pallas_call(ffn_kernel, grid=(4, hidden // tile), in_specs=[full, full...]
    ppermute x37 -> x34, starting transfers between devices: 113 us -> 65.2 us  [the longest x13 33.7 us: core(): return lax.ppermute(a, 'seq', [(s, s ^ 1) for s in range(2 * self.nx)])]
    psum x1 -> x0, blocking collectives: 37.8 us -> none  [local(): lax.psum((grad_gain_one, grad_gain_two, bias_full), ('dp', 'seq', 'tensor'))]
    unnamed x1 -> x7, waiting for transfers between devices: 0.02 us -> 34.7 us
    ppermute x37 -> x34, waiting for transfers between devices: 79.1 us -> 44.8 us  [the longest x8 38.8 us: over_x(): return lax.ppermute(a, 'seq', self.ring_x)]
    dot_general x14 -> x8, matrix products: 58.3 us -> 26.1 us  [dot(): lax.dot_general(a, b, (((ca,), (cb,)), ((), ())), preferred_element_type=...]
    reduce_scatter x0 -> x1, waiting for transfers between devices: none -> 13.8 us  [scatter_z(): return lax.psum_scatter(a, 'dp', scatter_dimension=0, tiled=True)]
    unnamed x61 -> x104, local copies, waits for them, and re-layouts: 6.97 us -> 19.3 us
  transfers between devices with their start and end apart: 43 -> 45, of which waited for: 14 -> 20; matrix products, arithmetic and copies ran while one was open for 22% -> 15% of each run, Pallas kernels for 13% -> 12%
where the time goes in v2:
time: 471 us; the launch traced here: 466 us
  Pallas kernels  140 us (30%)
  waiting for transfers between devices  128 us (27%)
  starting transfers between devices  74.4 us (16%)
  other arithmetic  48.3 us (10%)
  local copies, waits for them, and re-layouts  33.9 us (7%)
  matrix products  26.1 us (6%)
  between operations  15.6 us (3%)
    pallas_call x1, Pallas kernels, ffn(): pl.pallas_call(ffn_kernel, grid=(4, hidden // tile), in_specs=[full, full...  74.5 us
    ppermute x8, waiting for transfers between devices, over_x(): return lax.ppermute(a, 'seq', self.ring_x)  38.8 us
    unnamed x7, waiting for transfers between devices  34.7 us
    ppermute x13, starting transfers between devices, core(): return lax.ppermute(a, 'seq', [(s, s ^ 1) for s in range(2 * self.nx)])  33.7 us
    pallas_call x6, Pallas kernels, weight_grad(): pl.pallas_call(weight_grad_kernel, grid_spec=pltpu.PrefetchScalarGridSpec...  30.3 us
    dot_general x8, matrix products, dot(): lax.dot_general(a, b, (((ca,), (cb,)), ((), ())), preferred_element_type=...  26.1 us
    ppermute x5, waiting for transfers between devices, over_y(): return lax.ppermute(a, 'tensor', [(0, 1), (1, 0)])  23.3 us
    pallas_call x1, Pallas kernels, attn_backward(): pl.pallas_call(functools.partial(attn_bwd_kernel, length), grid=(heads, b...  20.5 us
  transfers between devices with their start and end apart: 45, of which 20 were waited for; matrix products, arithmetic and copies ran while one was open for 15% of the time, Pallas kernels for 12%

profile of v2, /device:TPU:0, one launch (start us, length us, event | category | flops | bytes accessed | tf_op | source)
XLA Modules:
  0.0 465.7 jit_solution(426043892763500250)
XLA Ops:
  19.8 13.5 %collective-permute-start.4 = (bf16[1472,512]{1,0:T(8,128)(2,1)S(1)}, bf16[1472,512]{1,0:T(8,128)(2,1)S(1)}, u32[]{:S(2)}, u32[]{:S(2)}) collective-permute-start(bf16[1472,512]{1,0:T(8,128)(2,1)S(1)} %fusion.5), channel_id=1, source_target_pairs={{0,2},{2,0},{4,6},{6,4},{1,3},{3,1},{5,7},{7,5},{8,10},{10,8},{12,... | collective-permute-start | bytes 4521992 | tf_op jit(solution)/shard_map/ppermute | solution.py:385
  43.5 14.5 %attn_forward.1 = (bf16[3,1024,1024]{2,1,0:T(8,128)(2,1)}, bf16[192,1024]{1,0:T(8,128)(2,1)S(1)}) custom-call(f32[32,3]{1,0:T(8,128)S(1)} %reshape.145.bias_ref, bf16[576,1024]{1,0:T(8,128)(2,1)S(1)} %convolution_convert_fusion.4.q_ref.k_ref.v_ref, bf16[576,1024]{1,0:T(8,128)(2,1)S(1)} %convolution_convert_fusion.4.q_ref.k_ref.v_ref, ...), custom_call_target="tpu_custom_call" | custom-call | flops 1000 | bytes 1000 | tf_op jit(solution)/shard_map/attn_forward/pallas_call | solution.py:71
  59.8 15.8 %collective-permute-start.5 = (bf16[1472,512]{1,0:T(8,128)(2,1)}, bf16[1472,512]{1,0:T(8,128)(2,1)}, u32[]{:S(2)}, u32[]{:S(2)}) collective-permute-start(bf16[1472,512]{1,0:T(8,128)(2,1)} %convolution_convert_fusion.2), channel_id=1, source_target_pairs={{0,2},{2,0},{4,6},{6,4},{1,3},{3,1},{5,7},{7,5},{8,10},{10,8},{12,... | collective-permute-start | bytes 4521992 | tf_op jit(solution)/shard_map/ppermute | solution.py:385
  83.8 10.9 %collective-permute-done.7.gr_ref.oth_ref = bf16[1472,512]{1,0:T(8,128)(2,1)S(1)} collective-permute-done((bf16[1472,512]{1,0:T(8,128)(2,1)}, bf16[1472,512]{1,0:T(8,128)(2,1)S(1)}, u32[]{:S(2)}, u32[]{:S(2)}) %collective-permute-start.7) | collective-permute-done | bytes 1507360 | tf_op jit(solution)/shard_map/ppermute | solution.py:379
  95.8 74.5 %ffn_both_ways.1 = (bf16[1024,1792]{1,0:T(8,128)(2,1)}, bf16[1024,1792]{1,0:T(8,128)(2,1)}, bf16[1024,1792]{1,0:T(8,128)(2,1)}, bf16[1472,512]{1,0:T(8,128)(2,1)...) custom-call(bf16[1472,512]{1,0:T(8,128)(2,1)} %multiply_convert_fusion.x_ref.own_ref, ...), custom_call_target="tpu_custom_call" | custom-call | flops 1000 | bytes 1000 | tf_op jit(solution)/shard_map/ffn_both_ways/pallas_call | solution.py:288
  173.8 4.0 weight_grad.6
  177.9 4.8 %weight_grad.7 = bf16[1472,896]{1,0:T(8,128)(2,1)} custom-call(s32[1]{0:T(128)} %bitcast.16.core_ref, bf16[1472,512]{1,0:T(8,128)(2,1)S(1)} %copy-done.1, bf16[1472,512]{1,0:T(8,128)(2,1)S(1)} %copy-done.4, bf16[1024,1792]{1,0:T(8,128)(2,1)S(1)} %copy-done.8), custom_call_target="tpu_custom_call" | custom-call | flops 1000 | bytes 1000 | tf_op jit(solution)/shard_map/weight_grad/pallas_call | solution.py:326
  183.2 4.8 %weight_grad.8 = bf16[1472,896]{1,0:T(8,128)(2,1)} custom-call(s32[1]{0:T(128)} %bitcast.16.core_ref, bf16[1472,512]{1,0:T(8,128)(2,1)S(1)} %copy-done.1, bf16[1472,512]{1,0:T(8,128)(2,1)S(1)} %copy-done.4, bf16[1024,1792]{1,0:T(8,128)(2,1)S(1)} %copy-done.6), custom_call_target="tpu_custom_call" | custom-call | flops 1000 | bytes 1000 | tf_op jit(solution)/shard_map/weight_grad/pallas_call | solution.py:326
  188.0 5.3 %weight_grad.9 = bf16[1472,896]{1,0:T(8,128)(2,1)S(1)} custom-call(s32[1]{0:T(128)} %bitcast.15.core_ref, bf16[1472,512]{1,0:T(8,128)(2,1)S(1)} %copy-done, bf16[1472,512]{1,0:T(8,128)(2,1)S(1)} %copy-done.12, bf16[1024,1792]{1,0:T(8,128)(2,1)S(1)} %copy-done.10, bf16[1472,896]{1,0:T(8,128)(2,1)} %collective-permute-done.10.refs_0_), custom_call_target="tpu_custom_call" | custom-call | flops 1000 | bytes 1000 | tf_op jit(solution)/shard_map/weight_grad/pallas_call | solution.py:326
  198.3 5.3 %weight_grad.10 = bf16[1472,896]{1,0:T(8,128)(2,1)S(1)} custom-call(s32[1]{0:T(128)} %bitcast.15.core_ref, bf16[1472,512]{1,0:T(8,128)(2,1)S(1)} %copy-done.1, bf16[1472,512]{1,0:T(8,128)(2,1)S(1)} %copy-done.5, bf16[1024,1792]{1,0:T(8,128)(2,1)S(1)} %copy-done.9, bf16[1472,896]{1,0:T(8,128)(2,1)} %collective-permute-done.11.refs_0_), custom_call_target="tpu_custom_call" | custom-call | flops 1000 | bytes 1000 | tf_op jit(solution)/shard_map/weight_grad/pallas_call | solution.py:326
  203.6 6.1 %weight_grad.11 = bf16[1472,896]{1,0:T(8,128)(2,1)S(1)} custom-call(s32[1]{0:T(128)} %bitcast.15.core_ref, bf16[1472,512]{1,0:T(8,128)(2,1)S(1)} %copy-done.1, bf16[1472,512]{1,0:T(8,128)(2,1)S(1)} %copy-done.5, bf16[1024,1792]{1,0:T(8,128)(2,1)S(1)} %copy-done.7, bf16[1472,896]{1,0:T(8,128)(2,1)} %collective-permute-done.12.refs_0_), custom_call_target="tpu_custom_call" | custom-call | flops 1000 | bytes 1000 | tf_op jit(solution)/shard_map/weight_grad/pallas_call | solution.py:326
  217.6 3.9 convolution_convert_fusion.5.go_ref
  221.6 20.5 %attn_backward.1 = (bf16[192,1024]{1,0:T(8,128)(2,1)S(1)}, bf16[192,1024]{1,0:T(8,128)(2,1)S(1)}, bf16[192,1024]{1,0:T(8,128)(2,1)S(1)}, f32[3,32,256]{2,1,0:T(8,128)S(1)}) custom-call(bf16[576,1024]{1,0:T(8,128)(2,1)S(1)} %copy-done.3, bf16[576,1024]{1,0:T(8,128)(2,1)S(1)} %copy-done.3, bf16[576,1024]{1,0:T(8,128)(2,1)S(1)} %copy-done.3, ...), custom_call_target="tpu_custom_call" | custom-call | flops 1000 | bytes 1000 | tf_op jit(solution)/shard_map/attn_backward/pallas_call | solution.py:152
  242.2 5.1 %collective-permute-done.14 = bf16[4,184,896]{2,1,0:T(8,128)(2,1)} collective-permute-done((bf16[4,184,896]{2,1,0:T(8,128)(2,1)}, bf16[4,184,896]{2,1,0:T(8,128)(2,1)}, u32[]{:S(2)}, u32[]{:S(2)}) %collective-permute-start.14) | collective-permute-done | bytes 1318944 | tf_op jit(solution)/shard_map/ppermute | solution.py:391
  250.1 4.0 convolution_convert_fusion.1
  254.0 4.1 convolution_convert_fusion.3
  272.0 9.0 %collective-permute-done.22 = bf16[2,2,184,384]{3,2,1,0:T(8,128)(2,1)} collective-permute-done((bf16[2,2,184,384]{3,2,1,0:T(8,128)(2,1)}, bf16[2,2,184,384]{3,2,1,0:T(8,128)(2,1)}, u32[]{:S(2)}, u32[]{:S(2)}) %collective-permute-start.22) | collective-permute-done | bytes 565280 | tf_op jit(solution)/shard_map/ppermute | solution.py:388
  306.1 22.4 %collective-permute-done.36 = bf16[4,184,896]{2,1,0:T(8,128)(2,1)S(1)} collective-permute-done((bf16[4,184,896]{2,1,0:T(8,128)(2,1)S(1)}, bf16[4,184,896]{2,1,0:T(8,128)(2,1)S(1)}, u32[]{:S(2)}, u32[]{:S(2)}) %collective-permute-start.36) | collective-permute-done | bytes 1318944 | tf_op jit(solution)/shard_map/ppermute | solution.py:391
  331.6 3.9 collective-permute-done.26
  340.5 5.4 %collective-permute-done.27 = bf16[368,384]{1,0:T(8,128)(2,1)} collective-permute-done((bf16[368,384]{1,0:T(8,128)(2,1)S(1)}, bf16[368,384]{1,0:T(8,128)(2,1)}, u32[]{:S(2)}, u32[]{:S(2)}) %collective-permute-start.27) | collective-permute-done | bytes 282656 | tf_op jit(solution)/shard_map/ppermute | solution.py:388
  354.5 6.4 %collective-permute-done.30 = f32[1664]{0:T(1024)S(1)} collective-permute-done((f32[1664]{0:T(1024)S(1)}, f32[1664]{0:T(1024)S(1)}, u32[]{:S(2)}, u32[]{:S(2)}) %collective-permute-start.30) | collective-permute-done | bytes 6688 | tf_op jit(solution)/shard_map/ppermute | solution.py:388
  391.7 13.8 %reduce-scatter.11.cloned.1.call-done = bf16[368,896]{1,0:T(8,128)(2,1)} async-done(((bf16[1472,896]{1,0:T(8,128)(2,1)}), bf16[368,896]{1,0:T(8,128)(2,1)}) %reduce-scatter.11.cloned.1.call-update) | async-done | bytes 659472 | tf_op jit(solution)/shard_map/reduce_scatter | solution.py:413
  406.9 32.0 %reduce-scatter.17.cloned.1.call-done = bf16[184,896]{1,0:T(8,128)(2,1)} async-done(((bf16[736,896]{1,0:T(8,128)(2,1)}), bf16[184,896]{1,0:T(8,128)(2,1)}) %reduce-scatter.17.cloned.1.call-update) | async-done | bytes 329744
  444.3 4.1 collective-permute-done.37
  (270 shorter events, 155.8 us)
Async XLA Ops:
  7.2 322.8 %reduce-scatter.13.cloned.1.call-start = ((), (), s32[]{:S(2)}) async-start(), calls=%async_computation.5 | async-start | bytes 706560
  14.9 23.0 %collective-permute-start.3 = (bf16[576,1472]{1,0:T(8,128)(2,1)}, bf16[576,1472]{1,0:T(8,128)(2,1)S(1)}, u32[]{:S(2)}, u32[]{:S(2)}) collective-permute-start(bf16[576,1472]{1,0:T(8,128)(2,1)} %pad_maximum_fusion.1), channel_id=1, source_target_pairs={{1,2},{2,1},{5,6},{6,5},{9,10},{10,9},{13,14},{14,13},{17,18},{18,... | collective-permute-start | bytes 5087240 | tf_op jit(solution)/shard_map/ppermute | solution.py:375
  19.8 18.8 %collective-permute-start.4 = (bf16[1472,512]{1,0:T(8,128)(2,1)S(1)}, bf16[1472,512]{1,0:T(8,128)(2,1)S(1)}, u32[]{:S(2)}, u32[]{:S(2)}) collective-permute-start(bf16[1472,512]{1,0:T(8,128)(2,1)S(1)} %fusion.5), channel_id=1, source_target_pairs={{0,2},{2,0},{4,6},{6,4},{1,3},{3,1},{5,7},{7,5},{8,10},{10,8},{12,... | collective-permute-start | bytes 4521992 | tf_op jit(solution)/shard_map/ppermute | solution.py:385
  34.6 42.6 %collective-permute-start.6 = (bf16[1472,512]{1,0:T(8,128)(2,1)}, bf16[1472,512]{1,0:T(8,128)(2,1)}, u32[]{:S(2)}, u32[]{:S(2)}) collective-permute-start(bf16[1472,512]{1,0:T(8,128)(2,1)} %fusion.16), channel_id=1, source_target_pairs={{1,2},{2,1},{5,6},{6,5},{9,10},{10,9},{13,14},{14,13},{17,18},{18,... | collective-permute-start | bytes 4521992 | tf_op jit(solution)/shard_map/ppermute | solution.py:375
  59.8 20.1 %collective-permute-start.5 = (bf16[1472,512]{1,0:T(8,128)(2,1)}, bf16[1472,512]{1,0:T(8,128)(2,1)}, u32[]{:S(2)}, u32[]{:S(2)}) collective-permute-start(bf16[1472,512]{1,0:T(8,128)(2,1)} %convolution_convert_fusion.2), channel_id=1, source_target_pairs={{0,2},{2,0},{4,6},{6,4},{1,3},{3,1},{5,7},{7,5},{8,10},{10,8},{12,... | collective-permute-start | bytes 4521992 | tf_op jit(solution)/shard_map/ppermute | solution.py:385
  75.5 19.2 %collective-permute-start.7 = (bf16[1472,512]{1,0:T(8,128)(2,1)}, bf16[1472,512]{1,0:T(8,128)(2,1)S(1)}, u32[]{:S(2)}, u32[]{:S(2)}) collective-permute-start(bf16[1472,512]{1,0:T(8,128)(2,1)} %fusion.16), channel_id=1, source_target_pairs={{0,1},{1,3},{2,0},{3,2},{4,5},{5,7},{6,4},{7,6},{8,9},{9,11},{10,8... | collective-permute-start | bytes 4521992 | tf_op jit(solution)/shard_map/ppermute | solution.py:379
  177.8 10.3 %collective-permute-start.10 = (bf16[1472,896]{1,0:T(8,128)(2,1)S(1)}, bf16[1472,896]{1,0:T(8,128)(2,1)}, u32[]{:S(2)}, u32[]{:S(2)}) collective-permute-start(bf16[1472,896]{1,0:T(8,128)(2,1)S(1)} %weight_grad.6), channel_id=1, source_target_pairs={{0,2},{2,0},{4,6},{6,4},{1,3},{3,1},{5,7},{7,5},{8,10},{10,8},{12,... | collective-permute-start | bytes 7913480 | tf_op jit(solution)/shard_map/ppermute | solution.py:385
  182.7 12.1 %collective-permute-start.11 = (bf16[1472,896]{1,0:T(8,128)(2,1)}, bf16[1472,896]{1,0:T(8,128)(2,1)}, u32[]{:S(2)}, u32[]{:S(2)}) collective-permute-start(bf16[1472,896]{1,0:T(8,128)(2,1)} %weight_grad.7), channel_id=1, source_target_pairs={{0,2},{2,0},{4,6},{6,4},{1,3},{3,1},{5,7},{7,5},{8,10},{10,8},{12,... | collective-permute-start | bytes 7913480 | tf_op jit(solution)/shard_map/ppermute | solution.py:385
  188.0 15.6 %collective-permute-start.12 = (bf16[1472,896]{1,0:T(8,128)(2,1)}, bf16[1472,896]{1,0:T(8,128)(2,1)}, u32[]{:S(2)}, u32[]{:S(2)}) collective-permute-start(bf16[1472,896]{1,0:T(8,128)(2,1)} %weight_grad.8), channel_id=1, source_target_pairs={{0,2},{2,0},{4,6},{6,4},{1,3},{3,1},{5,7},{7,5},{8,10},{10,8},{12,... | collective-permute-start | bytes 7913480 | tf_op jit(solution)/shard_map/ppermute | solution.py:385
  216.1 31.3 %collective-permute-start.14 = (bf16[4,184,896]{2,1,0:T(8,128)(2,1)}, bf16[4,184,896]{2,1,0:T(8,128)(2,1)}, u32[]{:S(2)}, u32[]{:S(2)}) collective-permute-start(bf16[4,184,896]{2,1,0:T(8,128)(2,1)} %dynamic-slice_bitcast_fusion.1), channel_id=1, source_target_pairs={{0,4},{2,6},{4,0},{6,2},{1,5},{3,7},{5,1},{7,3},{8,12},{10,14},{12... | collective-permute-start | bytes 3956744 | tf_op jit(solution)/shard_map/ppermute | solution.py:391
  266.8 14.3 %collective-permute-start.22 = (bf16[2,2,184,384]{3,2,1,0:T(8,128)(2,1)}, bf16[2,2,184,384]{3,2,1,0:T(8,128)(2,1)}, u32[]{:S(2)}, u32[]{:S(2)}) collective-permute-start(bf16[2,2,184,384]{3,2,1,0:T(8,128)(2,1)} %constant_dynamic-slice_fusion.1), channel_id=1, source_target_pairs={{0,1},{1,0},{2,3},{3,2},{4,5},{5,4},{6,7},{7,6},{8,9},{9,8},{10,11... | collective-permute-start | bytes 1695752 | tf_op jit(solution)/shard_map/ppermute | solution.py:388
  270.5 14.7 %collective-permute-start.24 = (bf16[2,184,768]{2,1,0:T(8,128)(2,1)}, bf16[2,184,768]{2,1,0:T(8,128)(2,1)S(1)}, u32[]{:S(2)}, u32[]{:S(2)}) collective-permute-start(bf16[2,184,768]{2,1,0:T(8,128)(2,1)} %dynamic-slice_bitcast_fusion.2), channel_id=1, source_target_pairs={{0,4},{2,6},{4,0},{6,2},{1,5},{3,7},{5,1},{7,3},{8,12},{10,14},{12... | collective-permute-start | bytes 1695752 | tf_op jit(solution)/shard_map/ppermute | solution.py:391
  294.0 55.7 %reduce-scatter.15.cloned.1.call-start = ((), (), s32[]{:S(2)}) async-start(), calls=%async_computation.6 | async-start | bytes 1648640
  294.7 110.7 %reduce-scatter.11.cloned.1.call-start = ((), (), s32[]{:S(2)}) async-start(), calls=%async_computation.4 | async-start | bytes 3297280 | tf_op jit(solution)/shard_map/reduce_scatter | solution.py:413
  295.5 143.4 %reduce-scatter.17.cloned.1.call-start = ((), (), s32[]{:S(2)}) async-start(), calls=%async_computation.7 | async-start | bytes 1648640
  297.2 31.3 %collective-permute-start.36 = (bf16[4,184,896]{2,1,0:T(8,128)(2,1)S(1)}, bf16[4,184,896]{2,1,0:T(8,128)(2,1)S(1)}, u32[]{:S(2)}, u32[]{:S(2)}) collective-permute-start(bf16[4,184,896]{2,1,0:T(8,128)(2,1)S(1)} %dynamic-slice_bitcast_fusion), channel_id=1, source_target_pairs={{0,4},{2,6},{4,0},{6,2},{1,5},{3,7},{5,1},{7,3},{8,12},{10,14},{12... | collective-permute-start | bytes 3956744 | tf_op jit(solution)/shard_map/ppermute | solution.py:391
  338.7 68.2 %collective-permute-start.16 = (bf16[1472,512]{1,0:T(8,128)(2,1)S(1)}, bf16[1472,512]{1,0:T(8,128)(2,1)}, u32[]{:S(2)}, u32[]{:S(2)}) collective-permute-start(bf16[1472,512]{1,0:T(8,128)(2,1)S(1)} %copy-done.26), channel_id=1, source_target_pairs={{1,2},{2,1},{5,6},{6,5},{9,10},{10,9},{13,14},{14,13},{17,18},{18,... | collective-permute-start | bytes 4521992 | tf_op jit(solution)/shard_map/ppermute | solution.py:375
  347.9 35.0 %collective-permute-start.28 = (bf16[368,768]{1,0:T(8,128)(2,1)}, bf16[368,768]{1,0:T(8,128)(2,1)}, u32[]{:S(2)}, u32[]{:S(2)}) collective-permute-start(bf16[368,768]{1,0:T(8,128)(2,1)} %maximum_select_fusion.7), channel_id=1, source_target_pairs={{0,2},{2,0},{4,6},{6,4},{1,3},{3,1},{5,7},{7,5},{8,10},{10,8},{12,... | collective-permute-start | bytes 1695752 | tf_op jit(solution)/shard_map/ppermute | solution.py:385
  349.6 29.2 %collective-permute-start.34 = (bf16[184,896]{1,0:T(8,128)(2,1)}, bf16[184,896]{1,0:T(8,128)(2,1)S(1)}, u32[]{:S(2)}, u32[]{:S(2)}) collective-permute-start(bf16[184,896]{1,0:T(8,128)(2,1)} %reduce-scatter.15.cloned.1.call-done), channel_id=1, source_target_pairs={{0,4},{2,6},{4,0},{6,2},{1,5},{3,7},{5,1},{7,3},{8,12},{10,14},{12... | collective-permute-start | bytes 989192 | tf_op jit(solution)/shard_map/ppermute | solution.py:391
  375.0 73.7 %collective-permute-start.9 = (bf16[1472,512]{1,0:T(8,128)(2,1)}, bf16[1472,512]{1,0:T(8,128)(2,1)}, u32[]{:S(2)}, u32[]{:S(2)}) collective-permute-start(bf16[1472,512]{1,0:T(8,128)(2,1)} %get-tuple-element.46), channel_id=1, source_target_pairs={{1,0},{3,1},{0,2},{2,3},{5,4},{7,5},{4,6},{6,7},{9,8},{11,9},{8,10... | collective-permute-start | bytes 4521992 | tf_op jit(solution)/shard_map/ppermute | solution.py:382
  376.2 72.5 %collective-permute-start.8 = (bf16[1472,512]{1,0:T(8,128)(2,1)S(1)}, bf16[1472,512]{1,0:T(8,128)(2,1)}, u32[]{:S(2)}, u32[]{:S(2)}) collective-permute-start(bf16[1472,512]{1,0:T(8,128)(2,1)S(1)} %copy-done.25), channel_id=1, source_target_pairs={{1,2},{2,1},{5,6},{6,5},{9,10},{10,9},{13,14},{14,13},{17,18},{18,... | collective-permute-start | bytes 4521992 | tf_op jit(solution)/shard_map/ppermute | solution.py:375
  381.0 70.9 %collective-permute-start.35 = (bf16[368,896]{1,0:T(8,128)(2,1)}, bf16[368,896]{1,0:T(8,128)(2,1)}, u32[]{:S(2)}, u32[]{:S(2)}) collective-permute-start(bf16[368,896]{1,0:T(8,128)(2,1)} %maximum_select_fusion.5), channel_id=1, source_target_pairs={{0,2},{2,0},{4,6},{6,4},{1,3},{3,1},{5,7},{7,5},{8,10},{10,8},{12,... | collective-permute-start | bytes 1978376 | tf_op jit(solution)/shard_map/ppermute | solution.py:385
  405.4 36.8 %collective-permute-start.39 = (bf16[368,896]{1,0:T(8,128)(2,1)}, bf16[368,896]{1,0:T(8,128)(2,1)}, u32[]{:S(2)}, u32[]{:S(2)}) collective-permute-start(bf16[368,896]{1,0:T(8,128)(2,1)} %reduce-scatter.11.cloned.1.call-done), channel_id=1, source_target_pairs={{0,4},{2,6},{4,0},{6,2},{1,5},{3,7},{5,1},{7,3},{8,12},{10,14},{12... | collective-permute-start | bytes 1978376 | tf_op jit(solution)/shard_map/ppermute | solution.py:391
  443.5 11.8 %collective-permute-start.40 = (bf16[368,896]{1,0:T(8,128)(2,1)S(1)}, bf16[368,896]{1,0:T(8,128)(2,1)S(1)}, u32[]{:S(2)}, u32[]{:S(2)}) collective-permute-start(bf16[368,896]{1,0:T(8,128)(2,1)S(1)} %add_convert_fusion.2), channel_id=1, source_target_pairs={{0,2},{2,0},{4,6},{6,4},{1,3},{3,1},{5,7},{7,5},{8,10},{10,8},{12,... | collective-permute-start | bytes 1978376 | tf_op jit(solution)/shard_map/ppermute | solution.py:385
  (69 other events, 803.6 us)
Sparse Core Ops, SparseCore 0:
  294.1 23.8 reduce-scatter.12
  320.2 29.3 reduce-scatter.14
  352.5 52.8 reduce-scatter.10
  408.2 30.7 reduce-scatter.16

commit v3 on v2

--- a/solution.py
+++ b/solution.py
@@ -181,7 +181,7 @@
 
 def ffn_kernel(
     x_ref, go_ref, gr_ref, gate_w, up_w, down_w,
-    hid_ref, gg_ref, gu_ref, xr_ref, out_ref, out_r_ref, gx_ref,
+    hid_ref, pair_ref, xr_ref, out_ref, out_r_ref, gx_ref,
     xs, gs, out_acc, gx_acc, x_in, gx_out, gx_in, sems,
 ):
     chunk = pl.program_id(0)
@@ -244,8 +244,8 @@
     gg = (grad * up * slope).astype(low)
     gu = (grad * gelu).astype(low)
     hid_ref[...] = hid
-    gg_ref[...] = gg
-    gu_ref[...] = gu
+    pair_ref[0] = gg
+    pair_ref[1] = gu
     out_acc[...] += dot(down_w[...], hid, 1, 1)
     gx_acc[...] += dot(gate_w[...], gg, 1, 1) + dot(up_w[...], gu, 1, 1)
 
@@ -289,8 +289,8 @@
         ffn_kernel,
         grid=(4, hidden // tile),
         in_specs=[full, full, full, weight, weight, weight],
-        out_specs=[act, act, act, full, full, full, full],
-        out_shape=[act_shape, act_shape, act_shape, tokens_of(low), tokens_of(wide), tokens_of(low), tokens_of(wide)],
+        out_specs=[act, pl.BlockSpec((2, size, tile), lambda s, j: (0, (s + 1) % 4, j)), full, full, full, full],
+        out_shape=[act_shape, jax.ShapeDtypeStruct((2, 2 * tokens, hidden), low), tokens_of(low), tokens_of(wide), tokens_of(low), tokens_of(wide)],
         scratch_shapes=[
             pltpu.VMEM((size, width), low),
             pltpu.VMEM((size, width), low),
@@ -343,6 +343,517 @@
     )(core.reshape(1), *args)
 
 
+def back_kernel(
+    hid_h, pair_h, go_h, gr_h, xo_h, xr_h, gx_h, hres_h, xin_h, probs_h, xn1_h, outp_h, outr_h,
+    out_w, w_t, qkv, mixed, gain2, gain1, scale2, scale1,
+    got_p, got_r, got_in, d_out, p_out, a_out, gin, small,
+    r_core, xp, zd, zp, dx, px, bf, rx, ya, xa, za, ab, ab2, sm_src, sm_in, send_sems, recv_sems, load_sems,
+):
+    s = lax.axis_index("seq")
+    y = lax.axis_index("tensor")
+    z = lax.axis_index("dp")
+    c = s % 2
+    m = s // 2
+    width = xp.shape[0]
+    rows = d_out.shape[0]
+    columns = xp.shape[1]
+    half_len = rx.shape[1]
+    length = 2 * half_len
+    heads = probs_h.shape[0]
+    dim = mixed.shape[0] // heads
+    zs = width // rows
+    mesh_id = dict(device_id_type=pl.DeviceIdType.MESH)
+    to_core = {"seq": 2 * m + 1 - c}
+    to_x = {"seq": 2 * (1 - m) + c}
+    to_y = {"tensor": 1 - y}
+    to_z = {"dp": (z + 1) % zs}
+    to_swap = {"seq": 2 * m + y, "tensor": c}
+    to_back = {"seq": 2 * m + 1 - y, "tensor": c}
+
+    barrier = pltpu.get_barrier_semaphore()
+    greet = [to_core, to_y, {"seq": 2 * m + 1 - c, "tensor": 1 - y}, to_x] + [{"dp": (z + i) % zs} for i in range(1, zs)]
+    for who in greet:
+        pl.semaphore_signal(barrier, inc=1, device_id=who, **mesh_id)
+    pl.semaphore_wait(barrier, len(greet))
+
+    def move(k, src, dst, who):
+        return pltpu.make_async_remote_copy(
+            src_ref=src, dst_ref=dst, send_sem=send_sems.at[k], recv_sem=recv_sems.at[k], device_id=who, **mesh_id
+        )
+
+    def load(k, src, dst):
+        return pltpu.make_async_copy(src, dst, load_sems.at[k])
+
+    def chunk(j):
+        return pl.ds(pl.multiple_of(j * rows, rows), rows)
+
+    def side(i, size):
+        return pl.ds(pl.multiple_of(i * size, 128), size)
+
+    order = [(z + zs - 1 - k) % zs for k in range(zs)]
+    mine = side(c, columns)
+    my_half = side(c, half_len)
+    other_half = side(1 - c, half_len)
+
+    swap_out = move(35, outp_h, got_p, to_swap)
+    back_out = move(36, outr_h, got_r, to_back)
+    z_down = [move(3, r_core.at[0, chunk(order[0])], zd.at[0], to_z)] + [
+        move(3 + t, zd.at[t - 1], zd.at[t], to_z) for t in range(1, zs - 1)
+    ]
+    x_down = move(6, zd.at[zs - 2], dx, to_x)
+    core_down = move(7, d_out.at[:, mine], d_out.at[:, mine], to_core)
+    x_pair = [move(8 + k, r_core.at[1, chunk(j)], xp.at[chunk(j)], to_x) for k, j in enumerate(order)]
+    z_pair = [move(12, r_core.at[2, chunk(order[0])], zp.at[0], to_z)] + [
+        move(12 + t, zp.at[t - 1], zp.at[t], to_z) for t in range(1, zs - 1)
+    ]
+    x_pair_back = move(15, zp.at[zs - 2], px, to_x)
+    core_pair = move(16, p_out.at[m, :, mine], p_out.at[m, :, mine], to_core)
+    core_pair_back = move(17, p_out.at[1 - m, :, mine], p_out.at[1 - m, :, mine], to_core)
+    core_branch = move(18, bf.at[:, my_half], bf.at[:, my_half], to_core)
+    a_cols = ya.shape[2]
+    a_rows = xa.shape[1]
+    my_cols = side(y, a_cols)
+    my_rows = pl.ds(pl.multiple_of(m * a_rows, a_rows), a_rows)
+    x_rows = pl.ds(pl.multiple_of((1 - m) * a_rows, a_rows), a_rows)
+    x_attn = [move(24 + k, ya.at[j, x_rows], xa.at[j], to_x) for k, j in enumerate(order)]
+    z_attn = [move(28, ya.at[order[0], my_rows], za.at[0], to_z)] + [
+        move(28 + t, za.at[t - 1], za.at[t], to_z) for t in range(1, zs - 1)
+    ]
+    x_attn_back = move(31, ab.at[my_rows], ab.at[my_rows], to_x)
+    y_attn_back = move(32, ab2.at[:, my_cols], ab2.at[:, my_cols], to_y)
+    core_attn = move(33, ab2, a_out, to_core)
+    swap_in = move(34, gin, got_in, to_swap)
+
+    @pl.when(c != y)
+    def _():
+        swap_out.start()
+
+    back_out.start()
+
+    def step_z_down(t):
+        z_down[t - 1].wait_recv()
+        zd[t - 1] = (zd[t - 1].astype(wide) + r_core[0, chunk(order[t]), :].astype(wide)).astype(low)
+        if t < zs - 1:
+            z_down[t].start()
+
+    def step_z_pair(t):
+        x_pair[t].wait_recv()
+        term = r_core[2, chunk(order[t]), :].astype(wide) + xp[chunk(order[t]), :].astype(wide)
+        if t:
+            z_pair[t - 1].wait_recv()
+            zp[t - 1] = (zp[t - 1].astype(wide) + term).astype(low)
+        else:
+            r_core[2, chunk(order[0]), :] = term.astype(low)
+        if t < zs - 1:
+            z_pair[t].start()
+
+    def weights(r_buf, l_go, l_gr, l_xo, l_xr, s_buf):
+        loads = [
+            load(0, hid_h, r_buf.at[0]),
+            load(1, go_h, l_go),
+            load(2, gr_h, l_gr),
+            load(3, pair_h.at[1 - m], r_buf.at[1]),
+            load(4, xo_h, l_xo),
+            load(5, xr_h, l_xr),
+        ]
+        load_own = load(6, pair_h.at[m], r_buf.at[0])
+        for each in loads:
+            each.start()
+        core = [move(k, s_buf.at[k % 2], r_core.at[k], to_core) for k in range(3)]
+
+        def product(left_o, left_r, right, col, out, add):
+            def block(i, carry):
+                at = chunk(i)
+                total = dot(left_o[at, :], right[:half_len, col], 1, 0)
+                total = total + dot(left_r[at, :], right[half_len:, col], 1, 0)
+                if add:
+                    total = total + out[at, :].astype(wide)
+                out[at, :] = total.astype(low)
+                return carry
+
+            lax.fori_loop(0, zs, block, 0)
+
+        theirs = side(1 - c, columns)
+        for each in loads[:3]:
+            each.wait()
+        product(l_go, l_gr, r_buf.at[0], theirs, s_buf.at[0], False)
+        core[0].start()
+        for each in loads[3:]:
+            each.wait()
+        product(l_xo, l_xr, r_buf.at[1], theirs, s_buf.at[1], False)
+        core[1].start()
+        core[0].wait_recv()
+        product(l_go, l_gr, r_buf.at[0], mine, r_core.at[0], True)
+        z_down[0].start()
+        load_own.start()
+        core[1].wait_recv()
+        product(l_xo, l_xr, r_buf.at[1], mine, r_core.at[1], True)
+        for each in x_pair:
+            each.start()
+        load_own.wait()
+        core[0].wait_send()
+        product(l_xo, l_xr, r_buf.at[0], theirs, s_buf.at[0], False)
+        core[2].start()
+        step_z_down(1)
+        core[2].wait_recv()
+        product(l_xo, l_xr, r_buf.at[0], mine, r_core.at[2], True)
+        core[1].wait_send()
+        core[2].wait_send()
+
+    hidden = hid_h.shape[1]
+    left = pltpu.VMEM((width, half_len), low)
+    pl.run_scoped(
+        weights,
+        pltpu.VMEM((2, length, hidden), low),
+        left,
+        left,
+        left,
+        left,
+        pltpu.VMEM((2, width, columns), low),
+    )
+
+    def attention(gxv, hv, gov, p_buf, k_acc, v_acc, sums, gqkv, gm, xn1, sx, ga):
+        loads = [load(7, gx_h, gxv), load(8, hres_h, hv), load(9, go_h, gov), load(10, xn1_h, xn1)]
+        load_x = load(11, xin_h, gov)
+        for each in loads:
+            each.start()
+
+        def probs_load(h, b, slot):
+            return load(12 + slot, probs_h.at[h, :, side(b, q_block)], p_buf.at[slot])
+
+        probs_load(0, 0, 0).start()
+        lanes = half_len // 128
+        piece = 64
+        pieces = width // piece
+
+        def fold(a):
+            return sum(a[:, i * 128 : (i + 1) * 128] for i in range(lanes))
+
+        def spread(a):
+            return jnp.concatenate([a] * lanes, axis=1)
+
+        def norm_backward(values, gain, scale, grad, store, row):
+            def first(i, total):
+                at = pl.ds(pl.multiple_of(i * piece, piece), piece)
+                return total + jnp.sum(values(at) * (spread(gain[at, :]) * grad(at)), axis=0, keepdims=True)
+
+            total = lax.fori_loop(0, pieces, first, jnp.zeros((1, half_len), wide))
+            mean = total * scale[...] * (1.0 / width)
+
+            def second(i, carry):
+                at = pl.ds(pl.multiple_of(i * piece, piece), piece)
+                g = grad(at)
+                normed = values(at) * scale[...]
+                store(at, scale[...] * (spread(gain[at, :]) * g - normed * mean))
+                ga_part[at, :] = fold(g * normed)
+                return carry
+
+            lax.fori_loop(0, pieces, second, 0)
+            small[row : row + 1, :] = jnp.sum(ga_part[...].T, axis=0, keepdims=True)
+
+        ga_part = sums.at[:width, :128]
+        small[...] = jnp.zeros_like(small)
+        for each in loads[:3]:
+            each.wait()
+
+        def store_hres(at, back):
+            total = gov[at, :].astype(wide) + back
+            gxv[at, :] = total
+            bf[at, my_half] = total.astype(low)
+
+        norm_backward(lambda at: hv[at, :], gain2, scale2, lambda at: gxv[at, :], store_hres, 0)
+        core_branch.start()
+        load_x.start()
+        step_z_down(2)
+        core_branch.wait_recv()
+        gm[...] = dot(out_w[...], bf[...], 1, 0).astype(low)
+
+        reach = length - q_block
+        blocks = length // q_block
+        near_rows = q_block + 2 * band_half
+        d = (
+            lax.broadcasted_iota(jnp.int32, (near_rows, q_block), 0)
+            - lax.broadcasted_iota(jnp.int32, (near_rows, q_block), 1)
+            - band_half
+        )
+        for h in range(heads):
+            head = pl.ds(h * dim, dim)
+            k_rows = pl.ds((heads + h) * dim, dim)
+            v_rows = pl.ds((2 * heads + h) * dim, dim)
+            k_acc[...] = jnp.zeros_like(k_acc)
+            v_acc[...] = jnp.zeros_like(v_acc)
+            sums[...] = jnp.zeros_like(sums)
+
+            def block(b, carry):
+                slot = b % 2
+                at = side(b, q_block)
+                probs_load(h, b, slot).wait()
+
+                @pl.when(b < blocks - 1)
+                def _():
+                    probs_load(h, b + 1, 1 - slot).start()
+
+                if h < heads - 1:
+
+                    @pl.when(b == blocks - 1)
+                    def _():
+                        probs_load(h + 1, 0, 1 - slot).start()
+
+                probs = p_buf[slot]
+                go = gm[head, at]
+                inner = jnp.sum(go.astype(wide) * mixed[head, at].astype(wide), axis=0, keepdims=True)
+                scores = probs.astype(wide) * (dot(qkv[v_rows, :], go, 0, 0) - inner)
+                first = pl.multiple_of(reach - b * q_block, q_block)
+                sums[pl.ds(first, length), :] += scores
+                scores = scores.astype(low)
+                gqkv[head, at] = dot(qkv[k_rows, :], scores, 1, 0).astype(low)
+                k_acc[...] += dot(qkv[head, at], scores, 1, 1)
+                v_acc[...] += dot(go, probs, 1, 1)
+                return carry
+
+            lax.fori_loop(0, blocks, block, 0)
+            gqkv[k_rows, :] = k_acc[...].astype(low)
+            gqkv[v_rows, :] = v_acc[...].astype(low)
+            near = sums[reach - band_half : reach + q_block + band_half, :]
+            n = jnp.abs(d)
+            bucket = jnp.zeros((near_rows, q_block), jnp.int32)
+            for step in steps_at:
+                bucket = bucket + jnp.where(n >= step, 1, 0)
+            bucket = bucket + jnp.where(d > 0, 16, 0)
+            totals = []
+            for b in range(32):
+                total = jnp.sum(jnp.where(bucket == b, near, 0.0), axis=0, keepdims=True)
+                if b == 15:
+                    total = total + jnp.sum(sums[: reach - band_half, :], axis=0, keepdims=True)
+                if b == 31:
+                    total = total + jnp.sum(sums[reach + q_block + band_half :, :], axis=0, keepdims=True)
+                totals.append(total)
+            totals = jnp.concatenate(totals, axis=0)
+            totals = jnp.concatenate([totals, jnp.zeros((96, q_block), wide)], axis=0)
+            line = jnp.sum(totals.T, axis=0, keepdims=True)
+            for side_c in range(2):
+                row = 8 + side_c * heads + h
+                small[row : row + 1, :128] = jnp.where(c == side_c, line, 0.0)
+            if h == 0:
+                step_z_down(3)
+            if h == 1:
+                step_z_pair(0)
+
+        def input_grad(half, store):
+            def block(i, carry):
+                at = chunk(i)
+                store(at, dot(w_t[at, :], gqkv[:, half], 1, 0))
+                return carry
+
+            lax.fori_loop(0, zs, block, 0)
+
+        def store_sent(at, value):
+            sx[at, :] = value.astype(low)
+
+        input_grad(other_half, store_sent)
+        core_x = move(19, sx, rx, to_core)
+        core_x.start()
+        loads[3].wait()
+        y_attn = [
+            move(20 + k, ga.at[j, :, side(1 - y, a_cols)], ya.at[j], to_y) for k, j in enumerate(order)
+        ]
+        wide_cols = gqkv.shape[0]
+        for k, j in enumerate(order):
+            ga[j, :rows, :wide_cols] = dot(xn1[chunk(j), :], gqkv[...], 1, 1).astype(low)
+            ga[j, :rows, wide_cols:] = dot(bf[chunk(j), :], mixed[...], 1, 1).astype(low)
+            ga[j, rows:, :] = jnp.zeros((ga.shape[1] - rows, ga.shape[2]), low)
+            y_attn[k].start()
+        step_z_pair(1)
+
+        def store_own(at, value):
+            hv[at, :] = value
+
+        input_grad(my_half, store_own)
+        load_x.wait()
+        core_x.wait_recv()
+
+        def store_in(at, back):
+            gin[at, :] = (gxv[at, :] + back).astype(low)
+
+        norm_backward(
+            lambda at: gov[at, :].astype(wide),
+            gain1,
+            scale1,
+            lambda at: hv[at, :] + rx[at, :].astype(wide),
+            store_in,
+            1,
+        )
+
+        @pl.when(c != y)
+        def _():
+            swap_in.start()
+
+        for k, j in enumerate(order):
+            y_attn[k].wait_recv()
+            ya[j] = (ya[j].astype(wide) + ga[j, :, my_cols].astype(wide)).astype(low)
+            x_attn[k].start()
+        step_z_pair(2)
+        x_down.start()
+        core_x.wait_send()
+        for each in y_attn:
+            each.wait_send()
+
+    f32 = lambda *shape: pltpu.VMEM(shape, wide)
+    b16 = lambda *shape: pltpu.VMEM(shape, low)
+    pl.run_scoped(
+        attention,
+        f32(width, half_len),
+        f32(width, half_len),
+        b16(width, half_len),
+        b16(2, length, q_block),
+        f32(dim, length),
+        f32(dim, length),
+        f32(2 * length - q_block, q_block),
+        b16(3 * heads * dim, length),
+        b16(heads * dim, length),
+        b16(width, length),
+        b16(width, half_len),
+        b16(zs, ya.shape[1], 2 * ya.shape[2]),
+    )
+
+    def step_attn(t):
+        x_attn[t].wait_recv()
+        term = ya[order[t], my_rows, :].astype(wide) + xa[order[t]].astype(wide)
+        if t:
+            z_attn[t - 1].wait_recv()
+            za[t - 1] = (za[t - 1].astype(wide) + term).astype(low)
+        else:
+            x_attn[0].wait_send()
+            ya[order[0], my_rows, :] = term.astype(low)
+        if t < zs - 1:
+            z_attn[t].start()
+
+    hops = [to_core, to_y, to_x, {"dp": z + 1 - 2 * (z % 2)}, {"dp": (z + 2) % zs}]
+    exchange = [move(37 + i, sm_src.at[i], sm_in.at[i], who) for i, who in enumerate(hops)]
+
+    def start_sum(i):
+        sm_src[i] = small[...]
+        exchange[i].start()
+
+    def end_sum(i):
+        exchange[i].wait_recv()
+        small[...] = sm_src[i] + sm_in[i]
+
+    start_sum(0)
+    step_attn(0)
+    end_sum(0)
+    start_sum(1)
+    step_attn(1)
+    end_sum(1)
+    start_sum(2)
+    step_attn(2)
+    step_attn(3)
+    ab[my_rows, :] = za[zs - 2]
+    x_attn_back.start()
+    step_z_pair(3)
+    p_out[m, :, mine] = zp[zs - 2]
+    x_pair_back.start()
+    core_pair.start()
+    end_sum(2)
+    start_sum(3)
+    x_down.wait_recv()
+    d_out[:, mine] = (zd[zs - 2].astype(wide) + dx[...].astype(wide)).astype(low)
+    core_down.start()
+    end_sum(3)
+    start_sum(4)
+    x_attn_back.wait_recv()
+    ab2[:, my_cols] = ab[...]
+    y_attn_back.start()
+    end_sum(4)
+    y_attn_back.wait_recv()
+
+    @pl.when(c == y)
+    def _():
+        core_attn.start()
+        a_out[...] = ab2[...]
+        core_attn.wait_send()
+
+    x_pair_back.wait_recv()
+    p_out[1 - m, :, mine] = px[...]
+    core_pair_back.start()
+
+    @pl.when(c != y)
+    def _():
+        core_attn.wait_recv()
+        swap_out.wait()
+        swap_in.wait()
+
+    back_out.wait()
+    for each in (core_down, core_pair, core_pair_back):
+        each.wait()
+    core_branch.wait_send()
+    x_down.wait_send()
+    x_pair_back.wait_send()
+    x_attn_back.wait_send()
+    y_attn_back.wait_send()
+    for each in z_down + x_pair + z_pair + x_attn[1:] + z_attn + exchange:
+        each.wait_send()
+
+
+def back_all(
+    hid, pair, g_own, g_oth, x_own, x_oth, gx, hres, x_in, probs, xn_one, out_first, out_oth,
+    out_w, qkv_w, qkv, mixed, gain_two, gain_one, scale_two, scale_one, zs,
+):
+    width, half_len = g_own.shape
+    length = 2 * half_len
+    rows = width // zs
+    columns = hid.shape[1] // 2
+    heads = probs.shape[0]
+    a_cols = 2 * (qkv_w.shape[0] + out_w.shape[0]) // 4
+    a_len = -(-rows // 32) * 32
+    hbm = pl.BlockSpec(memory_space=pl.ANY)
+    vmem = pl.BlockSpec(memory_space=pltpu.VMEM)
+    sds = lambda kind, *shape: jax.ShapeDtypeStruct(shape, kind)
+    b16 = lambda *shape: pltpu.VMEM(shape, low)
+    spread = lambda gain: jnp.broadcast_to(gain, (width, 128))
+    return pl.pallas_call(
+        back_kernel,
+        in_specs=[hbm] * 13 + [vmem] * 8,
+        out_specs=[hbm] * 3 + [vmem] * 5,
+        out_shape=[
+            sds(low, width, half_len),
+            sds(low, width, half_len),
+            sds(low, width, half_len),
+            sds(low, rows, 2 * columns),
+            sds(low, 2, rows, 2 * columns),
+            sds(low, a_len, 2 * a_cols),
+            sds(low, width, half_len),
+            sds(wide, 16, width),
+        ],
+        scratch_shapes=[
+            b16(3, width, columns),
+            b16(width, columns),
+            b16(zs - 1, rows, columns),
+            b16(zs - 1, rows, columns),
+            b16(rows, columns),
+            b16(rows, columns),
+            b16(width, length),
+            b16(width, half_len),
+            b16(zs, a_len, a_cols),
+            b16(zs, a_len // 2, a_cols),
+            b16(zs - 1, a_len // 2, a_cols),
+            b16(a_len, a_cols),
+            b16(a_len, 2 * a_cols),
+            pltpu.VMEM((5, 16, width), wide),
+            pltpu.VMEM((5, 16, width), wide),
+            pltpu.SemaphoreType.DMA((42,)),
+            pltpu.SemaphoreType.DMA((42,)),
+            pltpu.SemaphoreType.DMA((14,)),
+        ],
+        compiler_params=pltpu.CompilerParams(vmem_limit_bytes=61 << 20, collective_id=1, has_side_effects=True),
+        cost_estimate=hint,
+        name="back_all",
+    )(
+        hid, pair, g_own, g_oth, x_own, x_oth, gx, hres, x_in, probs, xn_one, out_first, out_oth,
+        out_w, qkv_w.T, qkv, mixed, spread(gain_two), spread(gain_one), scale_two, scale_one,
+    )
+
+
 def norm_of(values, gain):
     scale = lax.rsqrt(jnp.mean(values * values, axis=0, keepdims=True) + eps_norm)
     return values * scale * gain, scale
@@ -511,9 +1022,36 @@
 
     normed, scale_two = norm_of(hres, gain_two)
     xn_own = normed.astype(low)
-    hid, grad_gate, grad_up, xn_oth, out_own, out_oth, gx = ffn(
+    hid, pair, xn_oth, out_own, out_oth, gx = ffn(
         xn_own, g_own, g_oth, gate_weight, up_weight, down_weight.T
     )
+    if moves.nx == 2 and moves.nz == 4:
+        out_first = (hres + out_own).astype(low)
+        got_first, got_oth, got_in, sum_d, sum_p, sums, grad_in, small = back_all(
+            hid, pair, g_own, g_oth, xn_own, xn_oth, gx, hres, x_in, probs, xn_one, out_first, out_oth,
+            out_w, qkv_w, qkv, mixed, gain_two, gain_one, scale_two, scale_one, moves.nz,
+        )
+        out_y = jnp.where(c == y, out_first, got_first).astype(wide) + got_oth.astype(wide)
+        grad_in = jnp.where(c == y, grad_in, got_in).astype(wide)
+        sums = sums[: width // moves.nz].astype(wide)
+        sum_q, sum_k, sum_v, sum_o = (
+            sums[:, i * inner_width : (i + 1) * inner_width] for i in range(4)
+        )
+        return (
+            out_y.astype(low).T.reshape(half_len, 1, width),
+            grad_in.T.reshape(half_len, 1, width),
+            small[1],
+            sum_q,
+            sum_k,
+            sum_v,
+            small[8 : 8 + 2 * heads, : position_bias.shape[0]].T,
+            sum_o.T,
+            small[0],
+            sum_p[0].astype(wide),
+            sum_p[1].astype(wide),
+            sum_d.astype(wide).T,
+        )
+    grad_gate, grad_up = pair[0], pair[1]
 
     columns = hid.shape[1] // 2
     send_d = weight_grad(g_own, g_oth, hid, 1 - c)

time: 471 us -> 358 us (0.76)
  waiting for transfers between devices: 128 us -> 9.03 us
  Pallas kernels: 140 us -> 250 us
  starting transfers between devices: 74.4 us -> 26.9 us
  matrix products: 26.1 us -> 5.93 us
  other arithmetic: 48.3 us -> 34.6 us
  between operations: 15.6 us -> 2.05 us
  local copies, waits for them, and re-layouts: 33.9 us -> 23.7 us
    pallas_call x7 -> x1, Pallas kernels: 50.8 us -> 161 us  [back_all(): pl.pallas_call(back_kernel, in_specs=[hbm] * 13 + [vmem] * 8, out_specs=[...]
    ppermute x20 -> x0, waiting for transfers between devices: 67.2 us -> none  [the longest x8 38.8 us: over_x(): return lax.ppermute(a, 'seq', self.ring_x)]
    unnamed x7 -> x0, waiting for transfers between devices: 34.7 us -> none
    ppermute x20 -> x0, starting transfers between devices: 29.1 us -> none  [the longest x8 12.3 us: over_x(): return lax.ppermute(a, 'seq', self.ring_x)]
    dot_general x8 -> x3, matrix products: 26.1 us -> 5.93 us  [dot(): lax.dot_general(a, b, (((ca,), (cb,)), ((), ())), preferred_element_type=...]
    ppermute x13 -> x2, starting transfers between devices: 33.7 us -> 17.2 us  [core(): return lax.ppermute(a, 'seq', [(s, s ^ 1) for s in range(2 * self.nx)])]
    reduce_scatter x1 -> x0, waiting for transfers between devices: 13.8 us -> none  [scatter_z(): return lax.psum_scatter(a, 'dp', scatter_dimension=0, tiled=True)]
    convert_element_type x12 -> x3, other arithmetic: 18.4 us -> 7.69 us  [the longest x1 3.5 us: local(): out_first = (hres + out_own).astype(low)]
  transfers between devices with their start and end apart: 45 -> 8, of which waited for: 20 -> 1; matrix products, arithmetic and copies ran while one was open for 15% -> 11% of each run, Pallas kernels for 12% -> 4%
where the time goes in v3:
time: 358 us; the launch traced here: 352 us
  Pallas kernels  250 us (70%)
  other arithmetic  34.6 us (10%)
  starting transfers between devices  26.9 us (8%)
  local copies, waits for them, and re-layouts  23.7 us (7%)
  waiting for transfers between devices  9.03 us (3%)
  matrix products  5.93 us (2%)
    pallas_call x1, Pallas kernels, back_all(): pl.pallas_call(back_kernel, in_specs=[hbm] * 13 + [vmem] * 8, out_specs=[...  161 us
    pallas_call x1, Pallas kernels, ffn(): pl.pallas_call(ffn_kernel, grid=(4, hidden // tile), in_specs=[full, full...  74.8 us
    ppermute x2, starting transfers between devices, core(): return lax.ppermute(a, 'seq', [(s, s ^ 1) for s in range(2 * self.nx)])  17.2 us
    pallas_call x1, Pallas kernels, attn_forward(): pl.pallas_call(functools.partial(attn_fwd_kernel, length), grid=(blocks,...  14.5 us
    unnamed x54, local copies, waits for them, and re-layouts  11 us
    ppermute x1, waiting for transfers between devices, second(): return lax.ppermute(a, ('seq', 'tensor'), self.second_pairs)  9.02 us
    ppermute x5, starting transfers between devices, swap(): got = lax.ppermute(a, ('seq', 'tensor'), self.swap_pairs)  8.07 us
  transfers between devices with their start and end apart: 8, of which 1 were waited for; matrix products, arithmetic and copies ran while one was open for 11% of the time, Pallas kernels for 4%

profile of v3, /device:TPU:0, one launch (start us, length us, event | category | flops | bytes accessed | tf_op | source)
XLA Modules:
  0.0 352.4 jit_solution(7492739269654811520)
XLA Ops:
  0.7 2.0 collective-permute-start
  9.4 1.9 pad_maximum_fusion
  11.2 2.5 copy.56
  13.7 2.0 collective-permute-start.3
  15.7 2.6 fusion.5
  22.0 6.6 %collective-permute-start.4 = (bf16[1472,512]{1,0:T(8,128)(2,1)}, bf16[1472,512]{1,0:T(8,128)(2,1)}, u32[]{:S(2)}, u32[]{:S(2)}) collective-permute-start(bf16[1472,512]{1,0:T(8,128)(2,1)} %fusion.3), channel_id=1, source_target_pairs={{0,2},{2,0},{4,6},{6,4},{1,3},{3,1},{5,7},{7,5},{8,10},{10,8},{12,... | collective-permute-start | bytes 4521992 | tf_op jit(solution)/shard_map/ppermute | solution.py:896
  31.0 1.9 collective-permute-start.6
  34.3 3.9 %copy.57 = bf16[576,1472]{0,1:T(8,128)(2,1)} copy(bf16[576,1472]{1,0:T(8,128)(2,1)} %collective-permute-done.3) | data formatting | bytes 3391488 | tf_op jit(solution)/shard_map/ppermute | solution.py:886
  39.4 3.9 %maximum_select_fusion.xn1_h = bf16[1472,1024]{1,0:T(8,128)(2,1)S(1)} fusion(bf16[1472,512]{1,0:T(8,128)(2,1)} %collective-permute-done.4, bf16[1472,512]{1,0:T(8,128)(2,1)} %fusion.3, pred[]{:T(512)S(6)} %eq.7), kind=kLoop, calls=%fused_computation.7 | loop fusion | flops 13565952 | bytes 6029313 | tf_op jit(solution)/shard_map/jit(_where)/select_n | solution.py:1005
  43.4 2.0 convolution_convert_fusion.1.q_ref.k_ref.v_ref.qkv
  45.7 14.5 %attn_forward.1 = (bf16[3,1024,1024]{2,1,0:T(8,128)(2,1)}, bf16[192,1024]{1,0:T(8,128)(2,1)S(1)}) custom-call(f32[32,3]{1,0:T(8,128)S(1)} %reshape.125.bias_ref, bf16[576,1024]{1,0:T(8,128)(2,1)S(1)} %convolution_convert_fusion.1.q_ref.k_ref.v_ref.qkv, bf16[576,1024]{1,0:T(8,128)(2,1)S(1)} %convolution_convert_fusion.1.q_ref.k_ref.v_ref.qkv, ...), custom_call_target="tpu_custom_call" | custom-call | flops 1000 | bytes 1000 | tf_op jit(solution)/shard_map/attn_forward/pallas_call | solution.py:71
  60.2 1.7 convolution_convert_fusion
  61.9 10.6 %collective-permute-start.5 = (bf16[1472,512]{1,0:T(8,128)(2,1)}, bf16[1472,512]{1,0:T(8,128)(2,1)}, u32[]{:S(2)}, u32[]{:S(2)}) collective-permute-start(bf16[1472,512]{1,0:T(8,128)(2,1)} %convolution_convert_fusion), channel_id=1, source_target_pairs={{0,2},{2,0},{4,6},{6,4},{1,3},{3,1},{5,7},{7,5},{8,10},{10,8},{12,... | collective-permute-start | bytes 4521992 | tf_op jit(solution)/shard_map/ppermute | solution.py:896
  74.2 3.2 fusion.6.w_t
  78.7 2.2 multiply_reduce_fusion
  81.0 1.7 multiply_convert_fusion.x_ref.xo_h
  82.7 9.0 %collective-permute-done.7.gr_ref.gr_h = bf16[1472,512]{1,0:T(8,128)(2,1)} collective-permute-done((bf16[1472,512]{1,0:T(8,128)(2,1)}, bf16[1472,512]{1,0:T(8,128)(2,1)}, u32[]{:S(2)}, u32[]{:S(2)}) %collective-permute-start.7) | collective-permute-done | bytes 1507360 | tf_op jit(solution)/shard_map/ppermute | solution.py:890
  91.7 74.8 %ffn_both_ways.1 = (bf16[1024,1792]{1,0:T(8,128)(2,1)}, bf16[2,1024,1792]{2,1,0:T(8,128)(2,1)}, bf16[1472,512]{1,0:T(8,128)(2,1)}, f32[1472,512]{1,0:T(8,128)}, ...) custom-call(bf16[1472,512]{1,0:T(8,128)(2,1)} %multiply_convert_fusion.x_ref.xo_h, ...), custom_call_target="tpu_custom_call" | custom-call | flops 1000 | bytes 1000 | tf_op jit(solution)/shard_map/ffn_both_ways/pallas_call | solution.py:288
  166.6 3.5 add_convert_fusion.1.outp_h
  172.3 160.9 %back_all.1 = (bf16[1472,512]{1,0:T(8,128)(2,1)}, bf16[1472,512]{1,0:T(8,128)(2,1)}, bf16[1472,512]{1,0:T(8,128)(2,1)}, bf16[368,1792]{1,0:T(8,128)(2,1)}, bf16[...) custom-call(bf16[1024,1792]{1,0:T(8,128)(2,1)} %get-tuple-element.38.hid_h,, ...), custom_call_target="tpu_custom_call" | custom-call | flops 1000 | bytes 1000 | tf_op jit(solution)/shard_map/back_all/pallas_call | solution.py:814
  340.9 1.7 convert_bitcast_fusion.1
  343.6 3.1 bitcast_convert_fusion
  347.8 1.8 fusion.4
  350.2 1.8 convert_bitcast_fusion
  (93 shorter events, 30.6 us)
Async XLA Ops:
  0.6 7.6 %copy-start.18 = (bf16[1472,192]{0,1:T(8,128)(2,1)S(1)}, bf16[1472,192]{0,1:T(8,128)(2,1)}, u32[]{:S(2)}) copy-start(bf16[1472,192]{0,1:T(8,128)(2,1)} %param.21) | copy-start | bytes 1695748
  0.7 17.8 %collective-permute-start = (bf16[1472,512]{1,0:T(8,128)(2,1)}, bf16[1472,512]{1,0:T(8,128)(2,1)}, u32[]{:S(2)}, u32[]{:S(2)}) collective-permute-start(bf16[1472,512]{1,0:T(8,128)(2,1)} %bitcast.55), channel_id=1, source_target_pairs={{1,2},{2,1},{5,6},{6,5},{9,10},{10,9},{13,14},{14,13},{17,18},{18,... | collective-permute-start | bytes 4521992 | tf_op jit(solution)/shard_map/ppermute | solution.py:886
  4.9 13.5 %collective-permute-start.1 = (f32[101]{0:T(128)S(1)}, f32[101]{0:T(128)S(1)}, u32[]{:S(2)}, u32[]{:S(2)}) collective-permute-start(f32[101]{0:T(128)S(1)} %pad_maximum_fusion.1), channel_id=1, source_target_pairs={{1,2},{2,1},{5,6},{6,5},{9,10},{10,9},{13,14},{14,13},{17,18},{18,... | collective-permute-start | bytes 1220 | tf_op jit(solution)/shard_map/ppermute | solution.py:886
  11.2 7.1 %copy-start.9 = (bf16[576,1472]{0,1:T(8,128)(2,1)}, bf16[576,1472]{0,1:T(8,128)(2,1)S(1)}, u32[]{:S(2)}) copy-start(bf16[576,1472]{0,1:T(8,128)(2,1)S(1)} %pad_maximum_fusion) | copy-start | bytes 5087236
  13.7 4.6 %copy-start.21 = (bf16[1472]{0:T(1024)(128)(2,1)S(1)}, bf16[1472]{0:T(1024)(128)(2,1)}, u32[]{:S(2)}) copy-start(bf16[1472]{0:T(1024)(128)(2,1)} %param.18) | copy-start | bytes 8836
  13.7 20.6 %collective-permute-start.3 = (bf16[576,1472]{1,0:T(8,128)(2,1)}, bf16[576,1472]{1,0:T(8,128)(2,1)}, u32[]{:S(2)}, u32[]{:S(2)}) collective-permute-start(bf16[576,1472]{1,0:T(8,128)(2,1)} %copy.56), channel_id=1, source_target_pairs={{1,2},{2,1},{5,6},{6,5},{9,10},{10,9},{13,14},{14,13},{17,18},{18,... | collective-permute-start | bytes 5087240 | tf_op jit(solution)/shard_map/ppermute | solution.py:886
  20.0 58.7 %copy-start.3 = (bf16[1472,512]{1,0:T(8,128)(2,1)}, bf16[1472,512]{1,0:T(8,128)(2,1)S(1)}, u32[]{:S(2)}) copy-start(bf16[1472,512]{1,0:T(8,128)(2,1)S(1)} %broadcast_select_fusion.2.xin_h) | copy-start | bytes 4521988
  20.4 17.8 %copy-start.19 = (f32[512]{0:T(512)}, f32[512]{0:T(512)S(1)}, u32[]{:S(2)}) copy-start(f32[512]{0:T(512)S(1)} %add_rsqrt_fusion.1) | copy-start | bytes 6148
  22.0 17.4 %collective-permute-start.4 = (bf16[1472,512]{1,0:T(8,128)(2,1)}, bf16[1472,512]{1,0:T(8,128)(2,1)}, u32[]{:S(2)}, u32[]{:S(2)}) collective-permute-start(bf16[1472,512]{1,0:T(8,128)(2,1)} %fusion.3), channel_id=1, source_target_pairs={{0,2},{2,0},{4,6},{6,4},{1,3},{3,1},{5,7},{7,5},{8,10},{10,8},{12,... | collective-permute-start | bytes 4521992 | tf_op jit(solution)/shard_map/ppermute | solution.py:896
  28.8 9.4 %collective-permute-start.2 = (bf16[192,1472]{1,0:T(8,128)(2,1)}, bf16[192,1472]{1,0:T(8,128)(2,1)}, u32[]{:S(2)}, u32[]{:S(2)}) collective-permute-start(bf16[192,1472]{1,0:T(8,128)(2,1)} %param.23), channel_id=1, source_target_pairs={{1,2},{2,1},{5,6},{6,5},{9,10},{10,9},{13,14},{14,13},{17,18},{18,... | collective-permute-start | bytes 1695752 | tf_op jit(solution)/shard_map/ppermute | solution.py:886
  31.0 46.4 %collective-permute-start.6 = (bf16[1472,512]{1,0:T(8,128)(2,1)}, bf16[1472,512]{1,0:T(8,128)(2,1)}, u32[]{:S(2)}, u32[]{:S(2)}) collective-permute-start(bf16[1472,512]{1,0:T(8,128)(2,1)} %fusion.5), channel_id=1, source_target_pairs={{1,2},{2,1},{5,6},{6,5},{9,10},{10,9},{13,14},{14,13},{17,18},{18,... | collective-permute-start | bytes 4521992 | tf_op jit(solution)/shard_map/ppermute | solution.py:886
  39.3 20.9 %copy-start.6 = (bf16[192,1472]{1,0:T(8,128)(2,1)}, bf16[192,1472]{1,0:T(8,128)(2,1)S(1)}, u32[]{:S(2)}) copy-start(bf16[192,1472]{1,0:T(8,128)(2,1)S(1)} %broadcast_select_fusion.4.out_w) | copy-start | bytes 1695748
  39.3 4.0 %copy-start.8 = (bf16[576,1472]{0,1:T(8,128)(2,1)S(1)}, bf16[576,1472]{0,1:T(8,128)(2,1)}, u32[]{:S(2)}) copy-start(bf16[576,1472]{0,1:T(8,128)(2,1)} %copy.57) | copy-start | bytes 5087236
  39.4 4.1 %copy-start.10 = (bf16[576,1472]{0,1:T(8,128)(2,1)S(1)}, bf16[576,1472]{0,1:T(8,128)(2,1)}, u32[]{:S(2)}) copy-start(bf16[576,1472]{0,1:T(8,128)(2,1)} %copy-done.9) | copy-start | bytes 5087236
  45.5 14.7 %copy-start = (bf16[576,1024]{1,0:T(8,128)(2,1)}, bf16[576,1024]{1,0:T(8,128)(2,1)S(1)}, u32[]{:S(2)}) copy-start(bf16[576,1024]{1,0:T(8,128)(2,1)S(1)} %convolution_convert_fusion.1.q_ref.k_ref.v_ref.qkv) | copy-start | bytes 3538948
  60.2 18.5 %copy-start.1 = (bf16[192,1024]{1,0:T(8,128)(2,1)}, bf16[192,1024]{1,0:T(8,128)(2,1)S(1)}, u32[]{:S(2)}) copy-start(bf16[192,1024]{1,0:T(8,128)(2,1)S(1)} %get-tuple-element.35.mixed) | copy-start | bytes 1179652
  60.2 12.3 %copy-start.22 = (bf16[1472]{0:T(1024)(128)(2,1)S(1)}, bf16[1472]{0:T(1024)(128)(2,1)}, u32[]{:S(2)}) copy-start(bf16[1472]{0:T(1024)(128)(2,1)} %param.24) | copy-start | bytes 8836
  61.9 16.8 %collective-permute-start.5 = (bf16[1472,512]{1,0:T(8,128)(2,1)}, bf16[1472,512]{1,0:T(8,128)(2,1)}, u32[]{:S(2)}, u32[]{:S(2)}) collective-permute-start(bf16[1472,512]{1,0:T(8,128)(2,1)} %convolution_convert_fusion), channel_id=1, source_target_pairs={{0,2},{2,0},{4,6},{6,4},{1,3},{3,1},{5,7},{7,5},{8,10},{10,8},{12,... | collective-permute-start | bytes 4521992 | tf_op jit(solution)/shard_map/ppermute | solution.py:896
  72.5 4.9 %copy-start.11 = (bf16[1472,512]{1,0:T(8,128)(2,1)S(1)}, bf16[1472,512]{1,0:T(8,128)(2,1)}, u32[]{:S(2)}) copy-start(bf16[1472,512]{1,0:T(8,128)(2,1)} %fusion.5) | copy-start | bytes 4521988
  72.5 19.2 %collective-permute-start.7 = (bf16[1472,512]{1,0:T(8,128)(2,1)}, bf16[1472,512]{1,0:T(8,128)(2,1)}, u32[]{:S(2)}, u32[]{:S(2)}) collective-permute-start(bf16[1472,512]{1,0:T(8,128)(2,1)} %fusion.5), channel_id=1, source_target_pairs={{0,1},{1,3},{2,0},{3,2},{4,5},{5,7},{6,4},{7,6},{8,9},{9,11},{10,8... | collective-permute-start | bytes 4521992 | tf_op jit(solution)/shard_map/ppermute | solution.py:890
  80.9 85.6 %copy-start.2 = (f32[1472,512]{1,0:T(8,128)}, f32[1472,512]{1,0:T(8,128)S(1)}, u32[]{:S(2)}) copy-start(f32[1472,512]{1,0:T(8,128)S(1)} %get-tuple-element.109.hres_h) | copy-start | bytes 9043972
  337.4 3.5 copy-start.17
  343.6 3.1 copy-start.15
  343.6 4.2 %copy-start.16 = (bf16[1472,512]{1,0:T(8,128)(2,1)S(1)}, bf16[1472,512]{1,0:T(8,128)(2,1)}, u32[]{:S(2)}) copy-start(bf16[1472,512]{1,0:T(8,128)(2,1)} %get-tuple-element.45) | copy-start | bytes 4521988
  (7 other events, 15.1 us)

commit v4 on v3

--- a/solution.py
+++ b/solution.py
@@ -181,7 +181,7 @@
 
 def ffn_kernel(
     x_ref, go_ref, gr_ref, gate_w, up_w, down_w,
-    hid_ref, pair_ref, xr_ref, out_ref, out_r_ref, gx_ref,
+    hid_ref, pair_ref, xr_ref, out_ref, out_r_ref, gx_ref, late_ref,
     xs, gs, out_acc, gx_acc, x_in, gx_out, gx_in, sems,
 ):
     chunk = pl.program_id(0)
@@ -196,11 +196,10 @@
             device_id=there, device_id_type=pl.DeviceIdType.MESH,
         )
 
-    def send_gx(h):
-        return pltpu.make_async_remote_copy(
-            src_ref=gx_out.at[h], dst_ref=gx_in.at[h], send_sem=sems.at[4 + h], recv_sem=sems.at[6 + h],
-            device_id=there, device_id_type=pl.DeviceIdType.MESH,
-        )
+    send_gx = pltpu.make_async_remote_copy(
+        src_ref=gx_out, dst_ref=gx_in, send_sem=sems.at[4], recv_sem=sems.at[5],
+        device_id=there, device_id_type=pl.DeviceIdType.MESH,
+    )
 
     @pl.when(tile == 0)
     def _():
@@ -262,17 +261,19 @@
         @pl.when(last & (chunk == 1 + h))
         def _(h=h):
             out_r_ref[:, half[h]] = out_acc[...].astype(low)
-            gx_out[h] = gx_acc[...].astype(low)
-            send_gx(h).start()
+            if h:
+                late_ref[...] = gx_acc[...].astype(low)
+            else:
+                gx_out[...] = gx_acc[...].astype(low)
+                send_gx.start()
 
     @pl.when(last & (chunk == 3))
     def _():
-        for h in range(2):
-            send_gx(h).wait_recv()
-            gx_ref[:, half[h]] += gx_in[h].astype(wide)
+        send_gx.wait_recv()
+        gx_ref[:, half[0]] += gx_in[...].astype(wide)
         for h in range(2):
             send_x(h).wait_send()
-            send_gx(h).wait_send()
+        send_gx.wait_send()
 
 
 def ffn(x, g_own, g_oth, gate_w, up_w, down_w):
@@ -284,22 +285,24 @@
     act = pl.BlockSpec((size, tile), lambda s, j: ((s + 1) % 4, j))
     act_shape = jax.ShapeDtypeStruct((2 * tokens, hidden), low)
     tokens_of = lambda kind: jax.ShapeDtypeStruct((width, tokens), kind)
-    part = pltpu.VMEM((2, width, size), low)
+    part = pltpu.VMEM((width, size), low)
+    late = pl.BlockSpec((width, size), lambda s, j: (0, 0), pipeline_mode=pl.Buffered(1))
     return pl.pallas_call(
         ffn_kernel,
         grid=(4, hidden // tile),
         in_specs=[full, full, full, weight, weight, weight],
-        out_specs=[act, pl.BlockSpec((2, size, tile), lambda s, j: (0, (s + 1) % 4, j)), full, full, full, full],
-        out_shape=[act_shape, jax.ShapeDtypeStruct((2, 2 * tokens, hidden), low), tokens_of(low), tokens_of(wide), tokens_of(low), tokens_of(wide)],
+        out_specs=[act, pl.BlockSpec((2, size, tile), lambda s, j: (0, (s + 1) % 4, j)), full, full, full, full, late],
+        out_shape=[act_shape, jax.ShapeDtypeStruct((2, 2 * tokens, hidden), low), tokens_of(low), tokens_of(wide), tokens_of(low), tokens_of(wide)]
+        + [jax.ShapeDtypeStruct((width, size), low)],
         scratch_shapes=[
             pltpu.VMEM((size, width), low),
             pltpu.VMEM((size, width), low),
             pltpu.VMEM((width, size), wide),
             pltpu.VMEM((width, size), wide),
+            pltpu.VMEM((2, width, size), low),
             part,
             part,
-            part,
-            pltpu.SemaphoreType.DMA((8,)),
+            pltpu.SemaphoreType.DMA((6,)),
         ],
         compiler_params=pltpu.CompilerParams(vmem_limit_bytes=56 << 20, collective_id=0, has_side_effects=True),
         cost_estimate=hint,
@@ -344,10 +347,10 @@
 
 
 def back_kernel(
-    hid_h, pair_h, go_h, gr_h, xo_h, xr_h, gx_h, hres_h, xin_h, probs_h, xn1_h, outp_h, outr_h,
+    hid_h, pair_h, go_h, gr_h, xo_h, xr_h, gx_h, hres_h, xin_h, probs_h, xn1_h, outp_h, outr_h, late_h,
     out_w, w_t, qkv, mixed, gain2, gain1, scale2, scale1,
     got_p, got_r, got_in, d_out, p_out, a_out, gin, small,
-    r_core, xp, zd, zp, dx, px, bf, rx, ya, xa, za, ab, ab2, sm_src, sm_in, send_sems, recv_sems, load_sems,
+    r_core, xp, zd, zp, dx, px, bf, rx, ya, xa, za, ab, late_in, sm_src, sm_in, send_sems, recv_sems, load_sems,
 ):
     s = lax.axis_index("seq")
     y = lax.axis_index("tensor")
@@ -394,111 +397,190 @@
     mine = side(c, columns)
     my_half = side(c, half_len)
     other_half = side(1 - c, half_len)
-
-    swap_out = move(35, outp_h, got_p, to_swap)
-    back_out = move(36, outr_h, got_r, to_back)
-    z_down = [move(3, r_core.at[0, chunk(order[0])], zd.at[0], to_z)] + [
-        move(3 + t, zd.at[t - 1], zd.at[t], to_z) for t in range(1, zs - 1)
+    cut = [(0, 192), (192, rows - 192)]
+
+    def part(j, p):
+        return pl.ds(pl.multiple_of(j * rows + cut[p][0], 16), cut[p][1])
+
+    parts = [pl.ds(*each) for each in cut]
+
+    late = move(0, late_h, late_in, to_y)
+    swap_out = move(1, outp_h, got_p, to_swap)
+    back_out = move(2, outr_h, got_r, to_back)
+    z_down = [move(3, r_core.at[0, chunk(order[0])], zd.at[0], to_z), move(4, zd.at[0], zd.at[1], to_z)]
+    z_down_last = [move(5 + p, zd.at[1, parts[p]], zd.at[2, parts[p]], to_z) for p in range(2)]
+    x_down = [move(7 + p, zd.at[2, parts[p]], dx.at[parts[p]], to_x) for p in range(2)]
+    core_down = [move(9 + p, d_out.at[parts[p], mine], d_out.at[parts[p], mine], to_core) for p in range(2)]
+    z_pair = [move(11, r_core.at[2, chunk(order[0])], zp.at[0], to_z), move(12, zp.at[0], zp.at[1], to_z)]
+    z_pair_last = [move(13 + p, zp.at[1, parts[p]], zp.at[2, parts[p]], to_z) for p in range(2)]
+    x_pair_back = [move(15 + p, zp.at[2, parts[p]], px.at[parts[p]], to_x) for p in range(2)]
+    core_pair = [move(17 + p, p_out.at[m, parts[p], mine], p_out.at[m, parts[p], mine], to_core) for p in range(2)]
+    core_pair_back = [
+        move(19 + p, p_out.at[1 - m, parts[p], mine], p_out.at[1 - m, parts[p], mine], to_core) for p in range(2)
     ]
-    x_down = move(6, zd.at[zs - 2], dx, to_x)
-    core_down = move(7, d_out.at[:, mine], d_out.at[:, mine], to_core)
-    x_pair = [move(8 + k, r_core.at[1, chunk(j)], xp.at[chunk(j)], to_x) for k, j in enumerate(order)]
-    z_pair = [move(12, r_core.at[2, chunk(order[0])], zp.at[0], to_z)] + [
-        move(12 + t, zp.at[t - 1], zp.at[t], to_z) for t in range(1, zs - 1)
-    ]
-    x_pair_back = move(15, zp.at[zs - 2], px, to_x)
-    core_pair = move(16, p_out.at[m, :, mine], p_out.at[m, :, mine], to_core)
-    core_pair_back = move(17, p_out.at[1 - m, :, mine], p_out.at[1 - m, :, mine], to_core)
-    core_branch = move(18, bf.at[:, my_half], bf.at[:, my_half], to_core)
+    core_branch = move(21, bf.at[:, my_half], bf.at[:, my_half], to_core)
     a_cols = ya.shape[2]
     a_rows = xa.shape[1]
     my_cols = side(y, a_cols)
     my_rows = pl.ds(pl.multiple_of(m * a_rows, a_rows), a_rows)
     x_rows = pl.ds(pl.multiple_of((1 - m) * a_rows, a_rows), a_rows)
-    x_attn = [move(24 + k, ya.at[j, x_rows], xa.at[j], to_x) for k, j in enumerate(order)]
-    z_attn = [move(28, ya.at[order[0], my_rows], za.at[0], to_z)] + [
-        move(28 + t, za.at[t - 1], za.at[t], to_z) for t in range(1, zs - 1)
+    x_attn = [move(22 + k, ya.at[j, x_rows], xa.at[j], to_x) for k, j in enumerate(order)]
+    z_attn = [move(26, ya.at[order[0], my_rows], za.at[0], to_z)] + [
+        move(26 + t, za.at[t - 1], za.at[t], to_z) for t in range(1, zs - 1)
     ]
-    x_attn_back = move(31, ab.at[my_rows], ab.at[my_rows], to_x)
-    y_attn_back = move(32, ab2.at[:, my_cols], ab2.at[:, my_cols], to_y)
-    core_attn = move(33, ab2, a_out, to_core)
-    swap_in = move(34, gin, got_in, to_swap)
-
-    @pl.when(c != y)
-    def _():
-        swap_out.start()
-
-    back_out.start()
+    my_piece = ab.at[my_rows, my_cols]
+    spread_attn = [
+        move(29 + i, my_piece, my_piece, who)
+        for i, who in enumerate((to_x, to_y, {"seq": 2 * (1 - m) + c, "tensor": 1 - y}))
+    ]
+    core_attn = move(32, ab, a_out, to_core)
+    swap_in = move(33, gin, got_in, to_swap)
+
+    def x_pair(k):
+        at = chunk((z + zs - 1 - k) % zs)
+        return move(44 + k, r_core.at[1, at], xp.at[at], to_x)
+
+    late.start()
 
     def step_z_down(t):
         z_down[t - 1].wait_recv()
         zd[t - 1] = (zd[t - 1].astype(wide) + r_core[0, chunk(order[t]), :].astype(wide)).astype(low)
-        if t < zs - 1:
-            z_down[t].start()
+        for each in z_down_last if t == 2 else [z_down[t]]:
+            each.start()
+
+    def last_z_down(p):
+        z_down_last[p].wait_recv()
+        at = parts[p]
+        zd[2, at, :] = (zd[2, at, :].astype(wide) + r_core[0, part(z, p), :].astype(wide)).astype(low)
+        x_down[p].start()
+
+    def end_down(p):
+        x_down[p].wait_recv()
+        at = parts[p]
+        d_out[at, mine] = (zd[2, at, :].astype(wide) + dx[at, :].astype(wide)).astype(low)
+        core_down[p].start()
 
     def step_z_pair(t):
-        x_pair[t].wait_recv()
+        x_pair(t).wait_recv()
         term = r_core[2, chunk(order[t]), :].astype(wide) + xp[chunk(order[t]), :].astype(wide)
         if t:
             z_pair[t - 1].wait_recv()
             zp[t - 1] = (zp[t - 1].astype(wide) + term).astype(low)
         else:
             r_core[2, chunk(order[0]), :] = term.astype(low)
+        for each in z_pair_last if t == 2 else [z_pair[t]]:
+            each.start()
+
+    def last_z_pair(p):
+        if p == 0:
+            x_pair(3).wait_recv()
+        z_pair_last[p].wait_recv()
+        at = parts[p]
+        term = r_core[2, part(z, p), :].astype(wide) + xp[part(z, p), :].astype(wide)
+        total = (zp[2, at, :].astype(wide) + term).astype(low)
+        zp[2, at, :] = total
+        x_pair_back[p].start()
+        p_out[m, at, mine] = total
+        core_pair[p].start()
+
+    def end_pair(p):
+        x_pair_back[p].wait_recv()
+        at = parts[p]
+        p_out[1 - m, at, mine] = px[at, :]
+        core_pair_back[p].start()
+
+    def step_attn(t):
+        x_attn[t].wait_recv()
+        term = ya[order[t], my_rows, :].astype(wide) + xa[order[t]].astype(wide)
+        if t:
+            z_attn[t - 1].wait_recv()
+            za[t - 1] = (za[t - 1].astype(wide) + term).astype(low)
+        else:
+            x_attn[0].wait_send()
+            ya[order[0], my_rows, :] = term.astype(low)
         if t < zs - 1:
-            z_pair[t].start()
+            z_attn[t].start()
+
+    hops = [to_core, to_y, to_x, {"dp": z + 1 - 2 * (z % 2)}, {"dp": (z + 2) % zs}]
+    exchange = [move(39 + i, sm_src.at[i], sm_in.at[i], who) for i, who in enumerate(hops)]
+
+    def start_sum(i):
+        sm_src[i] = small[...]
+        exchange[i].start()
+
+    def end_sum(i):
+        exchange[i].wait_recv()
+        small[...] = sm_src[i] + sm_in[i]
 
     def weights(r_buf, l_go, l_gr, l_xo, l_xr, s_buf):
         loads = [
-            load(0, hid_h, r_buf.at[0]),
-            load(1, go_h, l_go),
-            load(2, gr_h, l_gr),
-            load(3, pair_h.at[1 - m], r_buf.at[1]),
-            load(4, xo_h, l_xo),
-            load(5, xr_h, l_xr),
+            load(0, pair_h.at[1 - m], r_buf.at[0]),
+            load(1, xo_h, l_xo),
+            load(2, xr_h, l_xr),
+            load(3, hid_h, r_buf.at[1]),
+            load(4, go_h, l_go),
+            load(5, gr_h, l_gr),
         ]
         load_own = load(6, pair_h.at[m], r_buf.at[0])
         for each in loads:
             each.start()
-        core = [move(k, s_buf.at[k % 2], r_core.at[k], to_core) for k in range(3)]
-
-        def product(left_o, left_r, right, col, out, add):
-            def block(i, carry):
-                at = chunk(i)
+        theirs = side(1 - c, columns)
+
+        def core(i, k):
+            at = chunk((z + zs - 1 - k) % zs)
+            return move(48 + i * zs + k, s_buf.at[i % 2, at], r_core.at[(1, 0, 2)[i], at], to_core)
+
+        def product(left_o, left_r, right, col, i, extra=None):
+            def block(k, carry):
+                at = chunk((z + zs - 1 - k) % zs)
                 total = dot(left_o[at, :], right[:half_len, col], 1, 0)
                 total = total + dot(left_r[at, :], right[half_len:, col], 1, 0)
-                if add:
-                    total = total + out[at, :].astype(wide)
-                out[at, :] = total.astype(low)
+                if extra is None:
+                    s_buf[i % 2, at, :] = total.astype(low)
+                    core(i, k).start()
+                else:
+                    out = (1, 0, 2)[i]
+                    core(i, k).wait_recv()
+                    r_core[out, at, :] = (total + r_core[out, at, :].astype(wide)).astype(low)
+                    extra(k)
                 return carry
 
             lax.fori_loop(0, zs, block, 0)
 
-        theirs = side(1 - c, columns)
+        def at_first(run):
+            def extra(k):
+                pl.when(k == 0)(run)
+
+            return extra
+
+        def sent(i):
+            def block(k, carry):
+                core(i, k).wait_send()
+                return carry
+
+            lax.fori_loop(0, zs, block, 0)
+
         for each in loads[:3]:
             each.wait()
-        product(l_go, l_gr, r_buf.at[0], theirs, s_buf.at[0], False)
-        core[0].start()
+        product(l_xo, l_xr, r_buf.at[0], theirs, 0)
+        product(l_xo, l_xr, r_buf.at[0], mine, 0, lambda k: x_pair(k).start())
+        load_own.start()
+
+        @pl.when(c != y)
+        def _():
+            swap_out.start()
+
+        back_out.start()
         for each in loads[3:]:
             each.wait()
-        product(l_xo, l_xr, r_buf.at[1], theirs, s_buf.at[1], False)
-        core[1].start()
-        core[0].wait_recv()
-        product(l_go, l_gr, r_buf.at[0], mine, r_core.at[0], True)
-        z_down[0].start()
-        load_own.start()
-        core[1].wait_recv()
-        product(l_xo, l_xr, r_buf.at[1], mine, r_core.at[1], True)
-        for each in x_pair:
-            each.start()
+        product(l_go, l_gr, r_buf.at[1], theirs, 1)
+        product(l_go, l_gr, r_buf.at[1], mine, 1, at_first(z_down[0].start))
         load_own.wait()
-        core[0].wait_send()
-        product(l_xo, l_xr, r_buf.at[0], theirs, s_buf.at[0], False)
-        core[2].start()
-        step_z_down(1)
-        core[2].wait_recv()
-        product(l_xo, l_xr, r_buf.at[0], mine, r_core.at[2], True)
-        core[1].wait_send()
-        core[2].wait_send()
+        sent(0)
+        product(l_xo, l_xr, r_buf.at[0], theirs, 2)
+        product(l_xo, l_xr, r_buf.at[0], mine, 2, at_first(lambda: step_z_pair(0)))
+        sent(1)
+        sent(2)
 
     hidden = hid_h.shape[1]
     left = pltpu.VMEM((width, half_len), low)
@@ -555,6 +637,8 @@
         small[...] = jnp.zeros_like(small)
         for each in loads[:3]:
             each.wait()
+        late.wait_recv()
+        gxv[:, late_in.shape[1] :] += late_in[...].astype(wide)
 
         def store_hres(at, back):
             total = gov[at, :].astype(wide) + back
@@ -564,7 +648,7 @@
         norm_backward(lambda at: hv[at, :], gain2, scale2, lambda at: gxv[at, :], store_hres, 0)
         core_branch.start()
         load_x.start()
-        step_z_down(2)
+        step_z_down(1)
         core_branch.wait_recv()
         gm[...] = dot(out_w[...], bf[...], 1, 0).astype(low)
 
@@ -634,10 +718,8 @@
             for side_c in range(2):
                 row = 8 + side_c * heads + h
                 small[row : row + 1, :128] = jnp.where(c == side_c, line, 0.0)
-            if h == 0:
-                step_z_down(3)
             if h == 1:
-                step_z_pair(0)
+                step_z_pair(1)
 
         def input_grad(half, store):
             def block(i, carry):
@@ -651,11 +733,11 @@
             sx[at, :] = value.astype(low)
 
         input_grad(other_half, store_sent)
-        core_x = move(19, sx, rx, to_core)
+        core_x = move(34, sx, rx, to_core)
         core_x.start()
         loads[3].wait()
         y_attn = [
-            move(20 + k, ga.at[j, :, side(1 - y, a_cols)], ya.at[j], to_y) for k, j in enumerate(order)
+            move(35 + k, ga.at[j, :, side(1 - y, a_cols)], ya.at[j], to_y) for k, j in enumerate(order)
         ]
         wide_cols = gqkv.shape[0]
         for k, j in enumerate(order):
@@ -663,7 +745,7 @@
             ga[j, :rows, wide_cols:] = dot(bf[chunk(j), :], mixed[...], 1, 1).astype(low)
             ga[j, rows:, :] = jnp.zeros((ga.shape[1] - rows, ga.shape[2]), low)
             y_attn[k].start()
-        step_z_pair(1)
+        step_z_down(2)
 
         def store_own(at, value):
             hv[at, :] = value
@@ -688,12 +770,23 @@
         def _():
             swap_in.start()
 
-        for k, j in enumerate(order):
+        def step_y_attn(k):
+            j = order[k]
             y_attn[k].wait_recv()
             ya[j] = (ya[j].astype(wide) + ga[j, :, my_cols].astype(wide)).astype(low)
             x_attn[k].start()
+
+        step_y_attn(0)
         step_z_pair(2)
-        x_down.start()
+        start_sum(0)
+        step_y_attn(1)
+        step_attn(0)
+        end_sum(0)
+        start_sum(1)
+        last_z_down(0)
+        step_y_attn(2)
+        last_z_down(1)
+        step_y_attn(3)
         core_x.wait_send()
         for each in y_attn:
             each.wait_send()
@@ -716,66 +809,34 @@
         b16(zs, ya.shape[1], 2 * ya.shape[2]),
     )
 
-    def step_attn(t):
-        x_attn[t].wait_recv()
-        term = ya[order[t], my_rows, :].astype(wide) + xa[order[t]].astype(wide)
-        if t:
-            z_attn[t - 1].wait_recv()
-            za[t - 1] = (za[t - 1].astype(wide) + term).astype(low)
-        else:
-            x_attn[0].wait_send()
-            ya[order[0], my_rows, :] = term.astype(low)
-        if t < zs - 1:
-            z_attn[t].start()
-
-    hops = [to_core, to_y, to_x, {"dp": z + 1 - 2 * (z % 2)}, {"dp": (z + 2) % zs}]
-    exchange = [move(37 + i, sm_src.at[i], sm_in.at[i], who) for i, who in enumerate(hops)]
-
-    def start_sum(i):
-        sm_src[i] = small[...]
-        exchange[i].start()
-
-    def end_sum(i):
-        exchange[i].wait_recv()
-        small[...] = sm_src[i] + sm_in[i]
-
-    start_sum(0)
-    step_attn(0)
-    end_sum(0)
-    start_sum(1)
-    step_attn(1)
     end_sum(1)
     start_sum(2)
-    step_attn(2)
-    step_attn(3)
-    ab[my_rows, :] = za[zs - 2]
-    x_attn_back.start()
-    step_z_pair(3)
-    p_out[m, :, mine] = zp[zs - 2]
-    x_pair_back.start()
-    core_pair.start()
+    end_down(0)
+    last_z_pair(0)
+    end_down(1)
+    last_z_pair(1)
+    step_attn(1)
     end_sum(2)
     start_sum(3)
-    x_down.wait_recv()
-    d_out[:, mine] = (zd[zs - 2].astype(wide) + dx[...].astype(wide)).astype(low)
-    core_down.start()
+    step_attn(2)
+    end_pair(0)
+    step_attn(3)
+    ab[my_rows, my_cols] = za[zs - 2]
+    for each in spread_attn:
+        each.start()
     end_sum(3)
     start_sum(4)
-    x_attn_back.wait_recv()
-    ab2[:, my_cols] = ab[...]
-    y_attn_back.start()
-    end_sum(4)
-    y_attn_back.wait_recv()
+    end_pair(1)
+    for each in spread_attn:
+        each.wait_recv()
 
     @pl.when(c == y)
     def _():
         core_attn.start()
-        a_out[...] = ab2[...]
+        a_out[...] = ab[...]
         core_attn.wait_send()
 
-    x_pair_back.wait_recv()
-    p_out[1 - m, :, mine] = px[...]
-    core_pair_back.start()
+    end_sum(4)
 
     @pl.when(c != y)
     def _():
@@ -784,19 +845,16 @@
         swap_in.wait()
 
     back_out.wait()
-    for each in (core_down, core_pair, core_pair_back):
+    for each in core_down + core_pair + core_pair_back:
         each.wait()
-    core_branch.wait_send()
-    x_down.wait_send()
-    x_pair_back.wait_send()
-    x_attn_back.wait_send()
-    y_attn_back.wait_send()
-    for each in z_down + x_pair + z_pair + x_attn[1:] + z_attn + exchange:
+    for each in [late, core_branch] + z_down + z_down_last + x_down + z_pair + z_pair_last + x_pair_back:
         each.wait_send()
+    for each in [x_pair(k) for k in range(zs)] + x_attn[1:] + z_attn + spread_attn + exchange:
+        each.wait_send()
 
 
 def back_all(
-    hid, pair, g_own, g_oth, x_own, x_oth, gx, hres, x_in, probs, xn_one, out_first, out_oth,
+    hid, pair, g_own, g_oth, x_own, x_oth, gx, hres, x_in, probs, xn_one, out_first, out_oth, late,
     out_w, qkv_w, qkv, mixed, gain_two, gain_one, scale_two, scale_one, zs,
 ):
     width, half_len = g_own.shape
@@ -813,7 +871,7 @@
     spread = lambda gain: jnp.broadcast_to(gain, (width, 128))
     return pl.pallas_call(
         back_kernel,
-        in_specs=[hbm] * 13 + [vmem] * 8,
+        in_specs=[hbm] * 14 + [vmem] * 8,
         out_specs=[hbm] * 3 + [vmem] * 5,
         out_shape=[
             sds(low, width, half_len),
@@ -837,19 +895,19 @@
             b16(zs, a_len, a_cols),
             b16(zs, a_len // 2, a_cols),
             b16(zs - 1, a_len // 2, a_cols),
-            b16(a_len, a_cols),
             b16(a_len, 2 * a_cols),
+            b16(width, half_len // 2),
             pltpu.VMEM((5, 16, width), wide),
             pltpu.VMEM((5, 16, width), wide),
-            pltpu.SemaphoreType.DMA((42,)),
-            pltpu.SemaphoreType.DMA((42,)),
+            pltpu.SemaphoreType.DMA((60,)),
+            pltpu.SemaphoreType.DMA((60,)),
             pltpu.SemaphoreType.DMA((14,)),
         ],
         compiler_params=pltpu.CompilerParams(vmem_limit_bytes=61 << 20, collective_id=1, has_side_effects=True),
         cost_estimate=hint,
         name="back_all",
     )(
-        hid, pair, g_own, g_oth, x_own, x_oth, gx, hres, x_in, probs, xn_one, out_first, out_oth,
+        hid, pair, g_own, g_oth, x_own, x_oth, gx, hres, x_in, probs, xn_one, out_first, out_oth, late,
         out_w, qkv_w.T, qkv, mixed, spread(gain_two), spread(gain_one), scale_two, scale_one,
     )
 
@@ -1022,13 +1080,13 @@
 
     normed, scale_two = norm_of(hres, gain_two)
     xn_own = normed.astype(low)
-    hid, pair, xn_oth, out_own, out_oth, gx = ffn(
+    hid, pair, xn_oth, out_own, out_oth, gx, late = ffn(
         xn_own, g_own, g_oth, gate_weight, up_weight, down_weight.T
     )
     if moves.nx == 2 and moves.nz == 4:
         out_first = (hres + out_own).astype(low)
         got_first, got_oth, got_in, sum_d, sum_p, sums, grad_in, small = back_all(
-            hid, pair, g_own, g_oth, xn_own, xn_oth, gx, hres, x_in, probs, xn_one, out_first, out_oth,
+            hid, pair, g_own, g_oth, xn_own, xn_oth, gx, hres, x_in, probs, xn_one, out_first, out_oth, late,
             out_w, qkv_w, qkv, mixed, gain_two, gain_one, scale_two, scale_one, moves.nz,
         )
         out_y = jnp.where(c == y, out_first, got_first).astype(wide) + got_oth.astype(wide)
@@ -1052,6 +1110,7 @@
             sum_d.astype(wide).T,
         )
     grad_gate, grad_up = pair[0], pair[1]
+    gx = gx.at[:, half_len // 2 :].add(moves.over_y(late).astype(wide))
 
     columns = hid.shape[1] // 2
     send_d = weight_grad(g_own, g_oth, hid, 1 - c)

time: 358 us -> 329 us (0.919)
  Pallas kernels: 250 us -> 221 us
    pallas_call x1, Pallas kernels: 161 us -> 138 us  [back_all(): pl.pallas_call(back_kernel, in_specs=[hbm] * 14 + [vmem] * 8, out_specs=[...]
    pallas_call x1, Pallas kernels: 74.8 us -> 68.9 us  [ffn(): pl.pallas_call(ffn_kernel, grid=(4, hidden // tile), in_specs=[full, full...]
    unnamed x54 -> x52, local copies, waits for them, and re-layouts: 11 us -> 9.98 us
  transfers between devices with their start and end apart: 8 -> 8, of which waited for: 1 -> 1; matrix products, arithmetic and copies ran while one was open for 11% -> 12% of each run, Pallas kernels for 4% -> 4%
where the time goes in v4:
time: 329 us; the launch traced here: 324 us
  Pallas kernels  221 us (67%)
  other arithmetic  36 us (11%)
  starting transfers between devices  26.9 us (8%)
  local copies, waits for them, and re-layouts  22.6 us (7%)
  waiting for transfers between devices  9.02 us (3%)
  matrix products  5.94 us (2%)
    pallas_call x1, Pallas kernels, back_all(): pl.pallas_call(back_kernel, in_specs=[hbm] * 14 + [vmem] * 8, out_specs=[...  138 us
    pallas_call x1, Pallas kernels, ffn(): pl.pallas_call(ffn_kernel, grid=(4, hidden // tile), in_specs=[full, full...  68.9 us
    ppermute x2, starting transfers between devices, core(): return lax.ppermute(a, 'seq', [(s, s ^ 1) for s in range(2 * self.nx)])  17.2 us
    pallas_call x1, Pallas kernels, attn_forward(): pl.pallas_call(functools.partial(attn_fwd_kernel, length), grid=(blocks,...  14.5 us
    unnamed x52, local copies, waits for them, and re-layouts  9.98 us
    ppermute x1, waiting for transfers between devices, second(): return lax.ppermute(a, ('seq', 'tensor'), self.second_pairs)  9.01 us
    ppermute x5, starting transfers between devices, swap(): got = lax.ppermute(a, ('seq', 'tensor'), self.swap_pairs)  8.06 us
  transfers between devices with their start and end apart: 8, of which 1 were waited for; matrix products, arithmetic and copies ran while one was open for 12% of the time, Pallas kernels for 4%

profile of v4, /device:TPU:0, one launch (start us, length us, event | category | flops | bytes accessed | tf_op | source)
XLA Modules:
  0.0 323.6 jit_solution(4786813873679721582)
XLA Ops:
  0.7 1.9 collective-permute-start
  9.4 1.9 pad_maximum_fusion
  11.2 2.5 copy.56
  13.7 2.0 collective-permute-start.3
  15.7 2.6 fusion.5
  22.0 6.7 %collective-permute-start.4 = (bf16[1472,512]{1,0:T(8,128)(2,1)}, bf16[1472,512]{1,0:T(8,128)(2,1)}, u32[]{:S(2)}, u32[]{:S(2)}) collective-permute-start(bf16[1472,512]{1,0:T(8,128)(2,1)} %fusion.3), channel_id=1, source_target_pairs={{0,2},{2,0},{4,6},{6,4},{1,3},{3,1},{5,7},{7,5},{8,10},{10,8},{12,... | collective-permute-start | bytes 4521992 | tf_op jit(solution)/shard_map/ppermute | solution.py:954
  31.0 1.9 collective-permute-start.6
  34.3 3.9 %copy.57 = bf16[576,1472]{0,1:T(8,128)(2,1)} copy(bf16[576,1472]{1,0:T(8,128)(2,1)} %collective-permute-done.3) | data formatting | bytes 3391488 | tf_op jit(solution)/shard_map/ppermute | solution.py:944
  39.4 3.9 %maximum_select_fusion.xn1_h = bf16[1472,1024]{1,0:T(8,128)(2,1)S(1)} fusion(bf16[1472,512]{1,0:T(8,128)(2,1)} %collective-permute-done.4, bf16[1472,512]{1,0:T(8,128)(2,1)} %fusion.3, pred[]{:T(512)S(6)} %eq.7), kind=kLoop, calls=%fused_computation.7 | loop fusion | flops 13565952 | bytes 6029313 | tf_op jit(solution)/shard_map/jit(_where)/select_n | solution.py:1063
  43.4 2.0 convolution_convert_fusion.1.q_ref.k_ref.v_ref.qkv
  45.7 14.5 %attn_forward.1 = (bf16[3,1024,1024]{2,1,0:T(8,128)(2,1)}, bf16[192,1024]{1,0:T(8,128)(2,1)S(1)}) custom-call(f32[32,3]{1,0:T(8,128)S(1)} %reshape.125.bias_ref, bf16[576,1024]{1,0:T(8,128)(2,1)S(1)} %convolution_convert_fusion.1.q_ref.k_ref.v_ref.qkv, bf16[576,1024]{1,0:T(8,128)(2,1)S(1)} %convolution_convert_fusion.1.q_ref.k_ref.v_ref.qkv, ...), custom_call_target="tpu_custom_call" | custom-call | flops 1000 | bytes 1000 | tf_op jit(solution)/shard_map/attn_forward/pallas_call | solution.py:71
  60.2 1.7 convolution_convert_fusion
  61.9 10.6 %collective-permute-start.5 = (bf16[1472,512]{1,0:T(8,128)(2,1)}, bf16[1472,512]{1,0:T(8,128)(2,1)}, u32[]{:S(2)}, u32[]{:S(2)}) collective-permute-start(bf16[1472,512]{1,0:T(8,128)(2,1)} %convolution_convert_fusion), channel_id=1, source_target_pairs={{0,2},{2,0},{4,6},{6,4},{1,3},{3,1},{5,7},{7,5},{8,10},{10,8},{12,... | collective-permute-start | bytes 4521992 | tf_op jit(solution)/shard_map/ppermute | solution.py:954
  74.2 3.2 fusion.6.w_t
  78.7 2.2 multiply_reduce_fusion
  81.0 1.7 multiply_convert_fusion.x_ref.xo_h
  82.7 9.0 %collective-permute-done.7.gr_ref.gr_h = bf16[1472,512]{1,0:T(8,128)(2,1)} collective-permute-done((bf16[1472,512]{1,0:T(8,128)(2,1)}, bf16[1472,512]{1,0:T(8,128)(2,1)}, u32[]{:S(2)}, u32[]{:S(2)}) %collective-permute-start.7) | collective-permute-done | bytes 1507360 | tf_op jit(solution)/shard_map/ppermute | solution.py:948
  91.7 68.9 %ffn_both_ways.1 = (bf16[1024,1792]{1,0:T(8,128)(2,1)}, bf16[2,1024,1792]{2,1,0:T(8,128)(2,1)}, bf16[1472,512]{1,0:T(8,128)(2,1)}, f32[1472,512]{1,0:T(8,128)}, ...) custom-call(bf16[1472,512]{1,0:T(8,128)(2,1)} %multiply_convert_fusion.x_ref.xo_h, ...), custom_call_target="tpu_custom_call" | custom-call | flops 1000 | bytes 1000 | tf_op jit(solution)/shard_map/ffn_both_ways/pallas_call | solution.py:290
  160.6 3.5 %add_convert_fusion.1.outp_h = bf16[1472,512]{1,0:T(8,128)(2,1)} fusion(f32[1472,512]{1,0:T(8,128)S(1)} %get-tuple-element.111.hres_h, f32[1472,512]{1,0:T(8,128)} %get-tuple-element.38), kind=kLoop, calls=%fused_computation.10 | loop fusion | flops 1507328 | bytes 7536640 | tf_op jit(solution)/shard_map/convert_element_type | solution.py:1087
  166.3 137.6 %back_all.1 = (bf16[1472,512]{1,0:T(8,128)(2,1)}, bf16[1472,512]{1,0:T(8,128)(2,1)}, bf16[1472,512]{1,0:T(8,128)(2,1)}, bf16[368,1792]{1,0:T(8,128)(2,1)}, bf16[...) custom-call(bf16[1024,1792]{1,0:T(8,128)(2,1)} %get-tuple-element.39.hid_h,, ...), custom_call_target="tpu_custom_call" | custom-call | flops 1000 | bytes 1000 | tf_op jit(solution)/shard_map/back_all/pallas_call | solution.py:872
  311.6 3.1 convert_bitcast_fusion.1
  314.8 3.1 bitcast_convert_fusion
  319.0 1.8 fusion.4
  321.3 1.8 convert_bitcast_fusion
  (91 shorter events, 29.6 us)
Async XLA Ops:
  0.6 7.6 %copy-start.17 = (bf16[1472,192]{0,1:T(8,128)(2,1)S(1)}, bf16[1472,192]{0,1:T(8,128)(2,1)}, u32[]{:S(2)}) copy-start(bf16[1472,192]{0,1:T(8,128)(2,1)} %param.21) | copy-start | bytes 1695748
  0.7 17.8 %collective-permute-start = (bf16[1472,512]{1,0:T(8,128)(2,1)}, bf16[1472,512]{1,0:T(8,128)(2,1)}, u32[]{:S(2)}, u32[]{:S(2)}) collective-permute-start(bf16[1472,512]{1,0:T(8,128)(2,1)} %bitcast.55), channel_id=1, source_target_pairs={{1,2},{2,1},{5,6},{6,5},{9,10},{10,9},{13,14},{14,13},{17,18},{18,... | collective-permute-start | bytes 4521992 | tf_op jit(solution)/shard_map/ppermute | solution.py:944
  4.9 13.5 %collective-permute-start.1 = (f32[101]{0:T(128)S(1)}, f32[101]{0:T(128)S(1)}, u32[]{:S(2)}, u32[]{:S(2)}) collective-permute-start(f32[101]{0:T(128)S(1)} %pad_maximum_fusion.1), channel_id=1, source_target_pairs={{1,2},{2,1},{5,6},{6,5},{9,10},{10,9},{13,14},{14,13},{17,18},{18,... | collective-permute-start | bytes 1220 | tf_op jit(solution)/shard_map/ppermute | solution.py:944
  11.2 7.1 %copy-start.9 = (bf16[576,1472]{0,1:T(8,128)(2,1)}, bf16[576,1472]{0,1:T(8,128)(2,1)S(1)}, u32[]{:S(2)}) copy-start(bf16[576,1472]{0,1:T(8,128)(2,1)S(1)} %pad_maximum_fusion) | copy-start | bytes 5087236
  13.7 4.7 %copy-start.20 = (bf16[1472]{0:T(1024)(128)(2,1)S(1)}, bf16[1472]{0:T(1024)(128)(2,1)}, u32[]{:S(2)}) copy-start(bf16[1472]{0:T(1024)(128)(2,1)} %param.18) | copy-start | bytes 8836
  13.7 20.6 %collective-permute-start.3 = (bf16[576,1472]{1,0:T(8,128)(2,1)}, bf16[576,1472]{1,0:T(8,128)(2,1)}, u32[]{:S(2)}, u32[]{:S(2)}) collective-permute-start(bf16[576,1472]{1,0:T(8,128)(2,1)} %copy.56), channel_id=1, source_target_pairs={{1,2},{2,1},{5,6},{6,5},{9,10},{10,9},{13,14},{14,13},{17,18},{18,... | collective-permute-start | bytes 5087240 | tf_op jit(solution)/shard_map/ppermute | solution.py:944
  20.0 58.7 %copy-start.3 = (bf16[1472,512]{1,0:T(8,128)(2,1)}, bf16[1472,512]{1,0:T(8,128)(2,1)S(1)}, u32[]{:S(2)}) copy-start(bf16[1472,512]{1,0:T(8,128)(2,1)S(1)} %broadcast_select_fusion.2.xin_h) | copy-start | bytes 4521988
  20.4 17.8 %copy-start.18 = (f32[512]{0:T(512)}, f32[512]{0:T(512)S(1)}, u32[]{:S(2)}) copy-start(f32[512]{0:T(512)S(1)} %add_rsqrt_fusion.1) | copy-start | bytes 6148
  22.0 17.4 %collective-permute-start.4 = (bf16[1472,512]{1,0:T(8,128)(2,1)}, bf16[1472,512]{1,0:T(8,128)(2,1)}, u32[]{:S(2)}, u32[]{:S(2)}) collective-permute-start(bf16[1472,512]{1,0:T(8,128)(2,1)} %fusion.3), channel_id=1, source_target_pairs={{0,2},{2,0},{4,6},{6,4},{1,3},{3,1},{5,7},{7,5},{8,10},{10,8},{12,... | collective-permute-start | bytes 4521992 | tf_op jit(solution)/shard_map/ppermute | solution.py:954
  28.8 9.4 %collective-permute-start.2 = (bf16[192,1472]{1,0:T(8,128)(2,1)}, bf16[192,1472]{1,0:T(8,128)(2,1)}, u32[]{:S(2)}, u32[]{:S(2)}) collective-permute-start(bf16[192,1472]{1,0:T(8,128)(2,1)} %param.23), channel_id=1, source_target_pairs={{1,2},{2,1},{5,6},{6,5},{9,10},{10,9},{13,14},{14,13},{17,18},{18,... | collective-permute-start | bytes 1695752 | tf_op jit(solution)/shard_map/ppermute | solution.py:944
  31.0 46.4 %collective-permute-start.6 = (bf16[1472,512]{1,0:T(8,128)(2,1)}, bf16[1472,512]{1,0:T(8,128)(2,1)}, u32[]{:S(2)}, u32[]{:S(2)}) collective-permute-start(bf16[1472,512]{1,0:T(8,128)(2,1)} %fusion.5), channel_id=1, source_target_pairs={{1,2},{2,1},{5,6},{6,5},{9,10},{10,9},{13,14},{14,13},{17,18},{18,... | collective-permute-start | bytes 4521992 | tf_op jit(solution)/shard_map/ppermute | solution.py:944
  39.3 20.9 %copy-start.6 = (bf16[192,1472]{1,0:T(8,128)(2,1)}, bf16[192,1472]{1,0:T(8,128)(2,1)S(1)}, u32[]{:S(2)}) copy-start(bf16[192,1472]{1,0:T(8,128)(2,1)S(1)} %broadcast_select_fusion.4.out_w) | copy-start | bytes 1695748
  39.3 4.0 %copy-start.8 = (bf16[576,1472]{0,1:T(8,128)(2,1)S(1)}, bf16[576,1472]{0,1:T(8,128)(2,1)}, u32[]{:S(2)}) copy-start(bf16[576,1472]{0,1:T(8,128)(2,1)} %copy.57) | copy-start | bytes 5087236
  39.4 4.1 %copy-start.10 = (bf16[576,1472]{0,1:T(8,128)(2,1)S(1)}, bf16[576,1472]{0,1:T(8,128)(2,1)}, u32[]{:S(2)}) copy-start(bf16[576,1472]{0,1:T(8,128)(2,1)} %copy-done.9) | copy-start | bytes 5087236
  45.5 14.7 %copy-start = (bf16[576,1024]{1,0:T(8,128)(2,1)}, bf16[576,1024]{1,0:T(8,128)(2,1)S(1)}, u32[]{:S(2)}) copy-start(bf16[576,1024]{1,0:T(8,128)(2,1)S(1)} %convolution_convert_fusion.1.q_ref.k_ref.v_ref.qkv) | copy-start | bytes 3538948
  60.2 18.5 %copy-start.1 = (bf16[192,1024]{1,0:T(8,128)(2,1)}, bf16[192,1024]{1,0:T(8,128)(2,1)S(1)}, u32[]{:S(2)}) copy-start(bf16[192,1024]{1,0:T(8,128)(2,1)S(1)} %get-tuple-element.36.mixed) | copy-start | bytes 1179652
  60.2 12.3 %copy-start.21 = (bf16[1472]{0:T(1024)(128)(2,1)S(1)}, bf16[1472]{0:T(1024)(128)(2,1)}, u32[]{:S(2)}) copy-start(bf16[1472]{0:T(1024)(128)(2,1)} %param.24) | copy-start | bytes 8836
  61.9 16.8 %collective-permute-start.5 = (bf16[1472,512]{1,0:T(8,128)(2,1)}, bf16[1472,512]{1,0:T(8,128)(2,1)}, u32[]{:S(2)}, u32[]{:S(2)}) collective-permute-start(bf16[1472,512]{1,0:T(8,128)(2,1)} %convolution_convert_fusion), channel_id=1, source_target_pairs={{0,2},{2,0},{4,6},{6,4},{1,3},{3,1},{5,7},{7,5},{8,10},{10,8},{12,... | collective-permute-start | bytes 4521992 | tf_op jit(solution)/shard_map/ppermute | solution.py:954
  72.5 4.9 %copy-start.11 = (bf16[1472,512]{1,0:T(8,128)(2,1)S(1)}, bf16[1472,512]{1,0:T(8,128)(2,1)}, u32[]{:S(2)}) copy-start(bf16[1472,512]{1,0:T(8,128)(2,1)} %fusion.5) | copy-start | bytes 4521988
  72.5 19.2 %collective-permute-start.7 = (bf16[1472,512]{1,0:T(8,128)(2,1)}, bf16[1472,512]{1,0:T(8,128)(2,1)}, u32[]{:S(2)}, u32[]{:S(2)}) collective-permute-start(bf16[1472,512]{1,0:T(8,128)(2,1)} %fusion.5), channel_id=1, source_target_pairs={{0,1},{1,3},{2,0},{3,2},{4,5},{5,7},{6,4},{7,6},{8,9},{9,11},{10,8... | collective-permute-start | bytes 4521992 | tf_op jit(solution)/shard_map/ppermute | solution.py:948
  80.9 79.6 %copy-start.2 = (f32[1472,512]{1,0:T(8,128)}, f32[1472,512]{1,0:T(8,128)S(1)}, u32[]{:S(2)}) copy-start(f32[1472,512]{1,0:T(8,128)S(1)} %get-tuple-element.111.hres_h) | copy-start | bytes 9043972
  311.6 3.1 copy-start.12
  314.8 3.1 copy-start.15
  314.8 4.2 %copy-start.16 = (bf16[1472,512]{1,0:T(8,128)(2,1)S(1)}, bf16[1472,512]{1,0:T(8,128)(2,1)}, u32[]{:S(2)}) copy-start(bf16[1472,512]{1,0:T(8,128)(2,1)} %get-tuple-element.47) | copy-start | bytes 4521988
  (6 other events, 12.4 us)

commit v5 on v4

--- a/solution.py
+++ b/solution.py
@@ -26,72 +26,296 @@
     return lax.optimization_barrier((value, *first))[0]
 
 
-def attn_fwd_kernel(length, bias_ref, q_ref, k_ref, v_ref, seg_k_ref, seg_q_ref, p_ref, o_ref, table):
-    block = pl.program_id(0)
-    head = pl.program_id(1)
+def front_kernel(
+    x_h, g_h, wq_h, wk_h, wv_h, wo_h, lengths, valid, bias, gain1_row, gain2_row,
+    x_in, g_in, g_own, w, w_t, xn1, qkv, mixed, probs_h, hres, xn2, scale1, scale2, gain1, gain2,
+    facts_src, facts, p_buf, table, sx, rx, seg_k, seg_q, send_sems, recv_sems, load_sems,
+):
+    s = lax.axis_index("seq")
+    y = lax.axis_index("tensor")
+    c = s % 2
+    m = s // 2
+    width, half_len = x_in.shape
+    length = 2 * half_len
+    heads, buckets = bias.shape
+    inner = mixed.shape[0]
+    dim = inner // heads
+    piece = 64
+    pieces = width // piece
+    lanes = half_len // 128
+    mesh_id = dict(device_id_type=pl.DeviceIdType.MESH)
+    to_core = {"seq": 2 * m + 1 - c}
+    to_swap = {"seq": 2 * m + 1 - c, "tensor": 1 - y}
+
+    def side(i, size):
+        return pl.ds(pl.multiple_of(i * size, 128), size)
+
+    my_half = side(c, half_len)
+    other_half = side(1 - c, half_len)
+
+    def move(k, src, dst, who):
+        return pltpu.make_async_remote_copy(
+            src_ref=src, dst_ref=dst, send_sem=send_sems.at[k], recv_sem=recv_sems.at[k], device_id=who, **mesh_id
+        )
+
+    named = [(x_h, x_in)] + [
+        (src, w.at[pl.ds(i * inner, inner)]) for i, src in enumerate((wq_h, wk_h, wv_h, wo_h))
+    ]
+    moves = [move(1 + i, src, dst, to_swap) for i, (src, dst) in enumerate(named)]
+    loads = [pltpu.make_async_copy(src, dst, load_sems.at[1 + i]) for i, (src, dst) in enumerate(named)]
+    move_facts = move(0, facts_src, facts, to_swap)
+    move_g = move(6, g_in, g_own, to_swap)
+    load_g = pltpu.make_async_copy(g_h, g_in, load_sems.at[0])
+    keep_g = pltpu.make_async_copy(g_in, g_own, load_sems.at[6])
+    core_one = move(7, xn1.at[:, my_half], xn1.at[:, my_half], to_core)
+    core_two = move(8, sx, rx, to_core)
+
+    load_g.start()
+    for h in range(heads):
+        for b in range(buckets):
+            at = h * buckets + b
+            facts_src[at : at + 1, :] = jnp.full((1, 128), bias[h, b], wide)
+    end = jnp.int32(0)
+    at = heads * buckets
+    for i in range(4):
+        end = end + lengths[0, i]
+        facts_src[at + i : at + i + 1, :] = jnp.full((1, 128), end.astype(wide), wide)
+    facts_src[at + 4 : at + 5, :] = jnp.full((1, 128), valid[0].astype(wide), wide)
+
+    barrier = pltpu.get_barrier_semaphore()
+    for who in (to_core, to_swap):
+        pl.semaphore_signal(barrier, inc=1, device_id=who, **mesh_id)
+    pl.semaphore_wait(barrier, 2)
+
+    @pl.when(c != y)
+    def _():
+        move_facts.start()
+        for each in moves:
+            each.start()
+
+    @pl.when(c == y)
+    def _():
+        for each in loads:
+            each.start()
+        facts[...] = facts_src[...]
+
+    load_g.wait()
+    live = lax.broadcasted_iota(jnp.int32, (piece, half_len), 1) + y * half_len < valid[0]
+
+    def mask(i, carry):
+        at = pl.ds(pl.multiple_of(i * piece, piece), piece)
+        g_in[at, :] = jnp.where(live, g_in[at, :].astype(wide), 0.0).astype(low)
+        return carry
+
+    lax.fori_loop(0, pieces, mask, 0)
+
+    @pl.when(c != y)
+    def _():
+        move_g.start()
+
+    @pl.when(c == y)
+    def _():
+        keep_g.start()
+
+    gain1[...] = jnp.broadcast_to(gain1_row[...].astype(wide), (128, width)).T
+    gain2[...] = jnp.broadcast_to(gain2_row[...].astype(wide), (128, width)).T
+
+    @pl.when(c != y)
+    def _():
+        move_facts.wait_recv()
+
+    at = heads * buckets
+
+    def segments(positions):
+        count = jnp.zeros(positions.shape, wide)
+        for i in range(4):
+            count = count + jnp.where(positions >= facts[at + i : at + i + 1, :], 1.0, 0.0)
+        return jnp.where(positions < facts[at + 4 : at + 5, :], count, 4.0)
+
+    seg_k[...] = segments(lax.broadcasted_iota(jnp.int32, (length, 128), 0).astype(wide))
+    for i in range(length // 128):
+        positions = (lax.broadcasted_iota(jnp.int32, (8, 128), 1) + i * 128).astype(wide)
+        seg_q[:, i * 128 : (i + 1) * 128] = segments(positions)
     reach = length - q_block
-
-    @pl.when(block == 0)
+    near_rows = q_block + 2 * band_half
+    d = (
+        lax.broadcasted_iota(jnp.int32, (near_rows, 128), 0)
+        - lax.broadcasted_iota(jnp.int32, (near_rows, 128), 1)
+        - band_half
+    )
+    far_rows = reach - band_half
+    for h in range(heads):
+
+        def value(b, h=h):
+            return facts[h * buckets + b : h * buckets + b + 1, :]
+
+        for i in range(q_block // 128):
+            offset = d - i * 128
+            n = jnp.abs(offset)
+            before = jnp.broadcast_to(value(0), n.shape)
+            later = jnp.broadcast_to(value(16), n.shape)
+            for number, step in enumerate(steps_at):
+                reached = n >= step
+                before = jnp.where(reached, value(number + 1), before)
+                later = jnp.where(reached, value(number + 17), later)
+            col = pl.ds(i * 128, 128)
+            table[h, pl.ds(far_rows, near_rows), col] = jnp.where(offset > 0, later, before)
+            table[h, pl.ds(0, far_rows), col] = jnp.broadcast_to(value(15), (far_rows, 128))
+            table[h, pl.ds(far_rows + near_rows, far_rows), col] = jnp.broadcast_to(value(31), (far_rows, 128))
+
+    def spread(a):
+        return jnp.concatenate([a] * lanes, axis=1)
+
+    def norm(read, gain, scale, write):
+        def first(i, total):
+            v = read(pl.ds(pl.multiple_of(i * piece, piece), piece))
+            return total + jnp.sum(v * v, axis=0, keepdims=True)
+
+        total = lax.fori_loop(0, pieces, first, jnp.zeros((1, half_len), wide))
+        scale[...] = lax.rsqrt(total * (1.0 / width) + eps_norm)
+
+        def second(i, carry):
+            at = pl.ds(pl.multiple_of(i * piece, piece), piece)
+            write(at, (read(at) * scale[...] * spread(gain[at, :])).astype(low))
+            return carry
+
+        lax.fori_loop(0, pieces, second, 0)
+
+    def arrived(i):
+        @pl.when(c != y)
+        def _():
+            moves[i].wait_recv()
+
+        @pl.when(c == y)
+        def _():
+            loads[i].wait()
+
+    arrived(0)
+
+    def write_one(at, value):
+        xn1[at, my_half] = value
+
+    norm(lambda at: x_in[at, :].astype(wide), gain1, scale1, write_one)
+    core_one.start()
+    for i in range(1, 4):
+        arrived(i)
+    core_one.wait_recv()
+    for i in range(3):
+        qkv[i * inner : (i + 1) * inner, :] = dot(w[i * inner : (i + 1) * inner, :], xn1[...], 1, 0).astype(low)
+
+    blocks = length // q_block
+
+    def store(i):
+        h, b = i // blocks, i % blocks
+        return pltpu.make_async_copy(p_buf.at[i % 2], probs_h.at[h, :, side(b, q_block)], load_sems.at[7 + i % 2])
+
+    def block(i, carry):
+        h, b = i // blocks, i % blocks
+        at = side(b, q_block)
+        rows = lambda part: pl.ds(pl.multiple_of((part * heads + h) * dim, dim), dim)
+        first = pl.multiple_of(reach - b * q_block, q_block)
+        scores = dot(qkv[rows(1), :], qkv[rows(0), at], 0, 0) + table[h, pl.ds(first, length), :]
+        keys = jnp.concatenate([seg_k[...]] * (q_block // 128), axis=1)
+        scores = jnp.where(keys == seg_q[0:1, at], scores, masked_score)
+        raised = jnp.exp(scores - jnp.max(scores, axis=0, keepdims=True))
+        probs = (raised * (1.0 / jnp.sum(raised, axis=0, keepdims=True))).astype(low)
+
+        @pl.when(i >= 2)
+        def _():
+            store(i - 2).wait()
+
+        p_buf[i % 2] = probs
+        store(i).start()
+        mixed[rows(0), at] = dot(qkv[rows(2), :], probs, 1, 0).astype(low)
+        return carry
+
+    lax.fori_loop(0, heads * blocks, block, 0)
+
+    arrived(4)
+    out_w = w[3 * inner :, :]
+    sx[...] = dot(out_w, mixed[:, other_half], 0, 0).astype(low)
+    core_two.start()
+    hres[...] = dot(out_w, mixed[:, my_half], 0, 0)
+    w_t[...] = w[: 3 * inner, :].T
+    core_two.wait_recv()
+
+    def add(i, carry):
+        at = pl.ds(pl.multiple_of(i * piece, piece), piece)
+        hres[at, :] += x_in[at, :].astype(wide) + rx[at, :].astype(wide)
+        return carry
+
+    lax.fori_loop(0, pieces, add, 0)
+
+    def write_two(at, value):
+        xn2[at, :] = value
+
+    norm(lambda at: hres[at, :], gain2, scale2, write_two)
+    last = heads * blocks
+    store(last - 2).wait()
+    store(last - 1).wait()
+    core_one.wait_send()
+    core_two.wait_send()
+
+    @pl.when(c != y)
     def _():
-        table[head, : reach - band_half, :] = jnp.full((reach - band_half, q_block), bias_ref[15, head], wide)
-        tail = length + reach - (reach + q_block + band_half)
-        table[head, reach + q_block + band_half :, :] = jnp.full((tail, q_block), bias_ref[31, head], wide)
-        rows = q_block + 2 * band_half
-        d = (
-            lax.broadcasted_iota(jnp.int32, (rows, q_block), 0)
-            - lax.broadcasted_iota(jnp.int32, (rows, q_block), 1)
-            - band_half
-        )
-        n = jnp.abs(d)
-        before = jnp.full((rows, q_block), bias_ref[0, head], wide)
-        after = jnp.full((rows, q_block), bias_ref[16, head], wide)
-        for number, step in enumerate(steps_at):
-            reached = n >= step
-            before = jnp.where(reached, bias_ref[number + 1, head], before)
-            after = jnp.where(reached, bias_ref[number + 17, head], after)
-        table[head, reach - band_half : reach + q_block + band_half, :] = jnp.where(d > 0, after, before)
-
-    first = pl.multiple_of(reach - block * q_block, q_block)
-    scores = dot(k_ref[...], q_ref[...], 0, 0) + table[head, pl.ds(first, length), :]
-    seg_k = jnp.concatenate([seg_k_ref[...]] * (q_block // 128), axis=1)
-    scores = jnp.where(seg_k == seg_q_ref[...], scores, masked_score)
-    raised = jnp.exp(scores - jnp.max(scores, axis=0, keepdims=True))
-    probs = (raised * (1.0 / jnp.sum(raised, axis=0, keepdims=True))).astype(low)
-    p_ref[0] = probs
-    o_ref[...] = dot(v_ref[...], probs, 1, 0).astype(low)
-
-
-def attn_forward(qkv, seg, bias):
-    width, length = qkv.shape
-    heads = bias.shape[1]
-    dim = width // (3 * heads)
-    seg_k = jnp.broadcast_to(seg[:, None], (length, 128))
-    seg_q = seg[None, :]
-    blocks = length // q_block
+        move_facts.wait_send()
+        for each in moves:
+            each.wait_send()
+        move_g.wait()
+
+    @pl.when(c == y)
+    def _():
+        keep_g.wait()
+
+
+def front(x, g, weights, lengths, valid, bias, gain_one, gain_two):
+    width, half_len = x.shape
+    length = 2 * half_len
+    heads = bias.shape[0]
+    inner = weights[0].shape[0]
+    hbm = pl.BlockSpec(memory_space=pl.ANY)
+    vmem = pl.BlockSpec(memory_space=pltpu.VMEM)
+    smem = pl.BlockSpec(memory_space=pltpu.SMEM)
+    sds = lambda kind, *shape: jax.ShapeDtypeStruct(shape, kind)
+    facts = pltpu.VMEM((heads * bias.shape[1] + 8, 128), wide)
     return pl.pallas_call(
-        functools.partial(attn_fwd_kernel, length),
-        grid=(blocks, heads),
-        in_specs=[
-            pl.BlockSpec(memory_space=pltpu.SMEM),
-            pl.BlockSpec((dim, q_block), lambda b, h: (h, b)),
-            pl.BlockSpec((dim, length), lambda b, h: (heads + h, 0)),
-            pl.BlockSpec((dim, length), lambda b, h: (2 * heads + h, 0)),
-            pl.BlockSpec((length, 128), lambda b, h: (0, 0)),
-            pl.BlockSpec((1, q_block), lambda b, h: (0, b)),
+        front_kernel,
+        in_specs=[hbm] * 6 + [smem] * 3 + [vmem] * 2,
+        out_specs=[vmem, vmem, hbm, vmem, vmem, vmem, vmem, vmem, hbm] + [vmem] * 6,
+        out_shape=[
+            sds(low, width, half_len),
+            sds(low, width, half_len),
+            sds(low, width, half_len),
+            sds(low, 4 * inner, width),
+            sds(low, width, 3 * inner),
+            sds(low, width, length),
+            sds(low, 3 * inner, length),
+            sds(low, inner, length),
+            sds(low, heads, length, length),
+            sds(wide, width, half_len),
+            sds(low, width, half_len),
+            sds(wide, 1, half_len),
+            sds(wide, 1, half_len),
+            sds(wide, width, 128),
+            sds(wide, width, 128),
         ],
-        out_specs=[
-            pl.BlockSpec((1, length, q_block), lambda b, h: (h, 0, b)),
-            pl.BlockSpec((dim, q_block), lambda b, h: (h, b)),
+        scratch_shapes=[
+            facts,
+            facts,
+            pltpu.VMEM((2, length, q_block), low),
+            pltpu.VMEM((heads, 2 * length - q_block, q_block), wide),
+            pltpu.VMEM((width, half_len), low),
+            pltpu.VMEM((width, half_len), low),
+            pltpu.VMEM((length, 128), wide),
+            pltpu.VMEM((8, length), wide),
+            pltpu.SemaphoreType.DMA((9,)),
+            pltpu.SemaphoreType.DMA((9,)),
+            pltpu.SemaphoreType.DMA((9,)),
         ],
-        out_shape=[
-            jax.ShapeDtypeStruct((heads, length, length), low),
-            jax.ShapeDtypeStruct((heads * dim, length), low),
-        ],
-        scratch_shapes=[pltpu.VMEM((heads, 2 * length - q_block, q_block), wide)],
-        compiler_params=pltpu.CompilerParams(vmem_limit_bytes=48 << 20),
+        compiler_params=pltpu.CompilerParams(vmem_limit_bytes=60 << 20, collective_id=2, has_side_effects=True),
         cost_estimate=hint,
-        name="attn_forward",
-    )(bias, qkv, qkv, qkv, seg_k, seg_q)
+        name="front_all",
+    )(x, g, *weights, lengths, valid, bias, gain_one, gain_two)
 
 
 def attn_bwd_kernel(length, q_ref, k_ref, v_ref, go_ref, o_ref, p_ref, gq_ref, gk_ref, gv_ref, gb_ref, k_acc, v_acc, sums):
@@ -180,26 +404,34 @@
 
 
 def ffn_kernel(
-    x_ref, go_ref, gr_ref, gate_w, up_w, down_w,
-    hid_ref, pair_ref, xr_ref, out_ref, out_r_ref, gx_ref, late_ref,
-    xs, gs, out_acc, gx_acc, x_in, gx_out, gx_in, sems,
+    x_ref, go_ref, hres_ref, g_h, gate_w, up_w, down_w,
+    hid_ref, pair_ref, xr_ref, gr_ref, out_ref, out_r_ref, gx_ref, late_ref,
+    xs, gs, out_acc, gx_acc, x_in, g_in, sems,
 ):
     chunk = pl.program_id(0)
     tile = pl.program_id(1)
     size = xs.shape[0]
-    there = {"tensor": 1 - lax.axis_index("tensor")}
+    s = lax.axis_index("seq")
+    y = lax.axis_index("tensor")
+    c = s % 2
+    first = s - c
+    mesh_id = dict(device_id_type=pl.DeviceIdType.MESH)
+    to_y = {"tensor": 1 - y}
+    to_core = {"seq": first + 1 - c}
+    to_second = {"seq": first + y, "tensor": 1 - c}
     half = [pl.ds(0, size), pl.ds(size, size)]
 
     def send_x(h):
         return pltpu.make_async_remote_copy(
             src_ref=x_ref.at[:, half[h]], dst_ref=x_in.at[h], send_sem=sems.at[h], recv_sem=sems.at[2 + h],
-            device_id=there, device_id_type=pl.DeviceIdType.MESH,
+            device_id=to_y, **mesh_id,
         )
 
-    send_gx = pltpu.make_async_remote_copy(
-        src_ref=gx_out, dst_ref=gx_in, send_sem=sems.at[4], recv_sem=sems.at[5],
-        device_id=there, device_id_type=pl.DeviceIdType.MESH,
-    )
+    def send_g(h):
+        return pltpu.make_async_remote_copy(
+            src_ref=g_h.at[:, half[h]], dst_ref=g_in.at[h], send_sem=sems.at[4 + h], recv_sem=sems.at[6 + h],
+            device_id=to_second, **mesh_id,
+        )
 
     @pl.when(tile == 0)
     def _():
@@ -209,36 +441,38 @@
     @pl.when((tile == 0) & (chunk == 0))
     def _():
         barrier = pltpu.get_barrier_semaphore()
-        pl.semaphore_signal(barrier, inc=1, device_id=there, device_id_type=pl.DeviceIdType.MESH)
-        pl.semaphore_wait(barrier, 1)
-        send_x(0).start()
-        send_x(1).start()
-        xs[...] = x_ref[:, half[1]].T
-        gs[...] = go_ref[:, half[1]].T
+        for who in (to_y, to_core):
+            pl.semaphore_signal(barrier, inc=1, device_id=who, **mesh_id)
+        pl.semaphore_wait(barrier, 2)
+        for h in range(2):
+            send_x(h).start()
+            send_g(h).start()
 
     for h in range(2):
 
-        @pl.when((tile == 0) & (chunk == 1 + h))
+        @pl.when((tile == 0) & (chunk == h))
+        def _(h=h):
+            xs[...] = x_ref[:, half[h]].T
+            gs[...] = go_ref[:, half[h]].T
+
+        @pl.when((tile == 0) & (chunk == 2 + h))
         def _(h=h):
             send_x(h).wait_recv()
             xs[...] = x_in[h].T
-            gs[...] = gr_ref[:, half[h]].T
             xr_ref[:, half[h]] = x_in[h]
-
-    @pl.when((tile == 0) & (chunk == 3))
-    def _():
-        xs[...] = x_ref[:, half[0]].T
-        gs[...] = go_ref[:, half[0]].T
+            send_g(h).wait_recv()
+            gs[...] = g_in[h].T
+            gr_ref[:, half[h]] = g_in[h]
 
     gate = dot(xs[...], gate_w[...], 1, 0)
     up = dot(xs[...], up_w[...], 1, 0)
     grad = dot(gs[...], down_w[...], 1, 0)
-    c = math.sqrt(2.0 / math.pi)
+    c_gelu = math.sqrt(2.0 / math.pi)
     square = gate * gate
-    t = jnp.tanh(c * gate * (1.0 + 0.044715 * square))
+    t = jnp.tanh(c_gelu * gate * (1.0 + 0.044715 * square))
     part = 0.5 * (1.0 + t)
     gelu = gate * part
-    slope = part + 0.5 * gate * (1.0 - t * t) * (c * (1.0 + 3 * 0.044715 * square))
+    slope = part + 0.5 * gate * (1.0 - t * t) * (c_gelu * (1.0 + 3 * 0.044715 * square))
     hid = (gelu * up).astype(low)
     gg = (grad * up * slope).astype(low)
     gu = (grad * gelu).astype(low)
@@ -249,65 +483,57 @@
     gx_acc[...] += dot(gate_w[...], gg, 1, 1) + dot(up_w[...], gu, 1, 1)
 
     last = tile == pl.num_programs(1) - 1
-    for at, h in ((0, 1), (3, 0)):
-
-        @pl.when(last & (chunk == at))
+    for h in range(2):
+
+        @pl.when(last & (chunk == h))
         def _(h=h):
-            out_ref[:, half[h]] = out_acc[...]
+            out_ref[:, half[h]] = (hres_ref[:, half[h]] + out_acc[...]).astype(low)
             gx_ref[:, half[h]] = gx_acc[...]
 
-    for h in range(2):
-
-        @pl.when(last & (chunk == 1 + h))
+        @pl.when(last & (chunk == 2 + h))
         def _(h=h):
             out_r_ref[:, half[h]] = out_acc[...].astype(low)
-            if h:
-                late_ref[...] = gx_acc[...].astype(low)
-            else:
-                gx_out[...] = gx_acc[...].astype(low)
-                send_gx.start()
+            late_ref[:, half[h]] = gx_acc[...].astype(low)
 
     @pl.when(last & (chunk == 3))
     def _():
-        send_gx.wait_recv()
-        gx_ref[:, half[0]] += gx_in[...].astype(wide)
         for h in range(2):
             send_x(h).wait_send()
-        send_gx.wait_send()
-
-
-def ffn(x, g_own, g_oth, gate_w, up_w, down_w):
+            send_g(h).wait_send()
+
+
+def ffn(x, g_own, hres, g_in, gate_w, up_w, down_w):
     width, tokens = x.shape
     hidden = gate_w.shape[1]
     tile, size = 256, tokens // 2
     full = pl.BlockSpec((width, tokens), lambda s, j: (0, 0), pipeline_mode=pl.Buffered(1))
     weight = pl.BlockSpec((width, tile), lambda s, j: (0, j))
-    act = pl.BlockSpec((size, tile), lambda s, j: ((s + 1) % 4, j))
     act_shape = jax.ShapeDtypeStruct((2 * tokens, hidden), low)
     tokens_of = lambda kind: jax.ShapeDtypeStruct((width, tokens), kind)
-    part = pltpu.VMEM((width, size), low)
-    late = pl.BlockSpec((width, size), lambda s, j: (0, 0), pipeline_mode=pl.Buffered(1))
     return pl.pallas_call(
         ffn_kernel,
         grid=(4, hidden // tile),
-        in_specs=[full, full, full, weight, weight, weight],
-        out_specs=[act, pl.BlockSpec((2, size, tile), lambda s, j: (0, (s + 1) % 4, j)), full, full, full, full, late],
-        out_shape=[act_shape, jax.ShapeDtypeStruct((2, 2 * tokens, hidden), low), tokens_of(low), tokens_of(wide), tokens_of(low), tokens_of(wide)]
-        + [jax.ShapeDtypeStruct((width, size), low)],
+        in_specs=[full, full, full, pl.BlockSpec(memory_space=pl.ANY), weight, weight, weight],
+        out_specs=[
+            pl.BlockSpec((size, tile), lambda s, j: (s, j)),
+            pl.BlockSpec((2, size, tile), lambda s, j: (0, s, j)),
+        ]
+        + [full] * 6,
+        out_shape=[act_shape, jax.ShapeDtypeStruct((2, 2 * tokens, hidden), low)]
+        + [tokens_of(kind) for kind in (low, low, low, low, wide, low)],
         scratch_shapes=[
             pltpu.VMEM((size, width), low),
             pltpu.VMEM((size, width), low),
             pltpu.VMEM((width, size), wide),
             pltpu.VMEM((width, size), wide),
             pltpu.VMEM((2, width, size), low),
-            part,
-            part,
-            pltpu.SemaphoreType.DMA((6,)),
+            pltpu.VMEM((2, width, size), low),
+            pltpu.SemaphoreType.DMA((8,)),
         ],
         compiler_params=pltpu.CompilerParams(vmem_limit_bytes=56 << 20, collective_id=0, has_side_effects=True),
         cost_estimate=hint,
         name="ffn_both_ways",
-    )(x, g_own, g_oth, gate_w, up_w, down_w)
+    )(x, g_own, hres, g_in, gate_w, up_w, down_w)
 
 
 def weight_grad_kernel(core_ref, own_ref, oth_ref, right_ref, *refs):
@@ -638,7 +864,13 @@
         for each in loads[:3]:
             each.wait()
         late.wait_recv()
-        gxv[:, late_in.shape[1] :] += late_in[...].astype(wide)
+
+        def add_late(i, carry):
+            at = pl.ds(pl.multiple_of(i * piece, piece), piece)
+            gxv[at, :] += late_in[at, :].astype(wide)
+            return carry
+
+        lax.fori_loop(0, pieces, add_late, 0)
 
         def store_hres(at, back):
             total = gov[at, :].astype(wide) + back
@@ -855,20 +1087,19 @@
 
 def back_all(
     hid, pair, g_own, g_oth, x_own, x_oth, gx, hres, x_in, probs, xn_one, out_first, out_oth, late,
-    out_w, qkv_w, qkv, mixed, gain_two, gain_one, scale_two, scale_one, zs,
+    out_w, w_t, qkv, mixed, gain_two, gain_one, scale_two, scale_one, zs,
 ):
     width, half_len = g_own.shape
     length = 2 * half_len
     rows = width // zs
     columns = hid.shape[1] // 2
     heads = probs.shape[0]
-    a_cols = 2 * (qkv_w.shape[0] + out_w.shape[0]) // 4
+    a_cols = (w_t.shape[1] + out_w.shape[0]) // 2
     a_len = -(-rows // 32) * 32
     hbm = pl.BlockSpec(memory_space=pl.ANY)
     vmem = pl.BlockSpec(memory_space=pltpu.VMEM)
     sds = lambda kind, *shape: jax.ShapeDtypeStruct(shape, kind)
     b16 = lambda *shape: pltpu.VMEM(shape, low)
-    spread = lambda gain: jnp.broadcast_to(gain, (width, 128))
     return pl.pallas_call(
         back_kernel,
         in_specs=[hbm] * 14 + [vmem] * 8,
@@ -896,7 +1127,7 @@
             b16(zs, a_len // 2, a_cols),
             b16(zs - 1, a_len // 2, a_cols),
             b16(a_len, 2 * a_cols),
-            b16(width, half_len // 2),
+            b16(width, half_len),
             pltpu.VMEM((5, 16, width), wide),
             pltpu.VMEM((5, 16, width), wide),
             pltpu.SemaphoreType.DMA((60,)),
@@ -908,13 +1139,8 @@
         name="back_all",
     )(
         hid, pair, g_own, g_oth, x_own, x_oth, gx, hres, x_in, probs, xn_one, out_first, out_oth, late,
-        out_w, qkv_w.T, qkv, mixed, spread(gain_two), spread(gain_one), scale_two, scale_one,
+        out_w, w_t, qkv, mixed, gain_two, gain_one, scale_two, scale_one,
     )
-
-
-def norm_of(values, gain):
-    scale = lax.rsqrt(jnp.mean(values * values, axis=0, keepdims=True) + eps_norm)
-    return values * scale * gain, scale
 
 
 def norm_back(values, scale, gain, grad):
@@ -944,9 +1170,6 @@
         got = lax.ppermute(a, ("seq", "tensor"), self.swap_pairs)
         return jnp.where(self.c == self.y, a, got)
 
-    def second(self, a):
-        return lax.ppermute(a, ("seq", "tensor"), self.second_pairs)
-
     def back(self, a):
         return lax.ppermute(a, ("seq", "tensor"), self.back_pairs)
 
@@ -1008,13 +1231,6 @@
             a = a + lax.ppermute(a, "dp", [(z, z ^ step) for z in range(self.nz)])
             step *= 2
         return a
-
-
-def segment_ids(lengths, valid, length):
-    ends = jnp.sum(jnp.where(jnp.arange(4)[None, :] <= jnp.arange(4)[:, None], lengths[None, :], 0), axis=1)
-    where_at = jnp.arange(length, dtype=jnp.int32)
-    counted = jnp.sum((where_at[:, None] >= ends[None, :]).astype(jnp.int32), axis=1)
-    return jnp.where(where_at < valid, counted, 4)
 
 
 def local(
@@ -1041,53 +1257,27 @@
     inner_width = query_weight.shape[1]
     y, c, m = moves.y, moves.c, moves.m
 
-    facts = jnp.concatenate([doc_lengths[0].astype(wide), valid_length.astype(wide), position_bias.reshape(-1)])
-    facts = moves.swap(facts)
-    bias = facts[5:].reshape(position_bias.shape)
-    facts = facts[:5].astype(jnp.int32)
-    x_in = moves.swap(layer_in.reshape(half_len, width).T)
-    qkv_w = jnp.concatenate([query_weight.T, key_weight.T, value_weight.T], axis=0)
-    qkv_w = moves.swap(qkv_w)
-    positions = y * half_len + jnp.arange(half_len, dtype=jnp.int32)
-    g_in = jnp.where((positions < valid_length[0])[None, :], out_grad.reshape(half_len, width).T, 0)
-    g_in, out_w, x_in, facts = lax.optimization_barrier((g_in.astype(low), output_weight, x_in, facts))
-    out_w = moves.swap(out_w)
-    g_own = moves.swap(g_in)
-    g_oth = moves.second(g_in)
-    segment = segment_ids(facts[:4], facts[4], length)
-    gain_one = gain_attn.astype(wide)[:, None]
-    gain_two = gain_ffn.astype(wide)[:, None]
-
-    def both_halves(own):
-        other = moves.core(own)
-        return jnp.where(
-            c == 0, jnp.concatenate([own, other], 1), jnp.concatenate([other, own], 1)
-        )
-
-    def my_half(a):
-        return lax.dynamic_slice_in_dim(a, c * half_len, half_len, 1)
-
-    def other_half(a):
-        return lax.dynamic_slice_in_dim(a, (1 - c) * half_len, half_len, 1)
-
-    x_wide = x_in.astype(wide)
-    normed, scale_one = norm_of(x_wide, gain_one)
-    xn_one = both_halves(normed.astype(low))
-    qkv = dot(qkv_w, xn_one, 1, 0).astype(low)
-    probs, mixed = attn_forward(qkv, segment, bias)
-    sent = dot(out_w, other_half(mixed), 0, 0).astype(low)
-    hres = x_wide + dot(out_w, my_half(mixed), 0, 0) + moves.core(sent).astype(wide)
-
-    normed, scale_two = norm_of(hres, gain_two)
-    xn_own = normed.astype(low)
-    hid, pair, xn_oth, out_own, out_oth, gx, late = ffn(
-        xn_own, g_own, g_oth, gate_weight, up_weight, down_weight.T
+    flat = lambda a: a.reshape(half_len, width).T
+    (
+        x_in, g_in, g_own, w, w_t, xn_one, qkv, mixed, probs, hres, xn_own, scale_one, scale_two, gain_one, gain_two
+    ) = front(
+        flat(layer_in),
+        flat(out_grad),
+        (query_weight.T, key_weight.T, value_weight.T, output_weight),
+        doc_lengths,
+        valid_length,
+        position_bias.T,
+        gain_attn[None, :],
+        gain_ffn[None, :],
+    )
+    qkv_w, out_w = w[: 3 * inner_width], w[3 * inner_width :]
+    hid, pair, xn_oth, g_oth, out_first, out_oth, gx, late = ffn(
+        xn_own, g_own, hres, g_in, gate_weight, up_weight, down_weight.T
     )
     if moves.nx == 2 and moves.nz == 4:
-        out_first = (hres + out_own).astype(low)
         got_first, got_oth, got_in, sum_d, sum_p, sums, grad_in, small = back_all(
             hid, pair, g_own, g_oth, xn_own, xn_oth, gx, hres, x_in, probs, xn_one, out_first, out_oth, late,
-            out_w, qkv_w, qkv, mixed, gain_two, gain_one, scale_two, scale_one, moves.nz,
+            out_w, w_t, qkv, mixed, gain_two, gain_one, scale_two, scale_one, moves.nz,
         )
         out_y = jnp.where(c == y, out_first, got_first).astype(wide) + got_oth.astype(wide)
         grad_in = jnp.where(c == y, grad_in, got_in).astype(wide)
@@ -1110,7 +1300,22 @@
             sum_d.astype(wide).T,
         )
     grad_gate, grad_up = pair[0], pair[1]
-    gx = gx.at[:, half_len // 2 :].add(moves.over_y(late).astype(wide))
+    gx = gx + moves.over_y(late).astype(wide)
+    x_wide = x_in.astype(wide)
+    gain_one, gain_two = gain_one[:, :1], gain_two[:, :1]
+
+    def both_halves(own):
+        other = moves.core(own)
+        return jnp.where(
+            c == 0, jnp.concatenate([own, other], 1), jnp.concatenate([other, own], 1)
+        )
+
+    def my_half(a):
+        return lax.dynamic_slice_in_dim(a, c * half_len, half_len, 1)
+
+    def other_half(a):
+        return lax.dynamic_slice_in_dim(a, (1 - c) * half_len, half_len, 1)
+
 
     columns = hid.shape[1] // 2
     send_d = weight_grad(g_own, g_oth, hid, 1 - c)
@@ -1126,7 +1331,7 @@
     x_sent = [moves.start_x(t.reshape(moves.nz, moves.nx, -1, columns)) for t in (total_g, total_u)]
 
     gx = after(gx, total_u)
-    out_y = moves.swap((hres + out_own).astype(low)).astype(wide) + moves.back(out_oth).astype(wide)
+    out_y = moves.swap(out_first).astype(wide) + moves.back(out_oth).astype(wide)
 
     back, grad_gain_two = norm_back(hres, scale_two, gain_two, gx)
     grad_hres = g_own.astype(wide) + back

time: 329 us -> 304 us (0.924); the launches traced: 324 us -> 303 us
  Pallas kernels: 221 us -> 279 us
  starting transfers between devices: 26.9 us -> 0 us
  other arithmetic: 36 us -> 9.95 us
  local copies, waits for them, and re-layouts: 22.6 us -> 12.2 us
  waiting for transfers between devices: 9.02 us -> 0 us
  matrix products: 5.94 us -> 0 us
    pallas_call x1, Pallas kernels: 14.5 us -> 66 us  [front(): pl.pallas_call(front_kernel, in_specs=[hbm] * 6 + [smem] * 3 + [vmem] * 2...]
    ppermute x8 -> x0, starting transfers between devices: 26.9 us -> none  [the longest x2 17.2 us: core(): return lax.ppermute(a, 'seq', [(s, s ^ 1) for s in range(2 * self.nx)])]
    select_n x8 -> x0, other arithmetic: 11.9 us -> none  [the longest x4 4.09 us: swap(): return jnp.where(self.c == self.y, a, got)]
    pallas_call x1, Pallas kernels: 138 us -> 149 us  [back_all(): pl.pallas_call(back_kernel, in_specs=[hbm] * 14 + [vmem] * 8, out_specs=[...]
    ppermute x8 -> x0, waiting for transfers between devices: 9.02 us -> none  [the longest x1 9.01 us: second(): return lax.ppermute(a, ('seq', 'tensor'), self.second_pairs)]
    convert_element_type x7 -> x0, other arithmetic: 7.41 us -> none  [the longest x1 3.5 us: local(): out_first = (hres + out_own).astype(low)]
    dot_general x3 -> x0, matrix products: 5.94 us -> none  [dot(): lax.dot_general(a, b, (((ca,), (cb,)), ((), ())), preferred_element_type=...]
    unnamed x52 -> x18, local copies, waits for them, and re-layouts: 9.98 us -> 4.71 us
  transfers between devices with their start and end apart: 8 -> 0, of which waited for: 1 -> 0; matrix products, arithmetic and copies ran while one was open for 12% -> 0% of each run, Pallas kernels for 4% -> 0%
where the time goes in v5:
time: 304 us; the launch traced here: 303 us
  Pallas kernels  279 us (92%)
  local copies, waits for them, and re-layouts  12.2 us (4%)
  other arithmetic  9.95 us (3%)
    pallas_call x1, Pallas kernels, back_all(): pl.pallas_call(back_kernel, in_specs=[hbm] * 14 + [vmem] * 8, out_specs=[...  149 us
    pallas_call x1, Pallas kernels, front(): pl.pallas_call(front_kernel, in_specs=[hbm] * 6 + [smem] * 3 + [vmem] * 2...  66 us
    pallas_call x1, Pallas kernels, ffn(): pl.pallas_call(ffn_kernel, grid=(4, hidden // tile), in_specs=[full, full...  64.1 us

profile of v5, /device:TPU:0, one launch (start us, length us, event | category | flops | bytes accessed | tf_op | source)
XLA Modules:
  0.0 302.6 jit_solution(16085848986087026696)
XLA Ops:
  0.6 1.3 broadcast_in_dim.6.gain1_row
  1.9 1.3 broadcast_in_dim.7.gain2_row
  3.9 66.0 %front_all.1 = (bf16[1472,512]{1,0:T(8,128)(2,1)}, bf16[1472,512]{1,0:T(8,128)(2,1)}, bf16[1472,512]{1,0:T(8,128)(2,1)}, bf16[768,1472]{1,0:T(8,128)(2,1)}, bf16...) custom-call(bf16[1472,512]{1,0:T(8,128)(2,1)} %bitcast.32, ...), custom_call_target="tpu_custom_call" | custom-call | flops 1000 | bytes 1000 | tf_op jit(solution)/shard_map/front_all/pallas_call | solution.py:281
  69.9 64.1 %ffn_both_ways.1 = (bf16[1024,1792]{1,0:T(8,128)(2,1)}, bf16[2,1024,1792]{2,1,0:T(8,128)(2,1)}, bf16[1472,512]{1,0:T(8,128)(2,1)}, bf16[1472,512]{1,0:T(8,128)(2...) custom-call(bf16[1472,512]{1,0:T(8,128)(2,1)} %get-tuple-element.43., ...), custom_call_target="tpu_custom_call" | custom-call | flops 1000 | bytes 1000 | tf_op jit(solution)/shard_map/ffn_both_ways/pallas_call | solution.py:513
  133.9 1.9 slice.33.out_w
  135.9 149.0 %back_all.1 = (bf16[1472,512]{1,0:T(8,128)(2,1)}, bf16[1472,512]{1,0:T(8,128)(2,1)}, bf16[1472,512]{1,0:T(8,128)(2,1)}, bf16[368,1792]{1,0:T(8,128)(2,1)}, bf16[...) custom-call(bf16[1024,1792]{1,0:T(8,128)(2,1)} %get-tuple-element.48.hid_h,, ...), custom_call_target="tpu_custom_call" | custom-call | flops 1000 | bytes 1000 | tf_op jit(solution)/shard_map/back_all/pallas_call | solution.py:1103
  284.9 0.0 copy-start.3
  284.9 0.0 copy-start.4
  284.9 4.6 %bitcast_convert_fusion = (f32[368,1792]{1,0:T(8,128)}, f32[368,1792]{1,0:T(8,128)}) fusion(bf16[2,368,1792]{2,1,0:T(8,128)(2,1)} %get-tuple-element.72), kind=kLoop, calls=%fused_computation.4 | loop fusion | flops 1318912 | bytes 7913472 | tf_op jit(solution)/shard_map/convert_element_type | solution.py:1299
  289.5 0.0 copy-done.3
  289.5 0.0 copy-done.4
  289.5 1.8 convert_bitcast_fusion
  291.3 0.1 slice_convert_fusion
  291.4 0.3 slice_bitcast_fusion
  291.7 0.9 copy.26
  292.5 0.9 copy.27
  293.4 0.9 copy.28
  294.3 0.9 copy.29
  295.1 1.7 convert_bitcast_fusion.1
  296.8 0.5 copy-done
  297.3 0.8 copy-done.1
  298.1 1.8 fusion
  299.8 1.5 slice_reduce_fusion
  301.3 1.3 slice_bitcast_fusion.1
  (8 shorter events, 0.0 us)
Async XLA Ops:
  284.9 4.6 %copy-start.3 = (bf16[1472,512]{1,0:T(8,128)(2,1)S(1)}, bf16[1472,512]{1,0:T(8,128)(2,1)}, u32[]{:S(2)}) copy-start(bf16[1472,512]{1,0:T(8,128)(2,1)} %get-tuple-element.69) | copy-start | bytes 4521988
  284.9 4.6 %copy-start.4 = (bf16[1472,512]{1,0:T(8,128)(2,1)S(1)}, bf16[1472,512]{1,0:T(8,128)(2,1)}, u32[]{:S(2)}) copy-start(bf16[1472,512]{1,0:T(8,128)(2,1)} %get-tuple-element.68) | copy-start | bytes 4521988
  289.5 1.8 copy-start.6
  291.7 3.5 %copy-start.5 = (bf16[368,1792]{1,0:T(8,128)(2,1)S(1)}, bf16[368,1792]{1,0:T(8,128)(2,1)}, u32[]{:S(2)}) copy-start(bf16[368,1792]{1,0:T(8,128)(2,1)} %get-tuple-element.73) | copy-start | bytes 3956740
  294.3 2.5 copy-start.2
  295.1 2.1 copy-start
  295.1 2.9 copy-start.1

commit v6 on v5

--- a/solution.py
+++ b/solution.py
@@ -27,8 +27,10 @@
 
 
 def front_kernel(
-    x_h, g_h, wq_h, wk_h, wv_h, wo_h, lengths, valid, bias, gain1_row, gain2_row,
-    x_in, g_in, g_own, w, w_t, xn1, qkv, mixed, probs_h, hres, xn2, scale1, scale2, gain1, gain2,
+    share, x_h, g_h, wq_h, wk_h, wv_h, wo_h, lengths, valid, bias, gain1_row, gain2_row,
+    x_out, g_own, g_oth, g_late, wo_out, w_t_out, xn1_out, qkv_out, mixed_out, probs_h, hres_out, xn2,
+    scale1, scale2, gain1, gain2,
+    x_in, g_in, w, w_t, xn1, qkv, mixed, hres,
     facts_src, facts, p_buf, table, sx, rx, seg_k, seg_q, send_sems, recv_sems, load_sems,
 ):
     s = lax.axis_index("seq")
@@ -58,15 +60,47 @@
             src_ref=src, dst_ref=dst, send_sem=send_sems.at[k], recv_sem=recv_sems.at[k], device_id=who, **mesh_id
         )
 
+    to_x = {"seq": 2 * (1 - m) + c}
+    to_second = {"seq": 2 * m + y, "tensor": 1 - c}
+
     named = [(x_h, x_in)] + [
         (src, w.at[pl.ds(i * inner, inner)]) for i, src in enumerate((wq_h, wk_h, wv_h, wo_h))
     ]
-    moves = [move(1 + i, src, dst, to_swap) for i, (src, dst) in enumerate(named)]
+    moves = [move(1, x_h, x_in, to_swap)]
+    passed = []
+    for i, src in enumerate((wq_h, wk_h, wv_h, wo_h)):
+        if share:
+            rows = inner // 2
+            dst = w.at[pl.ds(pl.multiple_of(i * inner + m * rows, rows), rows)]
+            moves.append(move(2 + i, src.at[pl.ds(pl.multiple_of(m * rows, rows), rows)], dst, to_swap))
+            passed.append(move(10 + i, dst, dst, to_x))
+        else:
+            moves.append(move(2 + i, src, w.at[pl.ds(i * inner, inner)], to_swap))
     loads = [pltpu.make_async_copy(src, dst, load_sems.at[1 + i]) for i, (src, dst) in enumerate(named)]
     move_facts = move(0, facts_src, facts, to_swap)
     move_g = move(6, g_in, g_own, to_swap)
+    early = half_len // 2
+    second_g = move(9, g_in.at[:, pl.ds(0, early)], g_oth, to_second)
+    to = lambda k, src, dst: pltpu.make_async_copy(src, dst, load_sems.at[k])
+    keep_late = to(16, g_in.at[:, pl.ds(early, early)], g_late)
     load_g = pltpu.make_async_copy(g_h, g_in, load_sems.at[0])
     keep_g = pltpu.make_async_copy(g_in, g_own, load_sems.at[6])
+    stores = [
+        pltpu.make_async_copy(src, dst, load_sems.at[9 + i])
+        for i, (src, dst) in enumerate(
+            ((x_in, x_out), (w.at[pl.ds(3 * inner, inner)], wo_out), (w_t, w_t_out), (xn1, xn1_out), (qkv, qkv_out),
+             (mixed, mixed_out), (hres, hres_out))
+        )
+    ]
+
+    def pass_on(i):
+        if share:
+
+            @pl.when(c != y)
+            def _():
+                moves[1 + i].wait_recv()
+                passed[i].start()
+
     core_one = move(7, xn1.at[:, my_half], xn1.at[:, my_half], to_core)
     core_two = move(8, sx, rx, to_core)
 
@@ -83,15 +117,16 @@
     facts_src[at + 4 : at + 5, :] = jnp.full((1, 128), valid[0].astype(wide), wide)
 
     barrier = pltpu.get_barrier_semaphore()
-    for who in (to_core, to_swap):
+    greet = [to_core, to_swap, {"tensor": 1 - y}] + ([to_x] if share else [])
+    for who in greet:
         pl.semaphore_signal(barrier, inc=1, device_id=who, **mesh_id)
-    pl.semaphore_wait(barrier, 2)
+    pl.semaphore_wait(barrier, len(greet))
 
     @pl.when(c != y)
     def _():
         move_facts.start()
-        for each in moves:
-            each.start()
+        for i in (1, 2, 3, 0, 4) if share else range(5):
+            moves[i].start()
 
     @pl.when(c == y)
     def _():
@@ -117,8 +152,10 @@
     def _():
         keep_g.start()
 
-    gain1[...] = jnp.broadcast_to(gain1_row[...].astype(wide), (128, width)).T
-    gain2[...] = jnp.broadcast_to(gain2_row[...].astype(wide), (128, width)).T
+    second_g.start()
+    keep_late.start()
+    gain1[...] = jnp.broadcast_to(gain1_row[...].astype(wide)[None, :], (128, width)).T
+    gain2[...] = jnp.broadcast_to(gain2_row[...].astype(wide)[None, :], (128, width)).T
 
     @pl.when(c != y)
     def _():
@@ -184,24 +221,31 @@
     def arrived(i):
         @pl.when(c != y)
         def _():
-            moves[i].wait_recv()
+            (passed[i - 1] if share and i else moves[i]).wait_recv()
 
         @pl.when(c == y)
         def _():
             loads[i].wait()
 
+    for i in range(3):
+        pass_on(i)
     arrived(0)
+    stores[0].start()
 
     def write_one(at, value):
         xn1[at, my_half] = value
 
     norm(lambda at: x_in[at, :].astype(wide), gain1, scale1, write_one)
     core_one.start()
+    pass_on(3)
     for i in range(1, 4):
         arrived(i)
     core_one.wait_recv()
+    stores[3].start()
     for i in range(3):
         qkv[i * inner : (i + 1) * inner, :] = dot(w[i * inner : (i + 1) * inner, :], xn1[...], 1, 0).astype(low)
+
+    stores[4].start()
 
     blocks = length // q_block
 
@@ -231,12 +275,15 @@
 
     lax.fori_loop(0, heads * blocks, block, 0)
 
+    stores[5].start()
     arrived(4)
+    stores[1].start()
     out_w = w[3 * inner :, :]
     sx[...] = dot(out_w, mixed[:, other_half], 0, 0).astype(low)
     core_two.start()
     hres[...] = dot(out_w, mixed[:, my_half], 0, 0)
     w_t[...] = w[: 3 * inner, :].T
+    stores[2].start()
     core_two.wait_recv()
 
     def add(i, carry):
@@ -245,6 +292,8 @@
         return carry
 
     lax.fori_loop(0, pieces, add, 0)
+
+    stores[6].start()
 
     def write_two(at, value):
         xn2[at, :] = value
@@ -259,7 +308,7 @@
     @pl.when(c != y)
     def _():
         move_facts.wait_send()
-        for each in moves:
+        for each in moves + passed:
             each.wait_send()
         move_g.wait()
 
@@ -267,8 +316,13 @@
     def _():
         keep_g.wait()
 
-
-def front(x, g, weights, lengths, valid, bias, gain_one, gain_two):
+    second_g.wait()
+    keep_late.wait()
+    for each in stores:
+        each.wait()
+
+
+def front(x, g, weights, lengths, valid, bias, gain_one, gain_two, share):
     width, half_len = x.shape
     length = 2 * half_len
     heads = bias.shape[0]
@@ -278,15 +332,17 @@
     smem = pl.BlockSpec(memory_space=pltpu.SMEM)
     sds = lambda kind, *shape: jax.ShapeDtypeStruct(shape, kind)
     facts = pltpu.VMEM((heads * bias.shape[1] + 8, 128), wide)
+    b16 = lambda *shape: pltpu.VMEM(shape, low)
     return pl.pallas_call(
-        front_kernel,
+        functools.partial(front_kernel, share),
         in_specs=[hbm] * 6 + [smem] * 3 + [vmem] * 2,
-        out_specs=[vmem, vmem, hbm, vmem, vmem, vmem, vmem, vmem, hbm] + [vmem] * 6,
+        out_specs=[hbm] * 11 + [vmem] * 5,
         out_shape=[
             sds(low, width, half_len),
             sds(low, width, half_len),
-            sds(low, width, half_len),
-            sds(low, 4 * inner, width),
+            sds(low, width, half_len // 2),
+            sds(low, width, half_len // 2),
+            sds(low, inner, width),
             sds(low, width, 3 * inner),
             sds(low, width, length),
             sds(low, 3 * inner, length),
@@ -300,17 +356,25 @@
             sds(wide, width, 128),
         ],
         scratch_shapes=[
+            b16(width, half_len),
+            b16(width, half_len),
+            b16(4 * inner, width),
+            b16(width, 3 * inner),
+            b16(width, length),
+            b16(3 * inner, length),
+            b16(inner, length),
+            pltpu.VMEM((width, half_len), wide),
             facts,
             facts,
-            pltpu.VMEM((2, length, q_block), low),
+            b16(2, length, q_block),
             pltpu.VMEM((heads, 2 * length - q_block, q_block), wide),
-            pltpu.VMEM((width, half_len), low),
-            pltpu.VMEM((width, half_len), low),
+            b16(width, half_len),
+            b16(width, half_len),
             pltpu.VMEM((length, 128), wide),
             pltpu.VMEM((8, length), wide),
-            pltpu.SemaphoreType.DMA((9,)),
-            pltpu.SemaphoreType.DMA((9,)),
-            pltpu.SemaphoreType.DMA((9,)),
+            pltpu.SemaphoreType.DMA((14,)),
+            pltpu.SemaphoreType.DMA((14,)),
+            pltpu.SemaphoreType.DMA((17,)),
         ],
         compiler_params=pltpu.CompilerParams(vmem_limit_bytes=60 << 20, collective_id=2, has_side_effects=True),
         cost_estimate=hint,
@@ -404,34 +468,35 @@
 
 
 def ffn_kernel(
-    x_ref, go_ref, hres_ref, g_h, gate_w, up_w, down_w,
-    hid_ref, pair_ref, xr_ref, gr_ref, out_ref, out_r_ref, gx_ref, late_ref,
-    xs, gs, out_acc, gx_acc, x_in, g_in, sems,
+    x_ref, go_ref, gr_ref, hres_ref, g_late, gate_w, up_w, down_w,
+    hid_ref, pair_ref, xr_h, gr_h, out_h, out_r_h, gx_h, late_h,
+    xs, gs, out_acc, gx_acc, x_in, g_in, gx_out, out_v, gx_v, sems, store_sems,
 ):
     chunk = pl.program_id(0)
     tile = pl.program_id(1)
     size = xs.shape[0]
+    mesh_id = dict(device_id_type=pl.DeviceIdType.MESH)
     s = lax.axis_index("seq")
     y = lax.axis_index("tensor")
     c = s % 2
-    first = s - c
-    mesh_id = dict(device_id_type=pl.DeviceIdType.MESH)
     to_y = {"tensor": 1 - y}
-    to_core = {"seq": first + 1 - c}
-    to_second = {"seq": first + y, "tensor": 1 - c}
+    to_second = {"seq": s - c + y, "tensor": 1 - c}
     half = [pl.ds(0, size), pl.ds(size, size)]
 
-    def send_x(h):
+    def move(k, src, dst, who):
         return pltpu.make_async_remote_copy(
-            src_ref=x_ref.at[:, half[h]], dst_ref=x_in.at[h], send_sem=sems.at[h], recv_sem=sems.at[2 + h],
-            device_id=to_y, **mesh_id,
+            src_ref=src, dst_ref=dst, send_sem=sems.at[k], recv_sem=sems.at[3 + k], device_id=who, **mesh_id
         )
 
-    def send_g(h):
-        return pltpu.make_async_remote_copy(
-            src_ref=g_h.at[:, half[h]], dst_ref=g_in.at[h], send_sem=sems.at[4 + h], recv_sem=sems.at[6 + h],
-            device_id=to_second, **mesh_id,
-        )
+    send_x = [move(h, x_ref.at[:, half[h]], x_in.at[h], to_y) for h in range(2)]
+    send_g = move(2, g_late, g_in, to_second)
+    to = lambda k, src, dst: pltpu.make_async_copy(src, dst, store_sems.at[k])
+    store_x = [to(h, x_in.at[h], xr_h.at[:, half[h]]) for h in range(2)]
+    store_out = [to(2 + h, out_v.at[h], out_h.at[:, half[h]]) for h in range(2)]
+    store_out_r = [to(4 + h, out_v.at[2 + h], out_r_h.at[:, half[h]]) for h in range(2)]
+    store_gx = [to(6 + h, gx_v.at[h], gx_h.at[:, half[h]]) for h in range(2)]
+    store_late = [to(8 + h, gx_out.at[h], late_h.at[:, half[h]]) for h in range(2)]
+    store_g = to(10, g_in, gr_h)
 
     @pl.when(tile == 0)
     def _():
@@ -441,12 +506,11 @@
     @pl.when((tile == 0) & (chunk == 0))
     def _():
         barrier = pltpu.get_barrier_semaphore()
-        for who in (to_y, to_core):
+        for who in (to_y, {"seq": s + 1 - 2 * c}):
             pl.semaphore_signal(barrier, inc=1, device_id=who, **mesh_id)
         pl.semaphore_wait(barrier, 2)
-        for h in range(2):
-            send_x(h).start()
-            send_g(h).start()
+        for each in (*send_x, send_g):
+            each.start()
 
     for h in range(2):
 
@@ -457,12 +521,15 @@
 
         @pl.when((tile == 0) & (chunk == 2 + h))
         def _(h=h):
-            send_x(h).wait_recv()
+            send_x[h].wait_recv()
             xs[...] = x_in[h].T
-            xr_ref[:, half[h]] = x_in[h]
-            send_g(h).wait_recv()
-            gs[...] = g_in[h].T
-            gr_ref[:, half[h]] = g_in[h]
+            store_x[h].start()
+            if h:
+                send_g.wait_recv()
+                gs[...] = g_in[...].T
+                store_g.start()
+            else:
+                gs[...] = gr_ref[...].T
 
     gate = dot(xs[...], gate_w[...], 1, 0)
     up = dot(xs[...], up_w[...], 1, 0)
@@ -487,53 +554,65 @@
 
         @pl.when(last & (chunk == h))
         def _(h=h):
-            out_ref[:, half[h]] = (hres_ref[:, half[h]] + out_acc[...]).astype(low)
-            gx_ref[:, half[h]] = gx_acc[...]
+            out_v[h] = (hres_ref[:, half[h]] + out_acc[...]).astype(low)
+            store_out[h].start()
+            gx_v[h] = gx_acc[...]
+            store_gx[h].start()
 
         @pl.when(last & (chunk == 2 + h))
         def _(h=h):
-            out_r_ref[:, half[h]] = out_acc[...].astype(low)
-            late_ref[:, half[h]] = gx_acc[...].astype(low)
+            out_v[2 + h] = out_acc[...].astype(low)
+            store_out_r[h].start()
+            gx_out[h] = gx_acc[...].astype(low)
+            store_late[h].start()
 
     @pl.when(last & (chunk == 3))
     def _():
-        for h in range(2):
-            send_x(h).wait_send()
-            send_g(h).wait_send()
-
-
-def ffn(x, g_own, hres, g_in, gate_w, up_w, down_w):
+        for each in (*send_x, send_g):
+            each.wait_send()
+        for each in store_x + store_out + store_out_r + store_gx + store_late + [store_g]:
+            each.wait()
+
+
+def ffn(x, g_own, g_oth, hres, g_late, gate_w, up_w, down_w):
     width, tokens = x.shape
     hidden = gate_w.shape[1]
     tile, size = 256, tokens // 2
+    hbm = pl.BlockSpec(memory_space=pl.ANY)
     full = pl.BlockSpec((width, tokens), lambda s, j: (0, 0), pipeline_mode=pl.Buffered(1))
     weight = pl.BlockSpec((width, tile), lambda s, j: (0, j))
+    first = pl.BlockSpec((width, size), lambda s, j: (0, 0), pipeline_mode=pl.Buffered(1))
     act_shape = jax.ShapeDtypeStruct((2 * tokens, hidden), low)
     tokens_of = lambda kind: jax.ShapeDtypeStruct((width, tokens), kind)
     return pl.pallas_call(
         ffn_kernel,
         grid=(4, hidden // tile),
-        in_specs=[full, full, full, pl.BlockSpec(memory_space=pl.ANY), weight, weight, weight],
+        in_specs=[full, full, first, full, hbm, weight, weight, weight],
         out_specs=[
             pl.BlockSpec((size, tile), lambda s, j: (s, j)),
             pl.BlockSpec((2, size, tile), lambda s, j: (0, s, j)),
         ]
-        + [full] * 6,
+        + [hbm] * 6,
         out_shape=[act_shape, jax.ShapeDtypeStruct((2, 2 * tokens, hidden), low)]
-        + [tokens_of(kind) for kind in (low, low, low, low, wide, low)],
+        + [tokens_of(low), jax.ShapeDtypeStruct((width, size), low)]
+        + [tokens_of(kind) for kind in (low, low, wide, low)],
         scratch_shapes=[
             pltpu.VMEM((size, width), low),
             pltpu.VMEM((size, width), low),
             pltpu.VMEM((width, size), wide),
             pltpu.VMEM((width, size), wide),
             pltpu.VMEM((2, width, size), low),
+            pltpu.VMEM((width, size), low),
             pltpu.VMEM((2, width, size), low),
-            pltpu.SemaphoreType.DMA((8,)),
+            pltpu.VMEM((4, width, size), low),
+            pltpu.VMEM((2, width, size), wide),
+            pltpu.SemaphoreType.DMA((6,)),
+            pltpu.SemaphoreType.DMA((11,)),
         ],
         compiler_params=pltpu.CompilerParams(vmem_limit_bytes=56 << 20, collective_id=0, has_side_effects=True),
         cost_estimate=hint,
         name="ffn_both_ways",
-    )(x, g_own, hres, g_in, gate_w, up_w, down_w)
+    )(x, g_own, g_oth, hres, g_late, gate_w, up_w, down_w)
 
 
 def weight_grad_kernel(core_ref, own_ref, oth_ref, right_ref, *refs):
@@ -573,7 +652,7 @@
 
 
 def back_kernel(
-    hid_h, pair_h, go_h, gr_h, xo_h, xr_h, gx_h, hres_h, xin_h, probs_h, xn1_h, outp_h, outr_h, late_h,
+    hid_h, pair_h, go_h, gr1_h, gr2_h, xo_h, xr_h, gx_h, hres_h, xin_h, probs_h, xn1_h, outp_h, outr_h, late_h,
     out_w, w_t, qkv, mixed, gain2, gain1, scale2, scale1,
     got_p, got_r, got_in, d_out, p_out, a_out, gin, small,
     r_core, xp, zd, zp, dx, px, bf, rx, ya, xa, za, ab, late_in, sm_src, sm_in, send_sems, recv_sems, load_sems,
@@ -745,7 +824,8 @@
             load(2, xr_h, l_xr),
             load(3, hid_h, r_buf.at[1]),
             load(4, go_h, l_go),
-            load(5, gr_h, l_gr),
+            load(5, gr1_h, l_gr.at[:, pl.ds(0, half_len // 2)]),
+            load(14, gr2_h, l_gr.at[:, pl.ds(half_len // 2, half_len // 2)]),
         ]
         load_own = load(6, pair_h.at[m], r_buf.at[0])
         for each in loads:
@@ -1086,7 +1166,7 @@
 
 
 def back_all(
-    hid, pair, g_own, g_oth, x_own, x_oth, gx, hres, x_in, probs, xn_one, out_first, out_oth, late,
+    hid, pair, g_own, g_oth, g_late, x_own, x_oth, gx, hres, x_in, probs, xn_one, out_first, out_oth, late,
     out_w, w_t, qkv, mixed, gain_two, gain_one, scale_two, scale_one, zs,
 ):
     width, half_len = g_own.shape
@@ -1102,7 +1182,7 @@
     b16 = lambda *shape: pltpu.VMEM(shape, low)
     return pl.pallas_call(
         back_kernel,
-        in_specs=[hbm] * 14 + [vmem] * 8,
+        in_specs=[hbm] * 15 + [vmem] * 8,
         out_specs=[hbm] * 3 + [vmem] * 5,
         out_shape=[
             sds(low, width, half_len),
@@ -1132,15 +1212,124 @@
             pltpu.VMEM((5, 16, width), wide),
             pltpu.SemaphoreType.DMA((60,)),
             pltpu.SemaphoreType.DMA((60,)),
-            pltpu.SemaphoreType.DMA((14,)),
+            pltpu.SemaphoreType.DMA((15,)),
         ],
         compiler_params=pltpu.CompilerParams(vmem_limit_bytes=61 << 20, collective_id=1, has_side_effects=True),
         cost_estimate=hint,
         name="back_all",
     )(
-        hid, pair, g_own, g_oth, x_own, x_oth, gx, hres, x_in, probs, xn_one, out_first, out_oth, late,
+        hid, pair, g_own, g_oth, g_late, x_own, x_oth, gx, hres, x_in, probs, xn_one, out_first, out_oth, late,
         out_w, w_t, qkv, mixed, gain_two, gain_one, scale_two, scale_one,
     )
+
+
+def finish_kernel(
+    d_h, p_h, a_h, own_in, got_in, own_out, got_out, oth_out, small,
+    d_out, g_out, u_out, q_out, k_out, v_out, o_out, in_out, y_out, gain1_out, gain2_out, bias_out,
+    w_in, w_out, a_in, i_in, i_out, y_in, sems,
+):
+    own = lax.axis_index("seq") % 2 == lax.axis_index("tensor")
+    rows = w_in.shape[1]
+    width = i_in.shape[0]
+    copy = lambda k, src, dst: pltpu.make_async_copy(src, dst, sems.at[k])
+    loads = [copy(0, d_h, w_in.at[0]), copy(1, p_h.at[0], w_in.at[1]), copy(2, p_h.at[1], w_in.at[2]), copy(3, a_h, a_in)]
+    load_y = copy(4, oth_out, y_in.at[1])
+    mine = [copy(5, own_in, i_in), copy(6, own_out, y_in.at[0])]
+    theirs = [copy(5, got_in, i_in), copy(6, got_out, y_in.at[0])]
+    stores = [copy(7 + i, w_out.at[i], out) for i, out in enumerate((d_out, g_out, u_out))]
+    store_i = copy(10, i_out, in_out)
+    store_y = copy(11, y_in.at[0], y_out)
+
+    def start(which):
+        @pl.when(own)
+        def _():
+            mine[which].start()
+
+        @pl.when(jnp.logical_not(own))
+        def _():
+            theirs[which].start()
+
+    loads[0].start()
+    start(0)
+    for each in loads[1:3]:
+        each.start()
+    start(1)
+    load_y.start()
+    loads[3].start()
+
+    def piecewise(count, size, run):
+        def step(i, carry):
+            run(pl.ds(pl.multiple_of(i * size, size), size))
+            return carry
+
+        lax.fori_loop(0, count, step, 0)
+
+    def widen(i):
+        loads[i].wait()
+
+        def run(at):
+            w_out[i, at, :] = w_in[i, at, :].astype(wide)
+
+        piecewise(rows // 16, 16, run)
+        stores[i].start()
+
+    widen(0)
+    mine[0].wait()
+
+    def run_in(at):
+        i_out[at, :] = i_in[at, :].astype(wide)
+
+    piecewise(width // 64, 64, run_in)
+    store_i.start()
+    widen(1)
+    widen(2)
+    mine[1].wait()
+    load_y.wait()
+
+    def run_y(at):
+        y_in[0, at, :] = (y_in[0, at, :].astype(wide) + y_in[1, at, :].astype(wide)).astype(low)
+
+    piecewise(width // 64, 64, run_y)
+    store_y.start()
+    loads[3].wait()
+    inner = q_out.shape[0]
+    for i, out in enumerate((q_out, k_out, v_out, o_out)):
+        out[...] = a_in[:rows, i * inner : (i + 1) * inner].astype(wide).T
+    gain1_out[...] = small[1, :]
+    gain2_out[...] = small[0, :]
+    bias_out[...] = small[8 : 8 + bias_out.shape[0], : bias_out.shape[1]]
+    for each in stores + [store_i, store_y]:
+        each.wait()
+
+
+def finish(d, p, a, own_in, got_in, own_out, got_out, oth_out, small, inner, bias_shape):
+    rows, hidden = d.shape
+    width, half_len = own_in.shape
+    hbm = pl.BlockSpec(memory_space=pl.ANY)
+    vmem = pl.BlockSpec(memory_space=pltpu.VMEM)
+    sds = lambda kind, *shape: jax.ShapeDtypeStruct(shape, kind)
+    return pl.pallas_call(
+        finish_kernel,
+        in_specs=[hbm] * 8 + [vmem],
+        out_specs=[hbm] * 3 + [vmem] * 4 + [hbm] * 2 + [vmem] * 3,
+        out_shape=[sds(wide, rows, hidden)] * 3
+        + [sds(wide, inner, rows)] * 4
+        + [sds(wide, width, half_len), sds(low, width, half_len)]
+        + [sds(wide, width)] * 2
+        + [sds(wide, *bias_shape)],
+        scratch_shapes=[
+            pltpu.VMEM((3, rows, hidden), low),
+            pltpu.VMEM((3, rows, hidden), wide),
+            pltpu.VMEM(a.shape, low),
+            pltpu.VMEM((width, half_len), low),
+            pltpu.VMEM((width, half_len), wide),
+            pltpu.VMEM((2, width, half_len), low),
+            pltpu.SemaphoreType.DMA((12,)),
+        ],
+        compiler_params=pltpu.CompilerParams(vmem_limit_bytes=60 << 20),
+        cost_estimate=hint,
+        name="finish_all",
+    )(d, p, a, own_in, got_in, own_out, got_out, oth_out, small)
 
 
 def norm_back(values, scale, gain, grad):
@@ -1259,7 +1448,7 @@
 
     flat = lambda a: a.reshape(half_len, width).T
     (
-        x_in, g_in, g_own, w, w_t, xn_one, qkv, mixed, probs, hres, xn_own, scale_one, scale_two, gain_one, gain_two
+        x_in, g_own, g_oth, g_send, out_w, w_t, xn_one, qkv, mixed, probs, hres, xn_own, scale_one, scale_two, gain_one, gain_two
     ) = front(
         flat(layer_in),
         flat(out_grad),
@@ -1267,40 +1456,40 @@
         doc_lengths,
         valid_length,
         position_bias.T,
-        gain_attn[None, :],
-        gain_ffn[None, :],
+        gain_attn,
+        gain_ffn,
+        moves.nx == 2,
     )
-    qkv_w, out_w = w[: 3 * inner_width], w[3 * inner_width :]
-    hid, pair, xn_oth, g_oth, out_first, out_oth, gx, late = ffn(
-        xn_own, g_own, hres, g_in, gate_weight, up_weight, down_weight.T
+    hid, pair, xn_oth, g_late, out_first, out_oth, gx, late = ffn(
+        xn_own, g_own, g_oth, hres, g_send, gate_weight, up_weight, down_weight.T
     )
     if moves.nx == 2 and moves.nz == 4:
         got_first, got_oth, got_in, sum_d, sum_p, sums, grad_in, small = back_all(
-            hid, pair, g_own, g_oth, xn_own, xn_oth, gx, hres, x_in, probs, xn_one, out_first, out_oth, late,
+            hid, pair, g_own, g_oth, g_late, xn_own, xn_oth, gx, hres, x_in, probs, xn_one, out_first, out_oth, late,
             out_w, w_t, qkv, mixed, gain_two, gain_one, scale_two, scale_one, moves.nz,
         )
-        out_y = jnp.where(c == y, out_first, got_first).astype(wide) + got_oth.astype(wide)
-        grad_in = jnp.where(c == y, grad_in, got_in).astype(wide)
-        sums = sums[: width // moves.nz].astype(wide)
-        sum_q, sum_k, sum_v, sum_o = (
-            sums[:, i * inner_width : (i + 1) * inner_width] for i in range(4)
+        sum_d, sum_g, sum_u, sum_q, sum_k, sum_v, sum_o, grad_in, out_y, gain_one_sum, gain_two_sum, bias_sum = finish(
+            sum_d, sum_p, sums, grad_in, got_in, out_first, got_first, got_oth, small,
+            inner_width, (2 * heads, position_bias.shape[0]),
         )
         return (
-            out_y.astype(low).T.reshape(half_len, 1, width),
+            out_y.T.reshape(half_len, 1, width),
             grad_in.T.reshape(half_len, 1, width),
-            small[1],
-            sum_q,
-            sum_k,
-            sum_v,
-            small[8 : 8 + 2 * heads, : position_bias.shape[0]].T,
-            sum_o.T,
-            small[0],
-            sum_p[0].astype(wide),
-            sum_p[1].astype(wide),
-            sum_d.astype(wide).T,
+            gain_one_sum,
+            sum_q.T,
+            sum_k.T,
+            sum_v.T,
+            bias_sum.T,
+            sum_o,
+            gain_two_sum,
+            sum_g,
+            sum_u,
+            sum_d.T,
         )
     grad_gate, grad_up = pair[0], pair[1]
     gx = gx + moves.over_y(late).astype(wide)
+    g_oth = jnp.concatenate([g_oth, g_late], axis=1)
+    qkv_w = w_t.T
     x_wide = x_in.astype(wide)
     gain_one, gain_two = gain_one[:, :1], gain_two[:, :1]
 

time: 304 us -> 277 us (0.911)
  local copies, waits for them, and re-layouts: 12.2 us -> 0 us
  other arithmetic: 9.95 us -> 0 us
  Pallas kernels: 279 us -> 273 us
    pallas_call x1, Pallas kernels: 64.1 us -> 58.7 us  [ffn(): pl.pallas_call(ffn_kernel, grid=(4, hidden // tile), in_specs=[full, full...]
    unnamed x18 -> x0, local copies, waits for them, and re-layouts: 4.71 us -> none
    convert_element_type x2 -> x0, other arithmetic: 4.69 us -> none  [the longest x1 4.61 us: local(): sum_p[1].astype(wide)]
    reshape x2 -> x0, other arithmetic: 3.59 us -> none  [the longest x1 1.82 us: local(): grad_in.T.reshape(half_len, 1, width)]
    slice x2 -> x0, local copies, waits for them, and re-layouts: 3.43 us -> none  [the longest x1 1.92 us: local(): qkv_w, out_w = (w[:3 * inner_width], w[3 * inner_width:])]
    pallas_call x2 -> x3, Pallas kernels: 215 us -> 214 us  [the longest x1 140 us: back_all(): pl.pallas_call(back_kernel, in_specs=[hbm] * 15 + [vmem] * 8, out_specs=[...]
where the time goes in v6:
time: 277 us; the launch traced here: 275 us
  Pallas kernels  273 us (99%)
    pallas_call x1, Pallas kernels, back_all(): pl.pallas_call(back_kernel, in_specs=[hbm] * 15 + [vmem] * 8, out_specs=[...  140 us
    pallas_call x1, Pallas kernels, front(): pl.pallas_call(functools.partial(front_kernel, share), in_specs=[hbm] * 6...  65 us
    pallas_call x1, Pallas kernels, ffn(): pl.pallas_call(ffn_kernel, grid=(4, hidden // tile), in_specs=[full, full...  58.7 us
    pallas_call x1, Pallas kernels, finish(): pl.pallas_call(finish_kernel, in_specs=[hbm] * 8 + [vmem], out_specs=[hbm...  9.27 us

profile of v6, /device:TPU:0, one launch (start us, length us, event | category | flops | bytes accessed | tf_op | source)
XLA Modules:
  0.0 274.7 jit_solution(3841109610237885069)
XLA Ops:
  1.3 65.0 %front_all.1 = (bf16[1472,512]{1,0:T(8,128)(2,1)}, bf16[1472,512]{1,0:T(8,128)(2,1)}, bf16[1472,256]{1,0:T(8,128)(2,1)}, bf16[1472,256]{1,0:T(8,128)(2,1)}, bf16...) custom-call(bf16[1472,512]{1,0:T(8,128)(2,1)} %bitcast.23, ...), custom_call_target="tpu_custom_call" | custom-call | flops 1000 | bytes 1000 | tf_op jit(solution)/shard_map/front_all/pallas_call | solution.py:336
  66.3 58.7 %ffn_both_ways.1 = (bf16[1024,1792]{1,0:T(8,128)(2,1)}, bf16[2,1024,1792]{2,1,0:T(8,128)(2,1)}, bf16[1472,512]{1,0:T(8,128)(2,1)}, bf16[1472,256]{1,0:T(8,128)(2...) custom-call(bf16[1472,512]{1,0:T(8,128)(2,1)} %get-tuple-element.56., ...), custom_call_target="tpu_custom_call" | custom-call | flops 1000 | bytes 1000 | tf_op jit(solution)/shard_map/ffn_both_ways/pallas_call | solution.py:587
  125.0 140.3 %back_all.1 = (bf16[1472,512]{1,0:T(8,128)(2,1)}, bf16[1472,512]{1,0:T(8,128)(2,1)}, bf16[1472,512]{1,0:T(8,128)(2,1)}, bf16[368,1792]{1,0:T(8,128)(2,1)}, bf16[...) custom-call(bf16[1024,1792]{1,0:T(8,128)(2,1)} %get-tuple-element.61.hid_h,, ...), custom_call_target="tpu_custom_call" | custom-call | flops 1000 | bytes 1000 | tf_op jit(solution)/shard_map/back_all/pallas_call | solution.py:1183
  265.2 9.3 %finish_all.1 = (f32[368,1792]{1,0:T(8,128)}, f32[368,1792]{1,0:T(8,128)}, f32[368,1792]{1,0:T(8,128)}, f32[192,368]{1,0:T(8,128)}, f32[192,368]{1,0:T(8,128)}, ...) custom-call(bf16[368,1792]{1,0:T(8,128)(2,1)} %get-tuple-element.80., ...), custom_call_target="tpu_custom_call" | custom-call | flops 1000 | bytes 1000 | tf_op jit(solution)/shard_map/finish_all/pallas_call | solution.py:1311

commit v7 on v6

--- a/solution.py
+++ b/solution.py
@@ -44,7 +44,6 @@
     dim = inner // heads
     piece = 64
     pieces = width // piece
-    lanes = half_len // 128
     mesh_id = dict(device_id_type=pl.DeviceIdType.MESH)
     to_core = {"seq": 2 * m + 1 - c}
     to_swap = {"seq": 2 * m + 1 - c, "tensor": 1 - y}
@@ -60,29 +59,38 @@
             src_ref=src, dst_ref=dst, send_sem=send_sems.at[k], recv_sem=recv_sems.at[k], device_id=who, **mesh_id
         )
 
-    to_x = {"seq": 2 * (1 - m) + c}
     to_second = {"seq": 2 * m + y, "tensor": 1 - c}
 
     named = [(x_h, x_in)] + [
         (src, w.at[pl.ds(i * inner, inner)]) for i, src in enumerate((wq_h, wk_h, wv_h, wo_h))
     ]
-    moves = [move(1, x_h, x_in, to_swap)]
-    passed = []
+    half_cols = half_len // 2
+    halves = [pl.ds(h * half_cols, half_cols) for h in range(2)]
+    move_x = [move((1, 15)[h], x_h.at[:, halves[h]], x_in.at[:, halves[h]], to_swap) for h in range(2)]
+    moves = []
+    z = lax.axis_index("dp")
+    rows = inner // 2
+
+    def half_of(ref, i, k):
+        return ref.at[pl.ds(pl.multiple_of(i * inner + k * rows, rows), rows)]
+
+    fetched, passed_z, passed_x = [], [], []
     for i, src in enumerate((wq_h, wk_h, wv_h, wo_h)):
         if share:
-            rows = inner // 2
-            dst = w.at[pl.ds(pl.multiple_of(i * inner + m * rows, rows), rows)]
-            moves.append(move(2 + i, src.at[pl.ds(pl.multiple_of(m * rows, rows), rows)], dst, to_swap))
-            passed.append(move(10 + i, dst, dst, to_x))
+            fetched.append(move(2, half_of(src, 0, m), half_of(w, i, m), to_swap))
+            part = half_of(w, (z + 4 - i) % 4, m)
+            passed_x.append(move(10 + i, part, part, {"seq": 2 * (1 - m) + c}))
+            if i < 3:
+                passed_z.append(move(3 + i if i else 14, part, part, {"dp": (z + 1) % 4}))
         else:
             moves.append(move(2 + i, src, w.at[pl.ds(i * inner, inner)], to_swap))
     loads = [pltpu.make_async_copy(src, dst, load_sems.at[1 + i]) for i, (src, dst) in enumerate(named)]
     move_facts = move(0, facts_src, facts, to_swap)
     move_g = move(6, g_in, g_own, to_swap)
-    early = half_len // 2
+    early = g_oth.shape[1]
     second_g = move(9, g_in.at[:, pl.ds(0, early)], g_oth, to_second)
     to = lambda k, src, dst: pltpu.make_async_copy(src, dst, load_sems.at[k])
-    keep_late = to(16, g_in.at[:, pl.ds(early, early)], g_late)
+    keep_late = to(16, g_in.at[:, pl.ds(early, half_len - early)], g_late)
     load_g = pltpu.make_async_copy(g_h, g_in, load_sems.at[0])
     keep_g = pltpu.make_async_copy(g_in, g_own, load_sems.at[6])
     stores = [
@@ -94,14 +102,21 @@
     ]
 
     def pass_on(i):
-        if share:
-
-            @pl.when(c != y)
-            def _():
-                moves[1 + i].wait_recv()
-                passed[i].start()
-
-    core_one = move(7, xn1.at[:, my_half], xn1.at[:, my_half], to_core)
+        if not share:
+            return
+
+        @pl.when(c != y)
+        def _():
+            if i:
+                passed_z[i - 1].wait_recv()
+            else:
+                fetched[0].wait_recv()
+            if i < 3:
+                passed_z[i].start()
+            passed_x[i].start()
+
+    my_parts = [pl.ds(pl.multiple_of(c * half_len + h * half_cols, 128), half_cols) for h in range(2)]
+    core_one = [move((7, 16)[h], xn1.at[:, my_parts[h]], xn1.at[:, my_parts[h]], to_core) for h in range(2)]
     core_two = move(8, sx, rx, to_core)
 
     load_g.start()
@@ -117,7 +132,9 @@
     facts_src[at + 4 : at + 5, :] = jnp.full((1, 128), valid[0].astype(wide), wide)
 
     barrier = pltpu.get_barrier_semaphore()
-    greet = [to_core, to_swap, {"tensor": 1 - y}] + ([to_x] if share else [])
+    greet = [to_core, to_swap, {"tensor": 1 - y}]
+    if share:
+        greet += [{"seq": 2 * (1 - m) + c}, {"dp": (z + 1) % 4}, {"dp": (z + 3) % 4}]
     for who in greet:
         pl.semaphore_signal(barrier, inc=1, device_id=who, **mesh_id)
     pl.semaphore_wait(barrier, len(greet))
@@ -125,8 +142,10 @@
     @pl.when(c != y)
     def _():
         move_facts.start()
-        for i in (1, 2, 3, 0, 4) if share else range(5):
-            moves[i].start()
+        for i, each in enumerate(fetched):
+            pl.when(z == i)(each.start)
+        for each in move_x + moves:
+            each.start()
 
     @pl.when(c == y)
     def _():
@@ -154,8 +173,11 @@
 
     second_g.start()
     keep_late.start()
+    pass_on(0)
     gain1[...] = jnp.broadcast_to(gain1_row[...].astype(wide)[None, :], (128, width)).T
     gain2[...] = jnp.broadcast_to(gain2_row[...].astype(wide)[None, :], (128, width)).T
+
+    pass_on(1)
 
     @pl.when(c != y)
     def _():
@@ -173,6 +195,7 @@
     for i in range(length // 128):
         positions = (lax.broadcasted_iota(jnp.int32, (8, 128), 1) + i * 128).astype(wide)
         seg_q[:, i * 128 : (i + 1) * 128] = segments(positions)
+    pass_on(2)
     reach = length - q_block
     near_rows = q_block + 2 * band_half
     d = (
@@ -200,20 +223,20 @@
             table[h, pl.ds(0, far_rows), col] = jnp.broadcast_to(value(15), (far_rows, 128))
             table[h, pl.ds(far_rows + near_rows, far_rows), col] = jnp.broadcast_to(value(31), (far_rows, 128))
 
-    def spread(a):
-        return jnp.concatenate([a] * lanes, axis=1)
-
-    def norm(read, gain, scale, write):
+    def norm(read, gain, scale, cols, write):
+        size = cols.size
+
         def first(i, total):
             v = read(pl.ds(pl.multiple_of(i * piece, piece), piece))
             return total + jnp.sum(v * v, axis=0, keepdims=True)
 
-        total = lax.fori_loop(0, pieces, first, jnp.zeros((1, half_len), wide))
-        scale[...] = lax.rsqrt(total * (1.0 / width) + eps_norm)
+        total = lax.fori_loop(0, pieces, first, jnp.zeros((1, size), wide))
+        scale[:, cols] = lax.rsqrt(total * (1.0 / width) + eps_norm)
 
         def second(i, carry):
             at = pl.ds(pl.multiple_of(i * piece, piece), piece)
-            write(at, (read(at) * scale[...] * spread(gain[at, :])).astype(low))
+            spread = jnp.concatenate([gain[at, :]] * (size // 128), axis=1)
+            write(at, (read(at) * scale[:, cols] * spread).astype(low))
             return carry
 
         lax.fori_loop(0, pieces, second, 0)
@@ -221,40 +244,62 @@
     def arrived(i):
         @pl.when(c != y)
         def _():
-            (passed[i - 1] if share and i else moves[i]).wait_recv()
+            if not share:
+                moves[i - 1].wait_recv()
 
         @pl.when(c == y)
         def _():
             loads[i].wait()
 
-    for i in range(3):
-        pass_on(i)
-    arrived(0)
+    pass_on(3)
+    for h in range(2):
+
+        @pl.when(c != y)
+        def _(h=h):
+            move_x[h].wait_recv()
+
+        if h == 0:
+
+            @pl.when(c == y)
+            def _():
+                loads[0].wait()
+
+        def write_one(at, value, h=h):
+            xn1[at, my_parts[h]] = value
+
+        norm(lambda at, h=h: x_in[at, halves[h]].astype(wide), gain1, scale1, halves[h], write_one)
+        core_one[h].start()
     stores[0].start()
-
-    def write_one(at, value):
-        xn1[at, my_half] = value
-
-    norm(lambda at: x_in[at, :].astype(wide), gain1, scale1, write_one)
-    core_one.start()
-    pass_on(3)
-    for i in range(1, 4):
-        arrived(i)
-    core_one.wait_recv()
+    if share:
+
+        @pl.when(c != y)
+        def _():
+            for each in passed_x:
+                each.wait_recv()
+
+    for each in core_one:
+        each.wait_recv()
     stores[3].start()
     for i in range(3):
+        arrived(1 + i)
         qkv[i * inner : (i + 1) * inner, :] = dot(w[i * inner : (i + 1) * inner, :], xn1[...], 1, 0).astype(low)
 
     stores[4].start()
 
     blocks = length // q_block
 
+    turns = heads * blocks // 2
+
+    def turn(i):
+        its = 1 - c + (i // turns) * (2 * c - 1)
+        return i % heads, its * (blocks // 2) + (i % turns) // heads
+
     def store(i):
-        h, b = i // blocks, i % blocks
+        h, b = turn(i)
         return pltpu.make_async_copy(p_buf.at[i % 2], probs_h.at[h, :, side(b, q_block)], load_sems.at[7 + i % 2])
 
     def block(i, carry):
-        h, b = i // blocks, i % blocks
+        h, b = turn(i)
         at = side(b, q_block)
         rows = lambda part: pl.ds(pl.multiple_of((part * heads + h) * dim, dim), dim)
         first = pl.multiple_of(reach - b * q_block, q_block)
@@ -273,17 +318,17 @@
         mixed[rows(0), at] = dot(qkv[rows(2), :], probs, 1, 0).astype(low)
         return carry
 
-    lax.fori_loop(0, heads * blocks, block, 0)
-
-    stores[5].start()
+    lax.fori_loop(0, turns, block, 0)
     arrived(4)
     stores[1].start()
     out_w = w[3 * inner :, :]
     sx[...] = dot(out_w, mixed[:, other_half], 0, 0).astype(low)
     core_two.start()
-    hres[...] = dot(out_w, mixed[:, my_half], 0, 0)
     w_t[...] = w[: 3 * inner, :].T
     stores[2].start()
+    lax.fori_loop(turns, 2 * turns, block, 0)
+    stores[5].start()
+    hres[...] = dot(out_w, mixed[:, my_half], 0, 0)
     core_two.wait_recv()
 
     def add(i, carry):
@@ -298,17 +343,19 @@
     def write_two(at, value):
         xn2[at, :] = value
 
-    norm(lambda at: hres[at, :], gain2, scale2, write_two)
+    norm(lambda at: hres[at, :], gain2, scale2, pl.ds(0, half_len), write_two)
     last = heads * blocks
     store(last - 2).wait()
     store(last - 1).wait()
-    core_one.wait_send()
-    core_two.wait_send()
+    for each in (*core_one, core_two):
+        each.wait_send()
 
     @pl.when(c != y)
     def _():
         move_facts.wait_send()
-        for each in moves + passed:
+        if share:
+            fetched[0].wait_send()
+        for each in move_x + moves + passed_z + passed_x:
             each.wait_send()
         move_g.wait()
 
@@ -340,8 +387,8 @@
         out_shape=[
             sds(low, width, half_len),
             sds(low, width, half_len),
-            sds(low, width, half_len // 2),
-            sds(low, width, half_len // 2),
+            sds(low, width, half_len - 128),
+            sds(low, width, 128),
             sds(low, inner, width),
             sds(low, width, 3 * inner),
             sds(low, width, length),
@@ -372,8 +419,8 @@
             b16(width, half_len),
             pltpu.VMEM((length, 128), wide),
             pltpu.VMEM((8, length), wide),
-            pltpu.SemaphoreType.DMA((14,)),
-            pltpu.SemaphoreType.DMA((14,)),
+            pltpu.SemaphoreType.DMA((17,)),
+            pltpu.SemaphoreType.DMA((17,)),
             pltpu.SemaphoreType.DMA((17,)),
         ],
         compiler_params=pltpu.CompilerParams(vmem_limit_bytes=60 << 20, collective_id=2, has_side_effects=True),
@@ -468,9 +515,9 @@
 
 
 def ffn_kernel(
-    x_ref, go_ref, gr_ref, hres_ref, g_late, gate_w, up_w, down_w,
+    x_ref, go_ref, gr_h0, hres_h, g_late, gate_w, up_w, down_w,
     hid_ref, pair_ref, xr_h, gr_h, out_h, out_r_h, gx_h, late_h,
-    xs, gs, out_acc, gx_acc, x_in, g_in, gx_out, out_v, gx_v, sems, store_sems,
+    xs, gs, out_acc, gx_acc, x_in, g_in, gx_out, gx_in, out_v, gx_v, gr_ref, hres_ref, sems, store_sems,
 ):
     chunk = pl.program_id(0)
     tile = pl.program_id(1)
@@ -485,11 +532,14 @@
 
     def move(k, src, dst, who):
         return pltpu.make_async_remote_copy(
-            src_ref=src, dst_ref=dst, send_sem=sems.at[k], recv_sem=sems.at[3 + k], device_id=who, **mesh_id
+            src_ref=src, dst_ref=dst, send_sem=sems.at[k], recv_sem=sems.at[4 + k], device_id=who, **mesh_id
         )
 
     send_x = [move(h, x_ref.at[:, half[h]], x_in.at[h], to_y) for h in range(2)]
     send_g = move(2, g_late, g_in, to_second)
+    back = gx_in.shape[1]
+    send_gx = move(3, gx_out.at[0, :, pl.ds(0, back)], gx_in, to_y)
+    begun = g_in.shape[1]
     to = lambda k, src, dst: pltpu.make_async_copy(src, dst, store_sems.at[k])
     store_x = [to(h, x_in.at[h], xr_h.at[:, half[h]]) for h in range(2)]
     store_out = [to(2 + h, out_v.at[h], out_h.at[:, half[h]]) for h in range(2)]
@@ -497,6 +547,8 @@
     store_gx = [to(6 + h, gx_v.at[h], gx_h.at[:, half[h]]) for h in range(2)]
     store_late = [to(8 + h, gx_out.at[h], late_h.at[:, half[h]]) for h in range(2)]
     store_g = to(10, g_in, gr_h)
+    load_h = to(11, hres_h, hres_ref)
+    load_g = to(12, gr_h0, gr_ref)
 
     @pl.when(tile == 0)
     def _():
@@ -505,6 +557,8 @@
 
     @pl.when((tile == 0) & (chunk == 0))
     def _():
+        load_h.start()
+        load_g.start()
         barrier = pltpu.get_barrier_semaphore()
         for who in (to_y, {"seq": s + 1 - 2 * c}):
             pl.semaphore_signal(barrier, inc=1, device_id=who, **mesh_id)
@@ -524,12 +578,15 @@
             send_x[h].wait_recv()
             xs[...] = x_in[h].T
             store_x[h].start()
+            if not h:
+                load_g.wait()
             if h:
+                gs[: size - begun, :] = gr_ref[:, size:].T
                 send_g.wait_recv()
-                gs[...] = g_in[...].T
+                gs[size - begun :, :] = g_in[...].T
                 store_g.start()
             else:
-                gs[...] = gr_ref[...].T
+                gs[...] = gr_ref[:, :size].T
 
     gate = dot(xs[...], gate_w[...], 1, 0)
     up = dot(xs[...], up_w[...], 1, 0)
@@ -554,21 +611,29 @@
 
         @pl.when(last & (chunk == h))
         def _(h=h):
+            if not h:
+                load_h.wait()
             out_v[h] = (hres_ref[:, half[h]] + out_acc[...]).astype(low)
             store_out[h].start()
             gx_v[h] = gx_acc[...]
-            store_gx[h].start()
+            if h:
+                store_gx[h].start()
 
         @pl.when(last & (chunk == 2 + h))
         def _(h=h):
             out_v[2 + h] = out_acc[...].astype(low)
             store_out_r[h].start()
             gx_out[h] = gx_acc[...].astype(low)
+            if not h:
+                send_gx.start()
             store_late[h].start()
 
     @pl.when(last & (chunk == 3))
     def _():
-        for each in (*send_x, send_g):
+        send_gx.wait_recv()
+        gx_v[0, :, :back] += gx_in[...].astype(wide)
+        store_gx[0].start()
+        for each in (*send_x, send_g, send_gx):
             each.wait_send()
         for each in store_x + store_out + store_out_r + store_gx + store_late + [store_g]:
             each.wait()
@@ -577,24 +642,24 @@
 def ffn(x, g_own, g_oth, hres, g_late, gate_w, up_w, down_w):
     width, tokens = x.shape
     hidden = gate_w.shape[1]
-    tile, size = 256, tokens // 2
+    tile, size = hidden // 2, tokens // 2
+    begun = g_late.shape[1]
     hbm = pl.BlockSpec(memory_space=pl.ANY)
     full = pl.BlockSpec((width, tokens), lambda s, j: (0, 0), pipeline_mode=pl.Buffered(1))
     weight = pl.BlockSpec((width, tile), lambda s, j: (0, j))
-    first = pl.BlockSpec((width, size), lambda s, j: (0, 0), pipeline_mode=pl.Buffered(1))
     act_shape = jax.ShapeDtypeStruct((2 * tokens, hidden), low)
     tokens_of = lambda kind: jax.ShapeDtypeStruct((width, tokens), kind)
     return pl.pallas_call(
         ffn_kernel,
         grid=(4, hidden // tile),
-        in_specs=[full, full, first, full, hbm, weight, weight, weight],
+        in_specs=[full, full, hbm, hbm, hbm, weight, weight, weight],
         out_specs=[
             pl.BlockSpec((size, tile), lambda s, j: (s, j)),
             pl.BlockSpec((2, size, tile), lambda s, j: (0, s, j)),
         ]
         + [hbm] * 6,
         out_shape=[act_shape, jax.ShapeDtypeStruct((2, 2 * tokens, hidden), low)]
-        + [tokens_of(low), jax.ShapeDtypeStruct((width, size), low)]
+        + [tokens_of(low), jax.ShapeDtypeStruct((width, begun), low)]
         + [tokens_of(kind) for kind in (low, low, wide, low)],
         scratch_shapes=[
             pltpu.VMEM((size, width), low),
@@ -602,14 +667,17 @@
             pltpu.VMEM((width, size), wide),
             pltpu.VMEM((width, size), wide),
             pltpu.VMEM((2, width, size), low),
-            pltpu.VMEM((width, size), low),
+            pltpu.VMEM((width, begun), low),
             pltpu.VMEM((2, width, size), low),
+            pltpu.VMEM((width, 128), low),
             pltpu.VMEM((4, width, size), low),
             pltpu.VMEM((2, width, size), wide),
-            pltpu.SemaphoreType.DMA((6,)),
-            pltpu.SemaphoreType.DMA((11,)),
+            pltpu.VMEM((width, tokens - begun), low),
+            pltpu.VMEM((width, tokens), wide),
+            pltpu.SemaphoreType.DMA((8,)),
+            pltpu.SemaphoreType.DMA((13,)),
         ],
-        compiler_params=pltpu.CompilerParams(vmem_limit_bytes=56 << 20, collective_id=0, has_side_effects=True),
+        compiler_params=pltpu.CompilerParams(vmem_limit_bytes=60 << 20, collective_id=0, has_side_effects=True),
         cost_estimate=hint,
         name="ffn_both_ways",
     )(x, g_own, g_oth, hres, g_late, gate_w, up_w, down_w)
@@ -709,7 +777,8 @@
 
     parts = [pl.ds(*each) for each in cut]
 
-    late = move(0, late_h, late_in, to_y)
+    late_from = half_len - late_in.shape[1]
+    late = move(0, late_h.at[:, pl.ds(late_from, half_len - late_from)], late_in, to_y)
     swap_out = move(1, outp_h, got_p, to_swap)
     back_out = move(2, outr_h, got_r, to_back)
     z_down = [move(3, r_core.at[0, chunk(order[0])], zd.at[0], to_z), move(4, zd.at[0], zd.at[1], to_z)]
@@ -819,13 +888,13 @@
 
     def weights(r_buf, l_go, l_gr, l_xo, l_xr, s_buf):
         loads = [
-            load(0, pair_h.at[1 - m], r_buf.at[0]),
-            load(1, xo_h, l_xo),
-            load(2, xr_h, l_xr),
-            load(3, hid_h, r_buf.at[1]),
-            load(4, go_h, l_go),
-            load(5, gr1_h, l_gr.at[:, pl.ds(0, half_len // 2)]),
-            load(14, gr2_h, l_gr.at[:, pl.ds(half_len // 2, half_len // 2)]),
+            load(0, hid_h, r_buf.at[0]),
+            load(1, go_h, l_go),
+            load(2, gr1_h, l_gr.at[:, pl.ds(0, gr1_h.shape[1])]),
+            load(3, gr2_h, l_gr.at[:, pl.ds(gr1_h.shape[1], gr2_h.shape[1])]),
+            load(4, pair_h.at[1 - m], r_buf.at[1]),
+            load(5, xo_h, l_xo),
+            load(14, xr_h, l_xr),
         ]
         load_own = load(6, pair_h.at[m], r_buf.at[0])
         for each in loads:
@@ -834,7 +903,7 @@
 
         def core(i, k):
             at = chunk((z + zs - 1 - k) % zs)
-            return move(48 + i * zs + k, s_buf.at[i % 2, at], r_core.at[(1, 0, 2)[i], at], to_core)
+            return move(48 + i * zs + k, s_buf.at[i % 2, at], r_core.at[i, at], to_core)
 
         def product(left_o, left_r, right, col, i, extra=None):
             def block(k, carry):
@@ -845,9 +914,8 @@
                     s_buf[i % 2, at, :] = total.astype(low)
                     core(i, k).start()
                 else:
-                    out = (1, 0, 2)[i]
                     core(i, k).wait_recv()
-                    r_core[out, at, :] = (total + r_core[out, at, :].astype(wide)).astype(low)
+                    r_core[i, at, :] = (total + r_core[i, at, :].astype(wide)).astype(low)
                     extra(k)
                 return carry
 
@@ -866,25 +934,27 @@
 
             lax.fori_loop(0, zs, block, 0)
 
-        for each in loads[:3]:
+        for each in loads[:4]:
             each.wait()
-        product(l_xo, l_xr, r_buf.at[0], theirs, 0)
-        product(l_xo, l_xr, r_buf.at[0], mine, 0, lambda k: x_pair(k).start())
+        product(l_go, l_gr, r_buf.at[0], theirs, 0)
+        product(l_go, l_gr, r_buf.at[0], mine, 0, at_first(z_down[0].start))
         load_own.start()
+        for each in loads[4:]:
+            each.wait()
+        product(l_xo, l_xr, r_buf.at[1], theirs, 1)
+        product(l_xo, l_xr, r_buf.at[1], mine, 1, lambda k: x_pair(k).start())
 
         @pl.when(c != y)
         def _():
             swap_out.start()
 
         back_out.start()
-        for each in loads[3:]:
-            each.wait()
-        product(l_go, l_gr, r_buf.at[1], theirs, 1)
-        product(l_go, l_gr, r_buf.at[1], mine, 1, at_first(z_down[0].start))
+        step_z_down(1)
         load_own.wait()
         sent(0)
         product(l_xo, l_xr, r_buf.at[0], theirs, 2)
-        product(l_xo, l_xr, r_buf.at[0], mine, 2, at_first(lambda: step_z_pair(0)))
+        product(l_xo, l_xr, r_buf.at[0], mine, 2, lambda k: None)
+        step_z_pair(0)
         sent(1)
         sent(2)
 
@@ -947,7 +1017,7 @@
 
         def add_late(i, carry):
             at = pl.ds(pl.multiple_of(i * piece, piece), piece)
-            gxv[at, :] += late_in[at, :].astype(wide)
+            gxv[at, late_from:] += late_in[at, :].astype(wide)
             return carry
 
         lax.fori_loop(0, pieces, add_late, 0)
@@ -960,7 +1030,7 @@
         norm_backward(lambda at: hv[at, :], gain2, scale2, lambda at: gxv[at, :], store_hres, 0)
         core_branch.start()
         load_x.start()
-        step_z_down(1)
+        step_z_down(2)
         core_branch.wait_recv()
         gm[...] = dot(out_w[...], bf[...], 1, 0).astype(low)
 
@@ -1030,7 +1100,7 @@
             for side_c in range(2):
                 row = 8 + side_c * heads + h
                 small[row : row + 1, :128] = jnp.where(c == side_c, line, 0.0)
-            if h == 1:
+            if h == 0:
                 step_z_pair(1)
 
         def input_grad(half, store):
@@ -1044,31 +1114,44 @@
         def store_sent(at, value):
             sx[at, :] = value.astype(low)
 
-        input_grad(other_half, store_sent)
         core_x = move(34, sx, rx, to_core)
-        core_x.start()
         loads[3].wait()
         y_attn = [
             move(35 + k, ga.at[j, :, side(1 - y, a_cols)], ya.at[j], to_y) for k, j in enumerate(order)
         ]
         wide_cols = gqkv.shape[0]
-        for k, j in enumerate(order):
+
+        def weight_part(k):
+            j = order[k]
             ga[j, :rows, :wide_cols] = dot(xn1[chunk(j), :], gqkv[...], 1, 1).astype(low)
             ga[j, :rows, wide_cols:] = dot(bf[chunk(j), :], mixed[...], 1, 1).astype(low)
             ga[j, rows:, :] = jnp.zeros((ga.shape[1] - rows, ga.shape[2]), low)
             y_attn[k].start()
-        step_z_down(2)
 
         def store_own(at, value):
             hv[at, :] = value
 
+        def store_in(at, back):
+            gin[at, :] = (gxv[at, :] + back).astype(low)
+
+        def step_y_attn(k):
+            j = order[k]
+            y_attn[k].wait_recv()
+            ya[j] = (ya[j].astype(wide) + ga[j, :, my_cols].astype(wide)).astype(low)
+            x_attn[k].start()
+
+        weight_part(0)
+        weight_part(1)
+        input_grad(other_half, store_sent)
+        core_x.start()
+        last_z_down(0)
+        last_z_down(1)
         input_grad(my_half, store_own)
+        weight_part(2)
+        weight_part(3)
+        step_y_attn(0)
         load_x.wait()
         core_x.wait_recv()
-
-        def store_in(at, back):
-            gin[at, :] = (gxv[at, :] + back).astype(low)
-
         norm_backward(
             lambda at: gov[at, :].astype(wide),
             gain1,
@@ -1077,27 +1160,23 @@
             store_in,
             1,
         )
+        step_z_pair(2)
+        start_sum(0)
+        step_y_attn(1)
+        end_sum(0)
+        start_sum(1)
 
         @pl.when(c != y)
         def _():
             swap_in.start()
 
-        def step_y_attn(k):
-            j = order[k]
-            y_attn[k].wait_recv()
-            ya[j] = (ya[j].astype(wide) + ga[j, :, my_cols].astype(wide)).astype(low)
-            x_attn[k].start()
-
-        step_y_attn(0)
-        step_z_pair(2)
-        start_sum(0)
-        step_y_attn(1)
+        end_down(0)
+        end_down(1)
+        step_y_attn(2)
+        last_z_pair(0)
         step_attn(0)
-        end_sum(0)
-        start_sum(1)
-        last_z_down(0)
-        step_y_attn(2)
-        last_z_down(1)
+        end_sum(1)
+        start_sum(2)
         step_y_attn(3)
         core_x.wait_send()
         for each in y_attn:
@@ -1121,17 +1200,12 @@
         b16(zs, ya.shape[1], 2 * ya.shape[2]),
     )
 
-    end_sum(1)
-    start_sum(2)
-    end_down(0)
-    last_z_pair(0)
-    end_down(1)
     last_z_pair(1)
     step_attn(1)
+    end_pair(0)
+    step_attn(2)
     end_sum(2)
     start_sum(3)
-    step_attn(2)
-    end_pair(0)
     step_attn(3)
     ab[my_rows, my_cols] = za[zs - 2]
     for each in spread_attn:
@@ -1207,7 +1281,7 @@
             b16(zs, a_len // 2, a_cols),
             b16(zs - 1, a_len // 2, a_cols),
             b16(a_len, 2 * a_cols),
-            b16(width, half_len),
+            b16(width, half_len - 128),
             pltpu.VMEM((5, 16, width), wide),
             pltpu.VMEM((5, 16, width), wide),
             pltpu.SemaphoreType.DMA((60,)),
@@ -1458,7 +1532,7 @@
         position_bias.T,
         gain_attn,
         gain_ffn,
-        moves.nx == 2,
+        moves.nx == 2 and moves.nz == 4,
     )
     hid, pair, xn_oth, g_late, out_first, out_oth, gx, late = ffn(
         xn_own, g_own, g_oth, hres, g_send, gate_weight, up_weight, down_weight.T
@@ -1487,7 +1561,7 @@
             sum_d.T,
         )
     grad_gate, grad_up = pair[0], pair[1]
-    gx = gx + moves.over_y(late).astype(wide)
+    gx = gx.at[:, 128:].add(moves.over_y(late)[:, 128:].astype(wide))
     g_oth = jnp.concatenate([g_oth, g_late], axis=1)
     qkv_w = w_t.T
     x_wide = x_in.astype(wide)

time: 277 us -> 267 us (0.964)
  Pallas kernels: 273 us -> 265 us
    pallas_call x1, Pallas kernels: 58.7 us -> 55.5 us  [ffn(): pl.pallas_call(ffn_kernel, grid=(4, hidden // tile), in_specs=[full, full...]
where the time goes in v7:
time: 267 us
  Pallas kernels  265 us (99%)
    pallas_call x1, Pallas kernels, back_all(): pl.pallas_call(back_kernel, in_specs=[hbm] * 15 + [vmem] * 8, out_specs=[...  138 us
    pallas_call x1, Pallas kernels, front(): pl.pallas_call(functools.partial(front_kernel, share), in_specs=[hbm] * 6...  62.7 us
    pallas_call x1, Pallas kernels, ffn(): pl.pallas_call(ffn_kernel, grid=(4, hidden // tile), in_specs=[full, full...  55.5 us
    pallas_call x1, Pallas kernels, finish(): pl.pallas_call(finish_kernel, in_specs=[hbm] * 8 + [vmem], out_specs=[hbm...  9.27 us

profile of v7, /device:TPU:0, one launch (start us, length us, event | category | flops | bytes accessed | tf_op | source)
XLA Modules:
  0.0 266.6 jit_solution(9167105387710844109)
XLA Ops:
  1.3 62.7 %front_all.1 = (bf16[1472,512]{1,0:T(8,128)(2,1)}, bf16[1472,512]{1,0:T(8,128)(2,1)}, bf16[1472,384]{1,0:T(8,128)(2,1)}, bf16[1472,128]{1,0:T(8,128)(2,1)}, bf16...) custom-call(bf16[1472,512]{1,0:T(8,128)(2,1)} %bitcast.23, ...), custom_call_target="tpu_custom_call" | custom-call | flops 1000 | bytes 1000 | tf_op jit(solution)/shard_map/front_all/pallas_call | solution.py:383
  64.0 55.5 %ffn_both_ways.1 = (bf16[1024,1792]{1,0:T(8,128)(2,1)}, bf16[2,1024,1792]{2,1,0:T(8,128)(2,1)}, bf16[1472,512]{1,0:T(8,128)(2,1)}, bf16[1472,128]{1,0:T(8,128)(2...) custom-call(bf16[1472,512]{1,0:T(8,128)(2,1)} %get-tuple-element.56., ...), custom_call_target="tpu_custom_call" | custom-call | flops 1000 | bytes 1000 | tf_op jit(solution)/shard_map/ffn_both_ways/pallas_call | solution.py:652
  119.5 137.7 %back_all.1 = (bf16[1472,512]{1,0:T(8,128)(2,1)}, bf16[1472,512]{1,0:T(8,128)(2,1)}, bf16[1472,512]{1,0:T(8,128)(2,1)}, bf16[368,1792]{1,0:T(8,128)(2,1)}, bf16[...) custom-call(bf16[1024,1792]{1,0:T(8,128)(2,1)} %get-tuple-element.61.hid_h,, ...), custom_call_target="tpu_custom_call" | custom-call | flops 1000 | bytes 1000 | tf_op jit(solution)/shard_map/back_all/pallas_call | solution.py:1257
  257.1 9.3 %finish_all.1 = (f32[368,1792]{1,0:T(8,128)}, f32[368,1792]{1,0:T(8,128)}, f32[368,1792]{1,0:T(8,128)}, f32[192,368]{1,0:T(8,128)}, f32[192,368]{1,0:T(8,128)}, ...) custom-call(bf16[368,1792]{1,0:T(8,128)(2,1)} %get-tuple-element.80., ...), custom_call_target="tpu_custom_call" | custom-call | flops 1000 | bytes 1000 | tf_op jit(solution)/shard_map/finish_all/pallas_call | solution.py:1385
